TPU v7x, 32 devices: a whole 2x2x4 slice. The times are simulated.
32 devices in a mesh: energy: 8 (over z, core), slab: 4 (over y, x).
Axes of the slice: x: 2, y: 2, z: 4, core: 2. Of those that a mesh axis runs over, the one named last changes fastest.
Arguments:
- h_diag: float32 [4, 128, 128], P('slab'), may hold values from -0.625 to 0.625, as said below
- coupling: float32 [4, 128, 128], P('slab'), may hold values from -1 to 1
- broadening: float32 [8], P('energy'), may hold values from 0.4 to 1.2
Outputs:
- green: float32 [8, 4, 2, 128, 128], P('energy', 'slab')
- polar: float32 [8, 4, 2, 128, 128], P('energy', 'slab')
Inputs may be any that keep to these rules, and one draw needn't show every extreme that they name: h_diag[i] is symmetric for every slab i.
All inputs are finite; a program needn't handle non-finite values.
Results may differ from a plain program's by a relative error of at most 0.0003.
Values sent between devices are 32-bit elements; how exact they have to be, the bound alone decides.
No kernel may reach another device: no remote copies, remote signals or barrier semaphores. Data moves between devices by JAX's collectives and lax.ppermute only.
A program may use at most 64 MiB of HBM per device.

v0:
```python
import functools

import jax
import jax.numpy as jnp
from jax import lax
from jax.experimental import pallas as pl
from jax.experimental.pallas import tpu as pltpu
from jax.sharding import PartitionSpec as P

f32 = jnp.float32
bf16 = jnp.bfloat16
highest = lax.Precision.HIGHEST
PANEL = 32
TILE = 8


def dot(left, right, dims=((1,), (0,))):
    return lax.dot_general(left, right, (dims, ((), ())), precision=highest, preferred_element_type=f32)


def three_parts(value):
    high = value.astype(bf16)
    rest = value - high.astype(f32)
    middle = rest.astype(bf16)
    low = (rest - middle.astype(f32)).astype(bf16)
    return high, middle, low


def row_of(tile, k):
    return jnp.broadcast_to(tile[k : k + 1, :], tile.shape)


def column_of(tile, k):
    return jnp.broadcast_to(tile[:, k : k + 1], tile.shape)


def eliminate_tile(real, imag, base, row, lane):
    height = real.shape[0]
    dr = [column_of(real, base + k) for k in range(height)]
    di = [column_of(imag, base + k) for k in range(height)]
    for k in range(height):
        at_row = row == k
        pr, pi = row_of(dr[k], k), row_of(di[k], k)
        inverse = 1.0 / (pr * pr + pi * pi)
        cr, ci = jnp.where(at_row, -1.0, dr[k]), jnp.where(at_row, 0.0, di[k])
        tr, ti = cr * pr + ci * pi, ci * pr - cr * pi
        fr, fi = tr * inverse, ti * inverse
        for c in range(k + 1, height):
            ar, ai = row_of(dr[c], k), row_of(di[c], k)
            zr, zi = jnp.where(at_row, 0.0, dr[c]), jnp.where(at_row, 0.0, di[c])
            if c == k + 1:
                dr[c] = zr - (tr * ar - ti * ai) * inverse
                di[c] = zi - (tr * ai + ti * ar) * inverse
            else:
                dr[c], di[c] = zr - (fr * ar - fi * ai), zi - (fr * ai + fi * ar)
        at_lane = lane == base + k
        ar = jnp.where(at_lane, 1.0, row_of(real, k))
        ai = jnp.where(at_lane, 0.0, row_of(imag, k))
        cleared = at_row | at_lane
        real = jnp.where(cleared, 0.0, real) - (fr * ar - fi * ai)
        imag = jnp.where(cleared, 0.0, imag) - (fr * ai + fi * ar)
    return real, imag


def eliminate_panel(real, imag, row, lane):
    tiles = len(real)
    for s in range(tiles):
        base = s * TILE
        columns = {
            t: [(column_of(real[t], base + k), column_of(imag[t], base + k)) for k in range(TILE)]
            for t in range(tiles)
            if t != s
        }
        new_real, new_imag = eliminate_tile(real[s], imag[s], base, row, lane)
        rows = [(row_of(new_real, k), row_of(new_imag, k)) for k in range(TILE)]
        inside = (lane >= base) & (lane < base + TILE)
        for t in [(s + 1 + u) % tiles for u in range(tiles - 1)]:
            xr, xi = jnp.where(inside, 0.0, real[t]), jnp.where(inside, 0.0, imag[t])
            for (cr, ci), (wr, wi) in zip(columns[t], rows):
                xr, xi = xr - (cr * wr - ci * wi), xi - (cr * wi + ci * wr)
            real[t], imag[t] = xr, xi
        real[s], imag[s] = new_real, new_imag
    return real, imag


def swept(ref, m):
    size = ref.shape[-1]
    width = min(PANEL, size)
    tiles = width // TILE
    row = lax.broadcasted_iota(jnp.int32, (TILE, size), 0)
    lane = lax.broadcasted_iota(jnp.int32, (TILE, size), 1)
    real = [ref[m, 0, t * TILE : (t + 1) * TILE, :] for t in range(tiles)]
    imag = [ref[m, 1, t * TILE : (t + 1) * TILE, :] for t in range(tiles)]
    lh, lm, ll = three_parts(jnp.concatenate(real + imag, 0))
    real, imag = eliminate_panel(real, imag, row, lane)
    block = lane < width
    wr = jnp.concatenate([pltpu.roll(jnp.where(block, -x, x), size - width, 1) for x in real], 0)
    wi = jnp.concatenate([pltpu.roll(jnp.where(block, -x, x), size - width, 1) for x in imag], 0)
    rh, rm, rl = three_parts(
        jnp.concatenate([jnp.concatenate([wr, wi], 1), jnp.concatenate([-wi, wr], 1)], 0)
    )
    change = lax.dot_general(
        jnp.concatenate([lh, lh, lm, lh, lm, ll], 0),
        jnp.concatenate([rh, rm, rh, rl, rm, rh], 0),
        (((0,), (0,)), ((), ())),
        preferred_element_type=f32,
    )
    cleared = lax.broadcasted_iota(jnp.int32, (size - width, size), 1) < width
    rest_real = pltpu.roll(jnp.where(cleared, 0.0, ref[m, 0, width:, :]), size - width, 1)
    rest_imag = pltpu.roll(jnp.where(cleared, 0.0, ref[m, 1, width:, :]), size - width, 1)
    return rest_real - change[width:, :size], rest_imag - change[width:, size:], wr, wi


def invert_in_place(ref, count):
    size = ref.shape[-1]
    width = min(PANEL, size)

    def step(_, carry):
        results = [swept(ref, m) for m in range(count)]
        for m, (rest_real, rest_imag, wr, wi) in enumerate(results):
            ref[m, 0, : size - width, :] = rest_real
            ref[m, 1, : size - width, :] = rest_imag
            ref[m, 0, size - width :, :] = wr
            ref[m, 1, size - width :, :] = wi
        return carry

    lax.fori_loop(0, size // width, step, 0)


def wide(real, imag):
    return jnp.concatenate([real, imag], 1)


def square(real, imag):
    return jnp.concatenate([wide(real, imag), wide(-imag, real)], 0)


def chain_kernel(count, total_energies, place_ref, damping_ref, *refs):
    blocks, (green_ref, diagonal_ref, link_ref, work_ref) = refs[: 2 * count], refs[2 * count :]
    h_refs, c_refs = blocks[:count], blocks[count:]
    size = green_ref.shape[-1]
    slab, position = place_ref[0], place_ref[1]
    energy = -4.0 + 8.0 * position.astype(f32) / (total_energies - 1)
    damping = damping_ref[0]
    row = lax.broadcasted_iota(jnp.int32, (size, size), 0)
    lane = lax.broadcasted_iota(jnp.int32, (size, size), 1)
    identity = jnp.where(row == lane, 1.0, 0.0).astype(f32)

    def is_last(step):
        return lax.rem(slab + step, count) == count - 1

    def cut_link(step):
        return c_refs[step][...] * jnp.where(is_last(step), 0.0, 1.0)

    for step in range(count):
        diagonal_ref[step, 0] = energy * identity - h_refs[step][...]
        diagonal_ref[step, 1] = damping * identity

        @pl.when(is_last(step))
        def _():
            link = c_refs[step][...]
            diagonal_ref[step, 1] = diagonal_ref[step, 1] + 0.5 * dot(link, link, ((1,), (1,)))

    def subtract(node, real, imag):
        diagonal_ref[node, 0] = diagonal_ref[node, 0] - real
        diagonal_ref[node, 1] = diagonal_ref[node, 1] - imag

    for level in range(count.bit_length() - 1):
        stride = 1 << level
        nodes = list(range(0, count, stride))
        odds = nodes[1::2]
        for first in range(0, len(odds), 2):
            group = odds[first : first + 2]
            for m, node in enumerate(group):
                work_ref[m] = diagonal_ref[node]
            invert_in_place(work_ref, len(group))
            for m, node in enumerate(group):
                before, after = node - stride, (node + stride) % count
                middle = (work_ref[m, 0], work_ref[m, 1])
                if level == 0:
                    left = (cut_link(before), None)
                    right = (cut_link(node).T, None)
                else:
                    left = (link_ref[before, 0], link_ref[before, 1])
                    right = (link_ref[node, 0].T, link_ref[node, 1].T)
                if before == after:
                    left = tuple(None if a is None else a + b for a, b in zip(left, right))

                def reached(pair):
                    if pair[1] is None:
                        both = dot(pair[0], wide(*middle))
                    else:
                        both = dot(wide(*pair), square(*middle))
                    return both[:, :size], both[:, size:]

                def closed(pair, end):
                    if end[1] is None:
                        both = dot(jnp.concatenate(pair, 0), end[0], ((1,), (1,)))
                        return both[:size], both[size:]
                    turned = jnp.concatenate([wide(end[0], -end[1]), wide(end[1], end[0])], 0)
                    both = dot(wide(*pair), turned, ((1,), (1,)))
                    return both[:, :size], both[:, size:]

                start = reached(left)
                real, imag = closed(start, left)
                subtract(before, -real, -imag)
                if before != after:
                    real, imag = closed(start, right)
                    link_ref[before, 0] = real
                    link_ref[before, 1] = imag
                    real, imag = closed(reached(right), right)
                    subtract(after, -real, -imag)
    work_ref[0] = diagonal_ref[0]
    invert_in_place(work_ref, 1)
    green_ref[...] = -work_ref[0]


def green_of(h_blocks, c_blocks, slab, position, damping, total_energies):
    count, size = len(h_blocks), h_blocks[0].shape[-1]
    whole = pl.BlockSpec(memory_space=pltpu.VMEM)
    scalar = pl.BlockSpec(memory_space=pltpu.SMEM)
    return pl.pallas_call(
        functools.partial(chain_kernel, count, total_energies),
        out_shape=jax.ShapeDtypeStruct((2, size, size), f32),
        in_specs=[scalar, scalar] + [whole] * (2 * count),
        out_specs=whole,
        scratch_shapes=[
            pltpu.VMEM((count, 2, size, size), f32),
            pltpu.VMEM((count, 2, size, size), f32),
            pltpu.VMEM((2, 2, size, size), f32),
        ],
        name="chain",
    )(jnp.stack([slab, position]).astype(jnp.int32), damping, *h_blocks, *c_blocks)


def correlate(own, groups):
    gathered = [own] + [
        lax.ppermute(own, "energy", [(s, s ^ d) for s in range(groups)]) for d in range(2, groups, 2)
    ]
    everything = []
    for block in gathered:
        everything.append(block)
        everything.append(lax.ppermute(block, "energy", [(s, s ^ 1) for s in range(groups)]))
    mine = lax.axis_index("energy")

    def kernel(mine_ref, *refs):
        blocks, (out_ref, held) = refs[:groups], refs[groups:]
        me = mine_ref[0]
        for step in range(groups):
            held[me ^ step] = blocks[step][...]
        real = imag = jnp.zeros(own.shape[1:], f32)
        for first in range(groups):
            inside = first + me < groups
            second = jnp.where(inside, first + me, 0)
            weight = jnp.where(inside, 1.0 / groups, 0.0)
            br, bi = held[first, 0] * weight, held[first, 1] * weight
            ar, ai = held[second, 0], held[second, 1]
            real = real + (ar * br + ai * bi)
            imag = imag + (ai * br - ar * bi)
        out_ref[0] = real
        out_ref[1] = imag

    whole = pl.BlockSpec(memory_space=pltpu.VMEM)
    return pl.pallas_call(
        kernel,
        out_shape=jax.ShapeDtypeStruct(own.shape, f32),
        in_specs=[pl.BlockSpec(memory_space=pltpu.SMEM)] + [whole] * groups,
        out_specs=whole,
        scratch_shapes=[pltpu.VMEM((groups,) + own.shape, f32)],
        name="polar",
    )(mine[None].astype(jnp.int32), *everything)


def correlate_spread(own, groups):
    _, size, _ = own.shape
    spread = own.reshape(2, groups, size * size // groups)
    mixed = lax.all_to_all(spread[None], "energy", split_axis=2, concat_axis=0, tiled=True)[:, :, 0]
    real, imag = mixed[:, 0], mixed[:, 1]
    pieces = []
    for offset in range(groups):
        ar, ai = real[offset:], imag[offset:]
        br, bi = real[: groups - offset], imag[: groups - offset]
        pieces.append(jnp.stack([jnp.sum(ar * br + ai * bi, 0), jnp.sum(ai * br - ar * bi, 0)]))
    result = (jnp.stack(pieces) / groups)[:, :, None, :]
    back = lax.all_to_all(result, "energy", split_axis=0, concat_axis=2, tiled=True)
    return back.reshape(own.shape)


def on_device(h_diag, coupling, broadening):
    slabs = lax.axis_size("slab")
    groups = lax.axis_size("energy")
    slab = lax.axis_index("slab")
    position = lax.axis_index("energy")
    size = h_diag.shape[-1]
    own = jnp.concatenate([h_diag, coupling], 0)
    blocks = [own] + [
        lax.ppermute(own, "slab", [(s, (s - r) % slabs) for s in range(slabs)]) for r in range(1, slabs)
    ]
    green = green_of([b[0] for b in blocks], [b[1] for b in blocks], slab, position, broadening, groups)
    polar = correlate(green, groups) if groups <= 8 else correlate_spread(green, groups)
    shape = (1, 1, 2, size, size)
    return green.reshape(shape), polar.reshape(shape)


def solution(mesh):
    return jax.shard_map(
        on_device,
        mesh=mesh,
        in_specs=(P("slab", None, None), P("slab", None, None), P("energy")),
        out_specs=(P("energy", "slab", None, None, None), P("energy", "slab", None, None, None)),
        check_vma=False,
    )
```

profile of v0, /device:TPU:0, one launch (start us, length us, event | category | flops | bytes accessed | tf_op | source)
XLA Modules:
  0.0 57.8 jit_solution(13614320950854200973)
XLA Ops:
  0.6 0.0 copy-start
  0.6 0.9 %constant_dynamic-update-slice_fusion.1 = f32[2,128,128]{2,1,0:T(8,128)S(1)} fusion(f32[1,128,128]{2,1,0:T(8,128)} %param.3), kind=kLoop, calls=%fused_computation.7 | loop fusion | bytes 131072
  1.5 0.0 copy-done
  1.5 3.0 %collective-permute-start.2 = (f32[2,128,128]{2,1,0:T(8,128)S(1)}, f32[2,128,128]{2,1,0:T(8,128)S(1)}, u32[]{:S(2)}, u32[]{:S(2)}) collective-permute-start(f32[2,128,128]{2,1,0:T(8,128)S(1)} %constant_dynamic-update-slice_fusion), channel_id=1, source_target_pairs={{0,1},{1,2},{2,3},{3,0},{4,5},{5,6},{6,7},{7,4},{8,9},{9,10},{10,1... | collective-permute-start | bytes 393224 | tf_op jit(solution)/shard_map/ppermute | solution.py:297
  4.5 1.5 %collective-permute-start.1 = (f32[2,128,128]{2,1,0:T(8,128)S(1)}, f32[2,128,128]{2,1,0:T(8,128)S(1)}, u32[]{:S(2)}, u32[]{:S(2)}) collective-permute-start(f32[2,128,128]{2,1,0:T(8,128)S(1)} %constant_dynamic-update-slice_fusion), channel_id=1, source_target_pairs={{0,2},{1,3},{2,0},{3,1},{4,6},{5,7},{6,4},{7,5},{8,10},{9,11},{10,... | collective-permute-start | bytes 393224 | tf_op jit(solution)/shard_map/ppermute | solution.py:297
  6.1 1.4 %collective-permute-start = (f32[2,128,128]{2,1,0:T(8,128)S(1)}, f32[2,128,128]{2,1,0:T(8,128)S(1)}, u32[]{:S(2)}, u32[]{:S(2)}) collective-permute-start(f32[2,128,128]{2,1,0:T(8,128)S(1)} %constant_dynamic-update-slice_fusion), channel_id=1, source_target_pairs={{0,3},{1,0},{2,1},{3,2},{4,7},{5,4},{6,5},{7,6},{8,11},{9,8},{10,9... | collective-permute-start | bytes 393224 | tf_op jit(solution)/shard_map/ppermute | solution.py:297
  8.2 0.6 %pad_add_fusion.place_ref = s32[2]{0:T(128)} fusion(s32[1]{0:T(128)} %bitcast.1.mine_ref, s32[1]{0:T(128)} %bitcast), kind=kLoop, calls=%fused_computation.8 | loop fusion | flops 2 | bytes 16 | tf_op jit(solution)/shard_map/stack | solution.py:233
  8.8 1.1 %collective-permute-done.2 = f32[2,128,128]{2,1,0:T(8,128)S(1)} collective-permute-done((f32[2,128,128]{2,1,0:T(8,128)S(1)}, f32[2,128,128]{2,1,0:T(8,128)S(1)}, u32[]{:S(2)}, u32[]{:S(2)}) %collective-permute-start.2) | collective-permute-done | bytes 131104 | tf_op jit(solution)/shard_map/ppermute | solution.py:297
  9.9 0.7 %slice_bitcast_fusion = (f32[128,128]{1,0:T(8,128)}, f32[128,128]{1,0:T(8,128)}) fusion(f32[2,128,128]{2,1,0:T(8,128)S(1)} %collective-permute-done.2), kind=kLoop, calls=%fused_computation | loop fusion | bytes 262144 | tf_op jit(solution)/shard_map/squeeze | solution.py:299
  10.5 1.3 %collective-permute-done.1 = f32[2,128,128]{2,1,0:T(8,128)S(1)} collective-permute-done((f32[2,128,128]{2,1,0:T(8,128)S(1)}, f32[2,128,128]{2,1,0:T(8,128)S(1)}, u32[]{:S(2)}, u32[]{:S(2)}) %collective-permute-start.1) | collective-permute-done | bytes 131104 | tf_op jit(solution)/shard_map/ppermute | solution.py:297
  11.8 0.6 %slice_bitcast_fusion.1 = (f32[128,128]{1,0:T(8,128)}, f32[128,128]{1,0:T(8,128)}) fusion(f32[2,128,128]{2,1,0:T(8,128)S(1)} %collective-permute-done.1), kind=kLoop, calls=%fused_computation.1 | loop fusion | bytes 262144 | tf_op jit(solution)/shard_map/squeeze | solution.py:299
  12.5 0.0 collective-permute-done
  12.5 0.6 %slice_bitcast_fusion.2 = (f32[128,128]{1,0:T(8,128)}, f32[128,128]{1,0:T(8,128)}) fusion(f32[2,128,128]{2,1,0:T(8,128)S(1)} %collective-permute-done), kind=kLoop, calls=%fused_computation.2 | loop fusion | bytes 262144 | tf_op jit(solution)/shard_map/squeeze | solution.py:299
  13.1 24.5 %chain.1.refs_0_ = f32[2,128,128]{2,1,0:T(8,128)} custom-call(s32[2]{0:T(128)} %pad_add_fusion.place_ref, f32[1]{0:T(128)S(6)} %copy.6.damping_ref, f32[128,128]{1,0:T(8,128)} %bitcast.19, f32[128,128]{1,0:T(8,128)} %get-tuple-element.7.refs_1_, f32[128,128]{1,0:T(8,128)} %get-tuple-element.5.refs_2_, f32[128,128]{1,0:T(8,128)} %get-tuple-element.3.refs_3_, ...), custom_call_target="tpu_custom_call" | custom-call | tf_op jit(solution)/shard_map/chain/pallas_call | solution.py:222
  37.6 3.8 %collective-permute-start.8 = (f32[2,128,128]{2,1,0:T(8,128)}, f32[2,128,128]{2,1,0:T(8,128)S(1)}, u32[]{:S(2)}, u32[]{:S(2)}) collective-permute-start(f32[2,128,128]{2,1,0:T(8,128)} %chain.1.refs_0_), channel_id=1, source_target_pairs={{0,24},{4,28},{8,16},{12,20},{16,8},{20,12},{24,0},{28,4},{1,25},{... | collective-permute-start | bytes 393224 | tf_op jit(solution)/shard_map/ppermute | solution.py:238
  41.4 0.0 collective-permute-start.6
  41.4 0.6 %collective-permute-start.4 = (f32[2,128,128]{2,1,0:T(8,128)}, f32[2,128,128]{2,1,0:T(8,128)S(1)}, u32[]{:S(2)}, u32[]{:S(2)}) collective-permute-start(f32[2,128,128]{2,1,0:T(8,128)} %chain.1.refs_0_), channel_id=1, source_target_pairs={{0,8},{4,12},{8,0},{12,4},{16,24},{20,28},{24,16},{28,20},{1,9},{5... | collective-permute-start | bytes 393224 | tf_op jit(solution)/shard_map/ppermute | solution.py:238
  42.0 0.0 collective-permute-start.3
  42.0 4.1 %collective-permute-done.8.refs_6_ = f32[2,128,128]{2,1,0:T(8,128)S(1)} collective-permute-done((f32[2,128,128]{2,1,0:T(8,128)}, f32[2,128,128]{2,1,0:T(8,128)S(1)}, u32[]{:S(2)}, u32[]{:S(2)}) %collective-permute-start.8) | collective-permute-done | bytes 131104 | tf_op jit(solution)/shard_map/ppermute | solution.py:238
  46.1 0.0 copy-start.1
  46.1 0.0 collective-permute-start.9
  46.1 6.8 %collective-permute-done.6.refs_4_ = f32[2,128,128]{2,1,0:T(8,128)S(1)} collective-permute-done((f32[2,128,128]{2,1,0:T(8,128)}, f32[2,128,128]{2,1,0:T(8,128)S(1)}, u32[]{:S(2)}, u32[]{:S(2)}) %collective-permute-start.6) | collective-permute-done | bytes 131104 | tf_op jit(solution)/shard_map/ppermute | solution.py:238
  52.9 0.0 copy-start.2
  52.9 0.0 collective-permute-start.7
  52.9 0.0 collective-permute-done.4.refs_2_
  52.9 0.0 copy-start.3
  52.9 0.5 collective-permute-start.5
  53.4 0.0 collective-permute-done.3.refs_1_
  53.4 0.0 copy-start.4
  53.4 0.0 collective-permute-done.9.refs_7_
  53.4 0.0 copy-start.5
  53.4 0.8 %collective-permute-done.7.refs_5_ = f32[2,128,128]{2,1,0:T(8,128)S(1)} collective-permute-done((f32[2,128,128]{2,1,0:T(8,128)S(1)}, f32[2,128,128]{2,1,0:T(8,128)S(1)}, u32[]{:S(2)}, u32[]{:S(2)}) %collective-permute-start.7) | collective-permute-done | bytes 131104 | tf_op jit(solution)/shard_map/ppermute | solution.py:243
  54.2 0.0 copy-start.6
  54.2 0.2 collective-permute-done.5.refs_3_
  54.4 0.0 copy-done.1
  54.4 0.0 copy-done.2
  54.4 0.0 copy-done.3
  54.4 0.0 copy-done.4
  54.4 0.0 copy-done.5
  54.4 0.4 copy-done.6
  54.9 0.0 copy-start.7
  54.9 0.6 %copy-done.7 = f32[2,128,128]{2,1,0:T(8,128)} copy-done((f32[2,128,128]{2,1,0:T(8,128)}, f32[2,128,128]{2,1,0:T(8,128)S(1)}, u32[]{:S(2)}) %copy-start.7) | copy-done | bytes 131096
  55.5 2.2 %polar.1 = f32[2,128,128]{2,1,0:T(8,128)} custom-call(s32[1]{0:T(128)} %bitcast.1.mine_ref, f32[2,128,128]{2,1,0:T(8,128)} %chain.1.refs_0_, f32[2,128,128]{2,1,0:T(8,128)} %copy-done.4, f32[2,128,128]{2,1,0:T(8,128)} %copy-done.3, f32[2,128,128]{2,1,0:T(8,128)} %copy-done.7, f32[2,128,128]{2,1,0:T(8,128)} %copy-done.2, f32[2,128,128]{2,1,0:T(8,128)} %copy-done.6, ...), custom_call_target="tpu_custom_call" | custom-call | tf_op jit(solution)/shard_map/polar/pallas_call | solution.py:264
  (1 shorter events, 0.0 us)
Async XLA Ops:
  0.6 0.9 %copy-start = (f32[1,128,128]{2,1,0:T(8,128)S(1)}, f32[1,128,128]{2,1,0:T(8,128)}, u32[]{:S(2)}) copy-start(f32[1,128,128]{2,1,0:T(8,128)} %param.4) | copy-start | bytes 196612
  1.5 8.3 %collective-permute-start.2 = (f32[2,128,128]{2,1,0:T(8,128)S(1)}, f32[2,128,128]{2,1,0:T(8,128)S(1)}, u32[]{:S(2)}, u32[]{:S(2)}) collective-permute-start(f32[2,128,128]{2,1,0:T(8,128)S(1)} %constant_dynamic-update-slice_fusion), channel_id=1, source_target_pairs={{0,1},{1,2},{2,3},{3,0},{4,5},{5,6},{6,7},{7,4},{8,9},{9,10},{10,1... | collective-permute-start | bytes 393224 | tf_op jit(solution)/shard_map/ppermute | solution.py:297
  4.5 7.3 %collective-permute-start.1 = (f32[2,128,128]{2,1,0:T(8,128)S(1)}, f32[2,128,128]{2,1,0:T(8,128)S(1)}, u32[]{:S(2)}, u32[]{:S(2)}) collective-permute-start(f32[2,128,128]{2,1,0:T(8,128)S(1)} %constant_dynamic-update-slice_fusion), channel_id=1, source_target_pairs={{0,2},{1,3},{2,0},{3,1},{4,6},{5,7},{6,4},{7,5},{8,10},{9,11},{10,... | collective-permute-start | bytes 393224 | tf_op jit(solution)/shard_map/ppermute | solution.py:297
  6.1 6.4 %collective-permute-start = (f32[2,128,128]{2,1,0:T(8,128)S(1)}, f32[2,128,128]{2,1,0:T(8,128)S(1)}, u32[]{:S(2)}, u32[]{:S(2)}) collective-permute-start(f32[2,128,128]{2,1,0:T(8,128)S(1)} %constant_dynamic-update-slice_fusion), channel_id=1, source_target_pairs={{0,3},{1,0},{2,1},{3,2},{4,7},{5,4},{6,5},{7,6},{8,11},{9,8},{10,9... | collective-permute-start | bytes 393224 | tf_op jit(solution)/shard_map/ppermute | solution.py:297
  37.6 8.5 %collective-permute-start.8 = (f32[2,128,128]{2,1,0:T(8,128)}, f32[2,128,128]{2,1,0:T(8,128)S(1)}, u32[]{:S(2)}, u32[]{:S(2)}) collective-permute-start(f32[2,128,128]{2,1,0:T(8,128)} %chain.1.refs_0_), channel_id=1, source_target_pairs={{0,24},{4,28},{8,16},{12,20},{16,8},{20,12},{24,0},{28,4},{1,25},{... | collective-permute-start | bytes 393224 | tf_op jit(solution)/shard_map/ppermute | solution.py:238
  41.4 11.5 %collective-permute-start.6 = (f32[2,128,128]{2,1,0:T(8,128)}, f32[2,128,128]{2,1,0:T(8,128)S(1)}, u32[]{:S(2)}, u32[]{:S(2)}) collective-permute-start(f32[2,128,128]{2,1,0:T(8,128)} %chain.1.refs_0_), channel_id=1, source_target_pairs={{0,16},{4,20},{8,24},{12,28},{16,0},{20,4},{24,8},{28,12},{1,17},{... | collective-permute-start | bytes 393224 | tf_op jit(solution)/shard_map/ppermute | solution.py:238
  41.4 11.5 %collective-permute-start.4 = (f32[2,128,128]{2,1,0:T(8,128)}, f32[2,128,128]{2,1,0:T(8,128)S(1)}, u32[]{:S(2)}, u32[]{:S(2)}) collective-permute-start(f32[2,128,128]{2,1,0:T(8,128)} %chain.1.refs_0_), channel_id=1, source_target_pairs={{0,8},{4,12},{8,0},{12,4},{16,24},{20,28},{24,16},{28,20},{1,9},{5... | collective-permute-start | bytes 393224 | tf_op jit(solution)/shard_map/ppermute | solution.py:238
  42.0 11.4 %collective-permute-start.3 = (f32[2,128,128]{2,1,0:T(8,128)}, f32[2,128,128]{2,1,0:T(8,128)S(1)}, u32[]{:S(2)}, u32[]{:S(2)}) collective-permute-start(f32[2,128,128]{2,1,0:T(8,128)} %chain.1.refs_0_), channel_id=1, source_target_pairs={{0,4},{4,0},{8,12},{12,8},{16,20},{20,16},{24,28},{28,24},{1,5},{5... | collective-permute-start | bytes 393224 | tf_op jit(solution)/shard_map/ppermute | solution.py:243
  46.1 8.3 %copy-start.1 = (f32[2,128,128]{2,1,0:T(8,128)}, f32[2,128,128]{2,1,0:T(8,128)S(1)}, u32[]{:S(2)}) copy-start(f32[2,128,128]{2,1,0:T(8,128)S(1)} %collective-permute-done.8.refs_6_) | copy-start | bytes 393220
  46.1 7.3 %collective-permute-start.9 = (f32[2,128,128]{2,1,0:T(8,128)S(1)}, f32[2,128,128]{2,1,0:T(8,128)S(1)}, u32[]{:S(2)}, u32[]{:S(2)}) collective-permute-start(f32[2,128,128]{2,1,0:T(8,128)S(1)} %collective-permute-done.8.refs_6_), channel_id=1, source_target_pairs={{0,4},{4,0},{8,12},{12,8},{16,20},{20,16},{24,28},{28,24},{1,5},{5... | collective-permute-start | bytes 393224 | tf_op jit(solution)/shard_map/ppermute | solution.py:243
  52.9 1.5 %copy-start.2 = (f32[2,128,128]{2,1,0:T(8,128)}, f32[2,128,128]{2,1,0:T(8,128)S(1)}, u32[]{:S(2)}) copy-start(f32[2,128,128]{2,1,0:T(8,128)S(1)} %collective-permute-done.6.refs_4_) | copy-start | bytes 393220
  52.9 1.3 %collective-permute-start.7 = (f32[2,128,128]{2,1,0:T(8,128)S(1)}, f32[2,128,128]{2,1,0:T(8,128)S(1)}, u32[]{:S(2)}, u32[]{:S(2)}) collective-permute-start(f32[2,128,128]{2,1,0:T(8,128)S(1)} %collective-permute-done.6.refs_4_), channel_id=1, source_target_pairs={{0,4},{4,0},{8,12},{12,8},{16,20},{20,16},{24,28},{28,24},{1,5},{5... | collective-permute-start | bytes 393224 | tf_op jit(solution)/shard_map/ppermute | solution.py:243
  52.9 1.5 %copy-start.3 = (f32[2,128,128]{2,1,0:T(8,128)}, f32[2,128,128]{2,1,0:T(8,128)S(1)}, u32[]{:S(2)}) copy-start(f32[2,128,128]{2,1,0:T(8,128)S(1)} %collective-permute-done.4.refs_2_) | copy-start | bytes 393220
  52.9 1.5 %collective-permute-start.5 = (f32[2,128,128]{2,1,0:T(8,128)S(1)}, f32[2,128,128]{2,1,0:T(8,128)S(1)}, u32[]{:S(2)}, u32[]{:S(2)}) collective-permute-start(f32[2,128,128]{2,1,0:T(8,128)S(1)} %collective-permute-done.4.refs_2_), channel_id=1, source_target_pairs={{0,4},{4,0},{8,12},{12,8},{16,20},{20,16},{24,28},{28,24},{1,5},{5... | collective-permute-start | bytes 393224 | tf_op jit(solution)/shard_map/ppermute | solution.py:243
  53.4 1.0 %copy-start.4 = (f32[2,128,128]{2,1,0:T(8,128)}, f32[2,128,128]{2,1,0:T(8,128)S(1)}, u32[]{:S(2)}) copy-start(f32[2,128,128]{2,1,0:T(8,128)S(1)} %collective-permute-done.3.refs_1_) | copy-start | bytes 393220
  53.4 1.0 %copy-start.5 = (f32[2,128,128]{2,1,0:T(8,128)}, f32[2,128,128]{2,1,0:T(8,128)S(1)}, u32[]{:S(2)}) copy-start(f32[2,128,128]{2,1,0:T(8,128)S(1)} %collective-permute-done.9.refs_7_) | copy-start | bytes 393220
  54.2 0.7 %copy-start.6 = (f32[2,128,128]{2,1,0:T(8,128)}, f32[2,128,128]{2,1,0:T(8,128)S(1)}, u32[]{:S(2)}) copy-start(f32[2,128,128]{2,1,0:T(8,128)S(1)} %collective-permute-done.7.refs_5_) | copy-start | bytes 393220
  54.9 0.6 %copy-start.7 = (f32[2,128,128]{2,1,0:T(8,128)}, f32[2,128,128]{2,1,0:T(8,128)S(1)}, u32[]{:S(2)}) copy-start(f32[2,128,128]{2,1,0:T(8,128)S(1)} %collective-permute-done.5.refs_3_) | copy-start | bytes 393220
where the time goes:
time: 58 us; the launch traced here: 57.8 us
  Pallas kernels  26.8 us (46%)
  waiting for transfers between devices  14.2 us (24%)
  starting transfers between devices  10.9 us (19%)
  local copies, waits for them, and re-layouts  3.94 us (7%)
  between operations  1.35 us (2%)
  other arithmetic  0.64 us (1%)
    pallas_call x1, Pallas kernels, green_of(): pl.pallas_call(functools.partial(chain_kernel, count, total_energies), ou...  24.5 us
    ppermute x3, waiting for transfers between devices, correlate(): lax.ppermute(own, 'energy', [(s, s ^ d) for s in range(groups)])  10.9 us
    ppermute x3, starting transfers between devices, on_device(): lax.ppermute(own, 'slab', [(s, (s - r) % slabs) for s in range(slabs)])  5.97 us
    ppermute x3, starting transfers between devices, correlate(): lax.ppermute(own, 'energy', [(s, s ^ d) for s in range(groups)])  4.39 us
    ppermute x3, waiting for transfers between devices, on_device(): lax.ppermute(own, 'slab', [(s, (s - r) % slabs) for s in range(slabs)])  2.35 us
    pallas_call x1, Pallas kernels, correlate(): pl.pallas_call(kernel, out_shape=jax.ShapeDtypeStruct(own.shape, f32), in...  2.25 us
    unnamed x17, local copies, waits for them, and re-layouts  1.99 us
    squeeze x3, local copies, waits for them, and re-layouts, on_device(): b[1]  1.95 us
  transfers between devices with their start and end apart: 10, of which 6 were waited for; matrix products, arithmetic and copies ran while one was open for 3% of the time, Pallas kernels for 0%

commit v1 on v0

v1 whole, which is shorter than its diff:
```python
import functools

import jax
import jax.numpy as jnp
from jax import lax
from jax.experimental import pallas as pl
from jax.experimental.pallas import tpu as pltpu
from jax.sharding import PartitionSpec as P

f32 = jnp.float32
bf16 = jnp.bfloat16
highest = lax.Precision.HIGHEST
PANEL = 16
TILE = 8


def dot(left, right, dims=((1,), (0,))):
    return lax.dot_general(left, right, (dims, ((), ())), precision=highest, preferred_element_type=f32)


def three_parts(value):
    high = value.astype(bf16)
    rest = value - high.astype(f32)
    middle = rest.astype(bf16)
    low = (rest - middle.astype(f32)).astype(bf16)
    return high, middle, low


def row_of(tile, k):
    return jnp.broadcast_to(tile[k : k + 1, :], tile.shape)


def column_of(tile, k):
    return jnp.broadcast_to(tile[:, k : k + 1], tile.shape)


def lanes_at(tile, index):
    return jnp.take_along_axis(tile, index, axis=1, mode="promise_in_bounds")


def spread_columns(real, imag, base):
    index = [jnp.zeros(real.shape, jnp.int32) + (base + k) for k in range(TILE)]
    return [lanes_at(real, i) for i in index], [lanes_at(imag, i) for i in index]


def eliminate_tiles(pairs, base, row, lane):
    columns = [spread_columns(real, imag, base) for real, imag in pairs]
    pairs = list(pairs)
    for k in range(TILE):
        at_row = row == k
        at_lane = lane == base + k
        cleared = at_row | at_lane
        factors = []
        for dr, di in columns:
            pr, pi = row_of(dr[k], k), row_of(di[k], k)
            inverse = 1.0 / (pr * pr + pi * pi)
            cr, ci = jnp.where(at_row, -1.0, dr[k]), jnp.where(at_row, 0.0, di[k])
            tr, ti = cr * pr + ci * pi, ci * pr - cr * pi
            factors.append((tr, ti, inverse, tr * inverse, ti * inverse))
        for c in range(k + 1, TILE):
            for (dr, di), (tr, ti, inverse, fr, fi) in zip(columns, factors):
                ar, ai = row_of(dr[c], k), row_of(di[c], k)
                zr, zi = jnp.where(at_row, 0.0, dr[c]), jnp.where(at_row, 0.0, di[c])
                if c == k + 1:
                    dr[c] = zr - (tr * ar - ti * ai) * inverse
                    di[c] = zi - (tr * ai + ti * ar) * inverse
                else:
                    dr[c], di[c] = zr - (fr * ar - fi * ai), zi - (fr * ai + fi * ar)
        for m, ((real, imag), (_, _, _, fr, fi)) in enumerate(zip(pairs, factors)):
            ar = jnp.where(at_lane, 1.0, row_of(real, k))
            ai = jnp.where(at_lane, 0.0, row_of(imag, k))
            pairs[m] = (
                jnp.where(cleared, 0.0, real) - (fr * ar - fi * ai),
                jnp.where(cleared, 0.0, imag) - (fr * ai + fi * ar),
            )
    return pairs


def eliminate_panel(panels, first, row, lane):
    tiles = len(panels[0])
    for s in range(tiles):
        base = first + s * TILE
        others = [(s + 1 + u) % tiles for u in range(tiles - 1)]
        columns = [{t: spread_columns(*panel[t], base) for t in others} for panel in panels]
        done = eliminate_tiles([panel[s] for panel in panels], base, row, lane)
        rows = [[(row_of(real, k), row_of(imag, k)) for k in range(TILE)] for real, imag in done]
        inside = (lane >= base) & (lane < base + TILE)
        for t in others:
            for m, panel in enumerate(panels):
                real, imag = panel[t]
                real, imag = jnp.where(inside, 0.0, real), jnp.where(inside, 0.0, imag)
                for cr, ci, (wr, wi) in zip(*columns[m][t], rows[m]):
                    real, imag = real - (cr * wr - ci * wi), imag - (cr * wi + ci * wr)
                panel[t] = (real, imag)
        for m, panel in enumerate(panels):
            panel[s] = done[m]
    return panels


def invert_in_place(ref, count):
    size = ref.shape[-1]
    width = min(PANEL, size)
    tiles = width // TILE

    def step(j, carry):
        first = j * width
        row = lax.broadcasted_iota(jnp.int32, (TILE, size), 0)
        lane = lax.broadcasted_iota(jnp.int32, (TILE, size), 1)
        panels, lefts, results = [], [], []
        for m in range(count):
            at = [pl.ds(pl.multiple_of(first + t * TILE, TILE), TILE) for t in range(tiles)]
            panels.append([(ref[m, 0, rows, :], ref[m, 1, rows, :]) for rows in at])
            parts = [real for real, _ in panels[m]] + [imag for _, imag in panels[m]]
            lh, lm, ll = three_parts(jnp.concatenate(parts, 0))
            lefts.append(jnp.concatenate([lh, lh, lm, lh, lm, ll], 0))
        panels = eliminate_panel(panels, first, row, lane)
        block = (lane >= first) & (lane < first + width)
        full_lane = lax.broadcasted_iota(jnp.int32, (size, size), 1)
        cleared = (full_lane >= first) & (full_lane < first + width)
        for m in range(count):
            wr = jnp.concatenate([jnp.where(block, -real, real) for real, _ in panels[m]], 0)
            wi = jnp.concatenate([jnp.where(block, -imag, imag) for _, imag in panels[m]], 0)
            rh, rm, rl = three_parts(square(wr, wi))
            change = lax.dot_general(
                lefts[m],
                jnp.concatenate([rh, rm, rh, rl, rm, rh], 0),
                (((0,), (0,)), ((), ())),
                preferred_element_type=f32,
            )
            real = jnp.where(cleared, 0.0, ref[m, 0]) - change[:, :size]
            imag = jnp.where(cleared, 0.0, ref[m, 1]) - change[:, size:]
            results.append((real, imag, wr, wi))
        for m, (real, imag, wr, wi) in enumerate(results):
            rows = pl.ds(pl.multiple_of(first, width), width)
            ref[m, 0] = real
            ref[m, 1] = imag
            ref[m, 0, rows, :] = wr
            ref[m, 1, rows, :] = wi
        return carry

    lax.fori_loop(0, size // width, step, 0)


def wide(real, imag):
    return jnp.concatenate([real, imag], 1)


def square(real, imag):
    return jnp.concatenate([wide(real, imag), wide(-imag, real)], 0)


def packed_half(value):
    size = value.shape[0]
    half = size // 2
    row = lax.broadcasted_iota(jnp.int32, (half, size), 0)
    lane = lax.broadcasted_iota(jnp.int32, (half, size), 1)
    quarters = jnp.where((lane < half) | (lane - half > row), pltpu.roll(value[:half], half, 1), value[half:])
    full_row = lax.broadcasted_iota(jnp.int32, (size, size), 0)
    full_lane = lax.broadcasted_iota(jnp.int32, (size, size), 1)
    diagonal = jnp.sum(jnp.where(full_row == full_lane, value, 0.0), axis=0, keepdims=True)
    return jnp.concatenate([quarters, jnp.broadcast_to(diagonal, (TILE, size))], 0)


def unpacked(packed):
    size = packed.shape[1]
    half = size // 2
    quarters = packed[:half]
    whole = jnp.concatenate([pltpu.roll(quarters, half, 1), quarters], 0)
    row = lax.broadcasted_iota(jnp.int32, (size, size), 0)
    lane = lax.broadcasted_iota(jnp.int32, (size, size), 1)
    as_is = ((row < half) & (lane > row)) | ((row >= half) & (lane >= half) & (lane < row))
    full = jnp.where(as_is, whole, whole.T)
    return jnp.where(row == lane, jnp.broadcast_to(packed[half : half + 1], (size, size)), full)


def chain_kernel(count, total_energies, damping_ref, *refs):
    blocks, (green_ref, packed_ref, diagonal_ref, link_ref, work_ref) = refs[:count], refs[count:]
    h_refs, c_refs = [block.at[0] for block in blocks], [block.at[1] for block in blocks]
    size = green_ref.shape[-1]
    slab, position = lax.axis_index("slab"), lax.axis_index("energy")
    energy = -4.0 + 8.0 * position.astype(f32) / (total_energies - 1)
    damping = damping_ref[0]
    row = lax.broadcasted_iota(jnp.int32, (size, size), 0)
    lane = lax.broadcasted_iota(jnp.int32, (size, size), 1)
    identity = jnp.where(row == lane, 1.0, 0.0).astype(f32)

    def is_last(step):
        return lax.rem(slab + step, count) == count - 1

    def cut_link(step):
        return c_refs[step][...] * jnp.where(is_last(step), 0.0, 1.0)

    for step in range(count):
        diagonal_ref[step, 0] = energy * identity - h_refs[step][...]
        diagonal_ref[step, 1] = damping * identity

        @pl.when(is_last(step))
        def _():
            link = c_refs[step][...]
            diagonal_ref[step, 1] = diagonal_ref[step, 1] + 0.5 * dot(link, link, ((1,), (1,)))

    def subtract(node, real, imag):
        diagonal_ref[node, 0] = diagonal_ref[node, 0] - real
        diagonal_ref[node, 1] = diagonal_ref[node, 1] - imag

    for level in range(count.bit_length() - 1):
        stride = 1 << level
        nodes = list(range(0, count, stride))
        odds = nodes[1::2]
        for first in range(0, len(odds), 2):
            group = odds[first : first + 2]
            for m, node in enumerate(group):
                work_ref[m] = diagonal_ref[node]
            invert_in_place(work_ref, len(group))
            for m, node in enumerate(group):
                before, after = node - stride, (node + stride) % count
                middle = (work_ref[m, 0], work_ref[m, 1])
                if level == 0:
                    left = (cut_link(before), None)
                    right = (cut_link(node).T, None)
                else:
                    left = (link_ref[before, 0], link_ref[before, 1])
                    right = (link_ref[node, 0].T, link_ref[node, 1].T)
                if before == after:
                    left = tuple(None if a is None else a + b for a, b in zip(left, right))

                def reached(pair):
                    if pair[1] is None:
                        both = dot(pair[0], wide(*middle))
                    else:
                        both = dot(wide(*pair), square(*middle))
                    return both[:, :size], both[:, size:]

                def closed(pair, end):
                    if end[1] is None:
                        both = dot(jnp.concatenate(pair, 0), end[0], ((1,), (1,)))
                        return both[:size], both[size:]
                    turned = jnp.concatenate([wide(end[0], -end[1]), wide(end[1], end[0])], 0)
                    both = dot(wide(*pair), turned, ((1,), (1,)))
                    return both[:, :size], both[:, size:]

                start = reached(left)
                real, imag = closed(start, left)
                subtract(before, -real, -imag)
                if before != after:
                    real, imag = closed(start, right)
                    link_ref[before, 0] = real
                    link_ref[before, 1] = imag
                    real, imag = closed(reached(right), right)
                    subtract(after, -real, -imag)
    work_ref[0] = diagonal_ref[0]
    invert_in_place(work_ref, 1)
    for part in range(2):
        value = -work_ref[0, part]
        green_ref[part] = value
        packed_ref[part] = packed_half(value)


def green_of(blocks, damping, total_energies):
    count, size = len(blocks), blocks[0].shape[-1]
    whole = pl.BlockSpec(memory_space=pltpu.VMEM)
    scalar = pl.BlockSpec(memory_space=pltpu.SMEM)
    return pl.pallas_call(
        functools.partial(chain_kernel, count, total_energies),
        out_shape=(
            jax.ShapeDtypeStruct((2, size, size), f32),
            jax.ShapeDtypeStruct((2, size // 2 + TILE, size), f32),
        ),
        in_specs=[scalar] + [whole] * count,
        out_specs=(whole, whole),
        scratch_shapes=[
            pltpu.VMEM((count, 2, size, size), f32),
            pltpu.VMEM((count, 2, size, size), f32),
            pltpu.VMEM((2, 2, size, size), f32),
        ],
        name="chain",
    )(damping, *blocks)


def polar_kernel(steps, *refs):
    groups = len(steps)
    blocks, (out_ref, held) = refs[:groups], refs[groups:]
    me = lax.axis_index("energy")
    for step, block in zip(steps, blocks):
        held[me ^ step] = block[...]
    real = imag = jnp.zeros(held.shape[2:], f32)
    for first in range(groups):
        inside = first + me < groups
        second = jnp.where(inside, first + me, 0)
        weight = jnp.where(inside, 1.0 / groups, 0.0)
        br, bi = held[first, 0] * weight, held[first, 1] * weight
        ar, ai = held[second, 0], held[second, 1]
        real = real + (ar * br + ai * bi)
        imag = imag + (ai * br - ar * bi)
    out_ref[0] = unpacked(real)
    out_ref[1] = unpacked(imag)


def correlate(packed, groups):
    def swapped(block, step):
        return lax.ppermute(block, "energy", [(s, s ^ step) for s in range(groups)])

    gathered = [(step, swapped(packed, step)) for step in range(groups - 2, 0, -2)]
    gathered.insert(0, (0, packed))
    gathered = gathered + [(step ^ 1, swapped(block, 1)) for step, block in gathered]
    steps, blocks = zip(*gathered)
    size = packed.shape[-1]
    whole = pl.BlockSpec(memory_space=pltpu.VMEM)
    return pl.pallas_call(
        functools.partial(polar_kernel, steps),
        out_shape=jax.ShapeDtypeStruct((2, size, size), f32),
        in_specs=[whole] * groups,
        out_specs=whole,
        scratch_shapes=[pltpu.VMEM((groups,) + packed.shape, f32)],
        name="polar",
    )(*blocks)


def correlate_spread(own, groups):
    _, size, _ = own.shape
    spread = own.reshape(2, groups, size * size // groups)
    mixed = lax.all_to_all(spread[None], "energy", split_axis=2, concat_axis=0, tiled=True)[:, :, 0]
    real, imag = mixed[:, 0], mixed[:, 1]
    pieces = []
    for offset in range(groups):
        ar, ai = real[offset:], imag[offset:]
        br, bi = real[: groups - offset], imag[: groups - offset]
        pieces.append(jnp.stack([jnp.sum(ar * br + ai * bi, 0), jnp.sum(ai * br - ar * bi, 0)]))
    result = (jnp.stack(pieces) / groups)[:, :, None, :]
    back = lax.all_to_all(result, "energy", split_axis=0, concat_axis=2, tiled=True)
    return back.reshape(own.shape)


def on_device(h_diag, coupling, broadening):
    slabs = lax.axis_size("slab")
    groups = lax.axis_size("energy")
    size = h_diag.shape[-1]
    own = jnp.concatenate([h_diag, coupling], 0)
    blocks = [own] + [
        lax.ppermute(own, "slab", [(s, (s - r) % slabs) for s in range(slabs)]) for r in range(1, slabs)
    ]
    green, packed = green_of(blocks, broadening, groups)
    polar = correlate(packed, groups) if groups <= 8 else correlate_spread(green, groups)
    shape = (1, 1, 2, size, size)
    return green.reshape(shape), polar.reshape(shape)


def solution(mesh):
    return jax.shard_map(
        on_device,
        mesh=mesh,
        in_specs=(P("slab", None, None), P("slab", None, None), P("energy")),
        out_specs=(P("energy", "slab", None, None, None), P("energy", "slab", None, None, None)),
        check_vma=False,
    )
```

time: 58 us -> 47.6 us (0.82)
  Pallas kernels: 26.8 us -> 21.4 us
  waiting for transfers between devices: 14.2 us -> 11.2 us
  local copies, waits for them, and re-layouts: 3.94 us -> 2.58 us
  other arithmetic: 0.64 us -> 0 us
    pallas_call x1, Pallas kernels: 24.5 us -> 19.3 us  [green_of(): pl.pallas_call(functools.partial(chain_kernel, count, total_energies), ou...]
    ppermute x7, waiting for transfers between devices: 11.9 us -> 7.33 us  [swapped(): return lax.ppermute(block, 'energy', [(s, s ^ step) for s in range(groups)])]
    squeeze x3 -> x0, local copies, waits for them, and re-layouts: 1.95 us -> none  [on_device(): b[1]]
    ppermute x3, waiting for transfers between devices: 2.35 us -> 3.9 us  [on_device(): lax.ppermute(own, 'slab', [(s, (s - r) % slabs) for s in range(slabs)])]
    another operation x1 -> x0, other arithmetic: 0.64 us -> none  [green_of(): jnp.stack([slab, position]).astype(jnp.int32)]
    unnamed x17 -> x25, local copies, waits for them, and re-layouts: 1.99 us -> 2.57 us
  transfers between devices with their start and end apart: 10 -> 10, of which waited for: 6 -> 8; matrix products, arithmetic and copies ran while one was open for 3% -> 0% of each run, Pallas kernels for 0% -> 0%
where the time goes in v1:
time: 47.6 us; the launch traced here: 47.3 us
  Pallas kernels  21.4 us (45%)
  waiting for transfers between devices  11.2 us (24%)
  starting transfers between devices  10.7 us (22%)
  local copies, waits for them, and re-layouts  2.58 us (5%)
  between operations  1.38 us (3%)
    pallas_call x1, Pallas kernels, green_of(): pl.pallas_call(functools.partial(chain_kernel, count, total_energies), ou...  19.3 us
    ppermute x7, waiting for transfers between devices, swapped(): return lax.ppermute(block, 'energy', [(s, s ^ step) for s in range(groups)])  7.33 us
    ppermute x3, starting transfers between devices, on_device(): lax.ppermute(own, 'slab', [(s, (s - r) % slabs) for s in range(slabs)])  5.97 us
    ppermute x7, starting transfers between devices, swapped(): return lax.ppermute(block, 'energy', [(s, s ^ step) for s in range(groups)])  4.73 us
    ppermute x3, waiting for transfers between devices, on_device(): lax.ppermute(own, 'slab', [(s, (s - r) % slabs) for s in range(slabs)])  3.9 us
    unnamed x25, local copies, waits for them, and re-layouts  2.57 us
    pallas_call x1, Pallas kernels, correlate(): pl.pallas_call(functools.partial(polar_kernel, steps), out_shape=jax.Shap...  2.09 us
  transfers between devices with their start and end apart: 10, of which 8 were waited for; matrix products, arithmetic and copies ran while one was open for 0% of the time, Pallas kernels for 0%

profile of v1, /device:TPU:0, one launch (start us, length us, event | category | flops | bytes accessed | tf_op | source)
XLA Modules:
  0.0 47.3 jit_solution(15355842323974374663)
XLA Ops:
  0.6 0.0 copy-start.11
  0.6 0.9 %constant_dynamic-update-slice_fusion.1 = f32[2,128,128]{2,1,0:T(8,128)S(1)} fusion(f32[1,128,128]{2,1,0:T(8,128)} %param.3), kind=kLoop, calls=%fused_computation.1 | loop fusion | bytes 131072
  1.5 0.0 copy-done.11
  1.5 0.0 copy-start
  1.5 3.0 %collective-permute-start.2 = (f32[2,128,128]{2,1,0:T(8,128)S(1)}, f32[2,128,128]{2,1,0:T(8,128)S(1)}, u32[]{:S(2)}, u32[]{:S(2)}) collective-permute-start(f32[2,128,128]{2,1,0:T(8,128)S(1)} %constant_dynamic-update-slice_fusion.refs_0_), channel_id=1, source_target_pairs={{0,1},{1,2},{2,3},{3,0},{4,5},{5,6},{6,7},{7,4},{8,9},{9,10},{10,1... | collective-permute-start | bytes 393224 | tf_op jit(solution)/shard_map/ppermute | solution.py:340
  4.6 1.5 %collective-permute-start.1 = (f32[2,128,128]{2,1,0:T(8,128)S(1)}, f32[2,128,128]{2,1,0:T(8,128)S(1)}, u32[]{:S(2)}, u32[]{:S(2)}) collective-permute-start(f32[2,128,128]{2,1,0:T(8,128)S(1)} %constant_dynamic-update-slice_fusion.refs_0_), channel_id=1, source_target_pairs={{0,2},{1,3},{2,0},{3,1},{4,6},{5,7},{6,4},{7,5},{8,10},{9,11},{10,... | collective-permute-start | bytes 393224 | tf_op jit(solution)/shard_map/ppermute | solution.py:340
  6.1 1.4 %collective-permute-start = (f32[2,128,128]{2,1,0:T(8,128)S(1)}, f32[2,128,128]{2,1,0:T(8,128)S(1)}, u32[]{:S(2)}, u32[]{:S(2)}) collective-permute-start(f32[2,128,128]{2,1,0:T(8,128)S(1)} %constant_dynamic-update-slice_fusion.refs_0_), channel_id=1, source_target_pairs={{0,3},{1,0},{2,1},{3,2},{4,7},{5,4},{6,5},{7,6},{8,11},{9,8},{10,9... | collective-permute-start | bytes 393224 | tf_op jit(solution)/shard_map/ppermute | solution.py:340
  8.2 1.7 %collective-permute-done.2.refs_3_ = f32[2,128,128]{2,1,0:T(8,128)S(1)} collective-permute-done((f32[2,128,128]{2,1,0:T(8,128)S(1)}, f32[2,128,128]{2,1,0:T(8,128)S(1)}, u32[]{:S(2)}, u32[]{:S(2)}) %collective-permute-start.2) | collective-permute-done | bytes 131104 | tf_op jit(solution)/shard_map/ppermute | solution.py:340
  9.9 0.0 copy-start.1
  9.9 2.0 %collective-permute-done.1.refs_2_ = f32[2,128,128]{2,1,0:T(8,128)S(1)} collective-permute-done((f32[2,128,128]{2,1,0:T(8,128)S(1)}, f32[2,128,128]{2,1,0:T(8,128)S(1)}, u32[]{:S(2)}, u32[]{:S(2)}) %collective-permute-start.1) | collective-permute-done | bytes 131104 | tf_op jit(solution)/shard_map/ppermute | solution.py:340
  11.8 0.0 copy-start.2
  11.8 0.2 collective-permute-done.refs_1_
  12.1 0.0 copy-done
  12.1 0.0 copy-done.1
  12.1 0.4 copy-done.2
  12.5 0.0 copy-start.3
  12.5 0.6 %copy-done.3 = f32[2,128,128]{2,1,0:T(8,128)} copy-done((f32[2,128,128]{2,1,0:T(8,128)}, f32[2,128,128]{2,1,0:T(8,128)S(1)}, u32[]{:S(2)}) %copy-start.3) | copy-done | bytes 131096
  13.1 19.3 %chain.1 = (f32[2,128,128]{2,1,0:T(8,128)}, f32[2,72,128]{2,1,0:T(8,128)}) custom-call(f32[1]{0:T(128)S(6)} %copy.6.damping_ref, f32[2,128,128]{2,1,0:T(8,128)} %copy-done, f32[2,128,128]{2,1,0:T(8,128)} %copy-done.3, f32[2,128,128]{2,1,0:T(8,128)} %copy-done.2, f32[2,128,128]{2,1,0:T(8,128)} %copy-done.1), custom_call_target="tpu_custom_call" | custom-call | tf_op jit(solution)/shard_map/chain/pallas_call | solution.py:263
  32.5 1.8 %collective-permute-start.5 = (f32[2,72,128]{2,1,0:T(8,128)}, f32[2,72,128]{2,1,0:T(8,128)S(1)}, u32[]{:S(2)}, u32[]{:S(2)}) collective-permute-start(f32[2,72,128]{2,1,0:T(8,128)} %get-tuple-element.5.refs_0_), channel_id=1, source_target_pairs={{0,8},{4,12},{8,0},{12,4},{16,24},{20,28},{24,16},{28,20},{1,9},{5... | collective-permute-start | bytes 221192 | tf_op jit(solution)/shard_map/ppermute | solution.py:301
  34.2 2.6 %collective-permute-start.4 = (f32[2,72,128]{2,1,0:T(8,128)}, f32[2,72,128]{2,1,0:T(8,128)S(1)}, u32[]{:S(2)}, u32[]{:S(2)}) collective-permute-start(f32[2,72,128]{2,1,0:T(8,128)} %get-tuple-element.5.refs_0_), channel_id=1, source_target_pairs={{0,16},{4,20},{8,24},{12,28},{16,0},{20,4},{24,8},{28,12},{1,17},{... | collective-permute-start | bytes 221192 | tf_op jit(solution)/shard_map/ppermute | solution.py:301
  36.8 0.0 collective-permute-start.3
  36.8 0.0 collective-permute-start.6
  36.8 0.2 collective-permute-done.5.refs_3_
  37.0 0.0 copy-start.4
  37.0 0.3 collective-permute-start.9
  37.4 5.1 %collective-permute-done.4.refs_2_ = f32[2,72,128]{2,1,0:T(8,128)S(1)} collective-permute-done((f32[2,72,128]{2,1,0:T(8,128)}, f32[2,72,128]{2,1,0:T(8,128)S(1)}, u32[]{:S(2)}, u32[]{:S(2)}) %collective-permute-start.4) | collective-permute-done | bytes 73760 | tf_op jit(solution)/shard_map/ppermute | solution.py:301
  42.4 0.0 copy-start.5
  42.4 0.0 collective-permute-start.8
  42.4 0.8 %collective-permute-done.3.refs_1_ = f32[2,72,128]{2,1,0:T(8,128)S(1)} collective-permute-done((f32[2,72,128]{2,1,0:T(8,128)}, f32[2,72,128]{2,1,0:T(8,128)S(1)}, u32[]{:S(2)}, u32[]{:S(2)}) %collective-permute-start.3) | collective-permute-done | bytes 73760 | tf_op jit(solution)/shard_map/ppermute | solution.py:301
  43.3 0.0 copy-start.6
  43.3 0.0 collective-permute-start.7
  43.3 0.0 collective-permute-done.6.refs_4_
  43.3 0.0 copy-start.7
  43.3 0.0 collective-permute-done.9.refs_7_
  43.3 0.0 copy-start.8
  43.3 0.4 collective-permute-done.8.refs_6_
  43.7 0.0 copy-start.9
  43.7 0.8 %collective-permute-done.7.refs_5_ = f32[2,72,128]{2,1,0:T(8,128)S(1)} collective-permute-done((f32[2,72,128]{2,1,0:T(8,128)S(1)}, f32[2,72,128]{2,1,0:T(8,128)S(1)}, u32[]{:S(2)}, u32[]{:S(2)}) %collective-permute-start.7) | collective-permute-done | bytes 73760 | tf_op jit(solution)/shard_map/ppermute | solution.py:301
  44.6 0.0 copy-done.4
  44.6 0.0 copy-done.5
  44.6 0.0 copy-done.6
  44.6 0.0 copy-done.7
  44.6 0.0 copy-done.8
  44.6 0.0 copy-done.9
  44.6 0.0 copy-start.10
  44.6 0.6 %copy-done.10 = f32[2,72,128]{2,1,0:T(8,128)} copy-done((f32[2,72,128]{2,1,0:T(8,128)}, f32[2,72,128]{2,1,0:T(8,128)S(1)}, u32[]{:S(2)}) %copy-start.10) | copy-done | bytes 73752
  45.2 2.1 %polar.1 = f32[2,128,128]{2,1,0:T(8,128)} custom-call(f32[2,72,128]{2,1,0:T(8,128)} %get-tuple-element.5.refs_0_, f32[2,72,128]{2,1,0:T(8,128)} %copy-done.6, f32[2,72,128]{2,1,0:T(8,128)} %copy-done.5, f32[2,72,128]{2,1,0:T(8,128)} %copy-done.4, f32[2,72,128]{2,1,0:T(8,128)} %copy-done.7, f32[2,72,128]{2,1,0:T(8,128)} %copy-done.10, ...), custom_call_target="tpu_custom_call" | custom-call | tf_op jit(solution)/shard_map/polar/pallas_call | solution.py:309
  (1 shorter events, 0.0 us)
Async XLA Ops:
  0.6 0.9 %copy-start.11 = (f32[1,128,128]{2,1,0:T(8,128)S(1)}, f32[1,128,128]{2,1,0:T(8,128)}, u32[]{:S(2)}) copy-start(f32[1,128,128]{2,1,0:T(8,128)} %param.4) | copy-start | bytes 196612
  1.5 10.5 %copy-start = (f32[2,128,128]{2,1,0:T(8,128)}, f32[2,128,128]{2,1,0:T(8,128)S(1)}, u32[]{:S(2)}) copy-start(f32[2,128,128]{2,1,0:T(8,128)S(1)} %constant_dynamic-update-slice_fusion.refs_0_) | copy-start | bytes 393220
  1.5 8.3 %collective-permute-start.2 = (f32[2,128,128]{2,1,0:T(8,128)S(1)}, f32[2,128,128]{2,1,0:T(8,128)S(1)}, u32[]{:S(2)}, u32[]{:S(2)}) collective-permute-start(f32[2,128,128]{2,1,0:T(8,128)S(1)} %constant_dynamic-update-slice_fusion.refs_0_), channel_id=1, source_target_pairs={{0,1},{1,2},{2,3},{3,0},{4,5},{5,6},{6,7},{7,4},{8,9},{9,10},{10,1... | collective-permute-start | bytes 393224 | tf_op jit(solution)/shard_map/ppermute | solution.py:340
  4.6 7.3 %collective-permute-start.1 = (f32[2,128,128]{2,1,0:T(8,128)S(1)}, f32[2,128,128]{2,1,0:T(8,128)S(1)}, u32[]{:S(2)}, u32[]{:S(2)}) collective-permute-start(f32[2,128,128]{2,1,0:T(8,128)S(1)} %constant_dynamic-update-slice_fusion.refs_0_), channel_id=1, source_target_pairs={{0,2},{1,3},{2,0},{3,1},{4,6},{5,7},{6,4},{7,5},{8,10},{9,11},{10,... | collective-permute-start | bytes 393224 | tf_op jit(solution)/shard_map/ppermute | solution.py:340
  6.1 6.0 %collective-permute-start = (f32[2,128,128]{2,1,0:T(8,128)S(1)}, f32[2,128,128]{2,1,0:T(8,128)S(1)}, u32[]{:S(2)}, u32[]{:S(2)}) collective-permute-start(f32[2,128,128]{2,1,0:T(8,128)S(1)} %constant_dynamic-update-slice_fusion.refs_0_), channel_id=1, source_target_pairs={{0,3},{1,0},{2,1},{3,2},{4,7},{5,4},{6,5},{7,6},{8,11},{9,8},{10,9... | collective-permute-start | bytes 393224 | tf_op jit(solution)/shard_map/ppermute | solution.py:340
  9.9 2.2 %copy-start.1 = (f32[2,128,128]{2,1,0:T(8,128)}, f32[2,128,128]{2,1,0:T(8,128)S(1)}, u32[]{:S(2)}) copy-start(f32[2,128,128]{2,1,0:T(8,128)S(1)} %collective-permute-done.2.refs_3_) | copy-start | bytes 393220
  11.8 0.6 %copy-start.2 = (f32[2,128,128]{2,1,0:T(8,128)}, f32[2,128,128]{2,1,0:T(8,128)S(1)}, u32[]{:S(2)}) copy-start(f32[2,128,128]{2,1,0:T(8,128)S(1)} %collective-permute-done.1.refs_2_) | copy-start | bytes 393220
  12.5 0.6 %copy-start.3 = (f32[2,128,128]{2,1,0:T(8,128)}, f32[2,128,128]{2,1,0:T(8,128)S(1)}, u32[]{:S(2)}) copy-start(f32[2,128,128]{2,1,0:T(8,128)S(1)} %collective-permute-done.refs_1_) | copy-start | bytes 393220
  32.5 4.6 %collective-permute-start.5 = (f32[2,72,128]{2,1,0:T(8,128)}, f32[2,72,128]{2,1,0:T(8,128)S(1)}, u32[]{:S(2)}, u32[]{:S(2)}) collective-permute-start(f32[2,72,128]{2,1,0:T(8,128)} %get-tuple-element.5.refs_0_), channel_id=1, source_target_pairs={{0,8},{4,12},{8,0},{12,4},{16,24},{20,28},{24,16},{28,20},{1,9},{5... | collective-permute-start | bytes 221192 | tf_op jit(solution)/shard_map/ppermute | solution.py:301
  34.2 8.2 %collective-permute-start.4 = (f32[2,72,128]{2,1,0:T(8,128)}, f32[2,72,128]{2,1,0:T(8,128)S(1)}, u32[]{:S(2)}, u32[]{:S(2)}) collective-permute-start(f32[2,72,128]{2,1,0:T(8,128)} %get-tuple-element.5.refs_0_), channel_id=1, source_target_pairs={{0,16},{4,20},{8,24},{12,28},{16,0},{20,4},{24,8},{28,12},{1,17},{... | collective-permute-start | bytes 221192 | tf_op jit(solution)/shard_map/ppermute | solution.py:301
  36.8 6.5 %collective-permute-start.3 = (f32[2,72,128]{2,1,0:T(8,128)}, f32[2,72,128]{2,1,0:T(8,128)S(1)}, u32[]{:S(2)}, u32[]{:S(2)}) collective-permute-start(f32[2,72,128]{2,1,0:T(8,128)} %get-tuple-element.5.refs_0_), channel_id=1, source_target_pairs={{0,24},{4,28},{8,16},{12,20},{16,8},{20,12},{24,0},{28,4},{1,25},{... | collective-permute-start | bytes 221192 | tf_op jit(solution)/shard_map/ppermute | solution.py:301
  36.8 6.5 %collective-permute-start.6 = (f32[2,72,128]{2,1,0:T(8,128)}, f32[2,72,128]{2,1,0:T(8,128)S(1)}, u32[]{:S(2)}, u32[]{:S(2)}) collective-permute-start(f32[2,72,128]{2,1,0:T(8,128)} %get-tuple-element.5.refs_0_), channel_id=1, source_target_pairs={{0,4},{4,0},{8,12},{12,8},{16,20},{20,16},{24,28},{28,24},{1,5},{5... | collective-permute-start | bytes 221192 | tf_op jit(solution)/shard_map/ppermute | solution.py:301
  37.0 7.5 %copy-start.4 = (f32[2,72,128]{2,1,0:T(8,128)}, f32[2,72,128]{2,1,0:T(8,128)S(1)}, u32[]{:S(2)}) copy-start(f32[2,72,128]{2,1,0:T(8,128)S(1)} %collective-permute-done.5.refs_3_) | copy-start | bytes 221188
  37.0 6.3 %collective-permute-start.9 = (f32[2,72,128]{2,1,0:T(8,128)S(1)}, f32[2,72,128]{2,1,0:T(8,128)S(1)}, u32[]{:S(2)}, u32[]{:S(2)}) collective-permute-start(f32[2,72,128]{2,1,0:T(8,128)S(1)} %collective-permute-done.5.refs_3_), channel_id=1, source_target_pairs={{0,4},{4,0},{8,12},{12,8},{16,20},{20,16},{24,28},{28,24},{1,5},{5... | collective-permute-start | bytes 221192 | tf_op jit(solution)/shard_map/ppermute | solution.py:301
  42.4 2.1 %copy-start.5 = (f32[2,72,128]{2,1,0:T(8,128)}, f32[2,72,128]{2,1,0:T(8,128)S(1)}, u32[]{:S(2)}) copy-start(f32[2,72,128]{2,1,0:T(8,128)S(1)} %collective-permute-done.4.refs_2_) | copy-start | bytes 221188
  42.4 1.3 %collective-permute-start.8 = (f32[2,72,128]{2,1,0:T(8,128)S(1)}, f32[2,72,128]{2,1,0:T(8,128)S(1)}, u32[]{:S(2)}, u32[]{:S(2)}) collective-permute-start(f32[2,72,128]{2,1,0:T(8,128)S(1)} %collective-permute-done.4.refs_2_), channel_id=1, source_target_pairs={{0,4},{4,0},{8,12},{12,8},{16,20},{20,16},{24,28},{28,24},{1,5},{5... | collective-permute-start | bytes 221192 | tf_op jit(solution)/shard_map/ppermute | solution.py:301
  43.3 1.3 %copy-start.6 = (f32[2,72,128]{2,1,0:T(8,128)}, f32[2,72,128]{2,1,0:T(8,128)S(1)}, u32[]{:S(2)}) copy-start(f32[2,72,128]{2,1,0:T(8,128)S(1)} %collective-permute-done.3.refs_1_) | copy-start | bytes 221188
  43.3 1.3 %collective-permute-start.7 = (f32[2,72,128]{2,1,0:T(8,128)S(1)}, f32[2,72,128]{2,1,0:T(8,128)S(1)}, u32[]{:S(2)}, u32[]{:S(2)}) collective-permute-start(f32[2,72,128]{2,1,0:T(8,128)S(1)} %collective-permute-done.3.refs_1_), channel_id=1, source_target_pairs={{0,4},{4,0},{8,12},{12,8},{16,20},{20,16},{24,28},{28,24},{1,5},{5... | collective-permute-start | bytes 221192 | tf_op jit(solution)/shard_map/ppermute | solution.py:301
  43.3 1.3 %copy-start.7 = (f32[2,72,128]{2,1,0:T(8,128)}, f32[2,72,128]{2,1,0:T(8,128)S(1)}, u32[]{:S(2)}) copy-start(f32[2,72,128]{2,1,0:T(8,128)S(1)} %collective-permute-done.6.refs_4_) | copy-start | bytes 221188
  43.3 1.3 %copy-start.8 = (f32[2,72,128]{2,1,0:T(8,128)}, f32[2,72,128]{2,1,0:T(8,128)S(1)}, u32[]{:S(2)}) copy-start(f32[2,72,128]{2,1,0:T(8,128)S(1)} %collective-permute-done.9.refs_7_) | copy-start | bytes 221188
  43.7 0.9 %copy-start.9 = (f32[2,72,128]{2,1,0:T(8,128)}, f32[2,72,128]{2,1,0:T(8,128)S(1)}, u32[]{:S(2)}) copy-start(f32[2,72,128]{2,1,0:T(8,128)S(1)} %collective-permute-done.8.refs_6_) | copy-start | bytes 221188
  44.6 0.6 %copy-start.10 = (f32[2,72,128]{2,1,0:T(8,128)}, f32[2,72,128]{2,1,0:T(8,128)S(1)}, u32[]{:S(2)}) copy-start(f32[2,72,128]{2,1,0:T(8,128)S(1)} %collective-permute-done.7.refs_5_) | copy-start | bytes 221188

commit v2 on v1

--- a/solution.py
+++ b/solution.py
@@ -9,13 +9,8 @@
 
 f32 = jnp.float32
 bf16 = jnp.bfloat16
-highest = lax.Precision.HIGHEST
 PANEL = 16
 TILE = 8
-
-
-def dot(left, right, dims=((1,), (0,))):
-    return lax.dot_general(left, right, (dims, ((), ())), precision=highest, preferred_element_type=f32)
 
 
 def three_parts(value):
@@ -173,36 +168,59 @@
     return jnp.where(row == lane, jnp.broadcast_to(packed[half : half + 1], (size, size)), full)
 
 
+def exact_dot(left, right, dims):
+    (over_left,), (over_right,) = dims
+    lh, lm, ll = three_parts(left)
+    rh, rm, rl = three_parts(right)
+    return lax.dot_general(
+        jnp.concatenate([lh, lh, lm, lh, lm, ll], over_left),
+        jnp.concatenate([rh, rm, rh, rl, rm, rh], over_right),
+        (dims, ((), ())),
+        preferred_element_type=f32,
+    )
+
+
 def chain_kernel(count, total_energies, damping_ref, *refs):
-    blocks, (green_ref, packed_ref, diagonal_ref, link_ref, work_ref) = refs[:count], refs[count:]
-    h_refs, c_refs = [block.at[0] for block in blocks], [block.at[1] for block in blocks]
+    blocks, refs = refs[:count], refs[count:]
+    green_ref, packed_ref, slab_ref, diagonal_ref, link_ref, work_ref, arrived = refs
     size = green_ref.shape[-1]
     slab, position = lax.axis_index("slab"), lax.axis_index("energy")
     energy = -4.0 + 8.0 * position.astype(f32) / (total_energies - 1)
     damping = damping_ref[0]
+    copies = [
+        pltpu.make_async_copy(blocks[d], slab_ref.at[((slab ^ d) - slab) & (count - 1)], arrived.at[d])
+        for d in range(count)
+    ]
+    in_order = list(range(1, count, 2)) + list(range(0, count, 2))
+    for d in in_order:
+        copies[d].start()
     row = lax.broadcasted_iota(jnp.int32, (size, size), 0)
     lane = lax.broadcasted_iota(jnp.int32, (size, size), 1)
     identity = jnp.where(row == lane, 1.0, 0.0).astype(f32)
 
     def is_last(step):
-        return lax.rem(slab + step, count) == count - 1
+        return ((slab + step) & (count - 1)) == count - 1
 
     def cut_link(step):
-        return c_refs[step][...] * jnp.where(is_last(step), 0.0, 1.0)
-
-    for step in range(count):
-        diagonal_ref[step, 0] = energy * identity - h_refs[step][...]
-        diagonal_ref[step, 1] = damping * identity
-
-        @pl.when(is_last(step))
-        def _():
-            link = c_refs[step][...]
-            diagonal_ref[step, 1] = diagonal_ref[step, 1] + 0.5 * dot(link, link, ((1,), (1,)))
+        return slab_ref[step, 1] * jnp.where(is_last(step), 0.0, 1.0)
+
+    def place(steps):
+        for d in steps:
+            copies[d].wait()
+        for step in steps:
+            diagonal_ref[step, 0] = energy * identity - slab_ref[step, 0]
+            diagonal_ref[step, 1] = damping * identity
+
+            @pl.when(is_last(step))
+            def _():
+                link = slab_ref[step, 1]
+                diagonal_ref[step, 1] = diagonal_ref[step, 1] + 0.5 * exact_dot(link, link, ((1,), (1,)))
 
     def subtract(node, real, imag):
         diagonal_ref[node, 0] = diagonal_ref[node, 0] - real
         diagonal_ref[node, 1] = diagonal_ref[node, 1] - imag
 
+    place(range(1, count, 2))
     for level in range(count.bit_length() - 1):
         stride = 1 << level
         nodes = list(range(0, count, stride))
@@ -212,42 +230,34 @@
             for m, node in enumerate(group):
                 work_ref[m] = diagonal_ref[node]
             invert_in_place(work_ref, len(group))
+            if level == 0 and first == 0:
+                place(range(0, count, 2))
             for m, node in enumerate(group):
                 before, after = node - stride, (node + stride) % count
                 middle = (work_ref[m, 0], work_ref[m, 1])
                 if level == 0:
-                    left = (cut_link(before), None)
-                    right = (cut_link(node).T, None)
+                    ends = [(cut_link(before),), (cut_link(node).T,)]
                 else:
-                    left = (link_ref[before, 0], link_ref[before, 1])
-                    right = (link_ref[node, 0].T, link_ref[node, 1].T)
+                    ends = [(link_ref[before, 0], link_ref[before, 1]), (link_ref[node, 0].T, link_ref[node, 1].T)]
                 if before == after:
-                    left = tuple(None if a is None else a + b for a, b in zip(left, right))
-
-                def reached(pair):
-                    if pair[1] is None:
-                        both = dot(pair[0], wide(*middle))
-                    else:
-                        both = dot(wide(*pair), square(*middle))
-                    return both[:, :size], both[:, size:]
-
-                def closed(pair, end):
-                    if end[1] is None:
-                        both = dot(jnp.concatenate(pair, 0), end[0], ((1,), (1,)))
-                        return both[:size], both[size:]
-                    turned = jnp.concatenate([wide(end[0], -end[1]), wide(end[1], end[0])], 0)
-                    both = dot(wide(*pair), turned, ((1,), (1,)))
-                    return both[:, :size], both[:, size:]
-
-                start = reached(left)
-                real, imag = closed(start, left)
-                subtract(before, -real, -imag)
+                    ends = [tuple(a + b for a, b in zip(*ends))]
+                ends = tuple(jnp.concatenate(parts, 0) for parts in zip(*ends))
+                height = ends[0].shape[0]
+                if level == 0:
+                    both = exact_dot(ends[0], wide(*middle), ((1,), (0,)))
+                    both = jnp.concatenate([both[:, :size], both[:, size:]], 0)
+                    both = exact_dot(both, ends[0], ((1,), (1,)))
+                    real, imag = both[:height], both[height:]
+                else:
+                    both = exact_dot(wide(*ends), square(*middle), ((1,), (0,)))
+                    turned = jnp.concatenate([wide(ends[0], -ends[1]), wide(ends[1], ends[0])], 0)
+                    both = exact_dot(both, turned, ((1,), (1,)))
+                    real, imag = both[:, :height], both[:, height:]
+                subtract(before, -real[:size, :size], -imag[:size, :size])
                 if before != after:
-                    real, imag = closed(start, right)
-                    link_ref[before, 0] = real
-                    link_ref[before, 1] = imag
-                    real, imag = closed(reached(right), right)
-                    subtract(after, -real, -imag)
+                    subtract(after, -real[size:, size:], -imag[size:, size:])
+                    link_ref[before, 0] = real[:size, size:]
+                    link_ref[before, 1] = imag[:size, size:]
     work_ref[0] = diagonal_ref[0]
     invert_in_place(work_ref, 1)
     for part in range(2):
@@ -266,12 +276,14 @@
             jax.ShapeDtypeStruct((2, size, size), f32),
             jax.ShapeDtypeStruct((2, size // 2 + TILE, size), f32),
         ),
-        in_specs=[scalar] + [whole] * count,
+        in_specs=[scalar] + [pl.BlockSpec(memory_space=pl.ANY)] * count,
         out_specs=(whole, whole),
         scratch_shapes=[
             pltpu.VMEM((count, 2, size, size), f32),
             pltpu.VMEM((count, 2, size, size), f32),
+            pltpu.VMEM((count, 2, size, size), f32),
             pltpu.VMEM((2, 2, size, size), f32),
+            pltpu.SemaphoreType.DMA((count,)),
         ],
         name="chain",
     )(damping, *blocks)
@@ -279,10 +291,16 @@
 
 def polar_kernel(steps, *refs):
     groups = len(steps)
-    blocks, (out_ref, held) = refs[:groups], refs[groups:]
+    blocks, (out_ref, held, arrived) = refs[:groups], refs[groups:]
     me = lax.axis_index("energy")
-    for step, block in zip(steps, blocks):
-        held[me ^ step] = block[...]
+    copies = [
+        pltpu.make_async_copy(block, held.at[me ^ step], arrived.at[i])
+        for i, (step, block) in enumerate(zip(steps, blocks))
+    ]
+    for copy in copies:
+        copy.start()
+    for copy in copies:
+        copy.wait()
     real = imag = jnp.zeros(held.shape[2:], f32)
     for first in range(groups):
         inside = first + me < groups
@@ -309,9 +327,9 @@
     return pl.pallas_call(
         functools.partial(polar_kernel, steps),
         out_shape=jax.ShapeDtypeStruct((2, size, size), f32),
-        in_specs=[whole] * groups,
+        in_specs=[pl.BlockSpec(memory_space=pl.ANY)] * groups,
         out_specs=whole,
-        scratch_shapes=[pltpu.VMEM((groups,) + packed.shape, f32)],
+        scratch_shapes=[pltpu.VMEM((groups,) + packed.shape, f32), pltpu.SemaphoreType.DMA((groups,))],
         name="polar",
     )(*blocks)
 
@@ -336,9 +354,10 @@
     groups = lax.axis_size("energy")
     size = h_diag.shape[-1]
     own = jnp.concatenate([h_diag, coupling], 0)
-    blocks = [own] + [
-        lax.ppermute(own, "slab", [(s, (s - r) % slabs) for s in range(slabs)]) for r in range(1, slabs)
-    ]
+    blocks = {0: own}
+    for d in list(range(slabs - 1, 0, -2)) + list(range(slabs - 2, 0, -2)):
+        blocks[d] = lax.ppermute(own, "slab", [(s, s ^ d) for s in range(slabs)])
+    blocks = [blocks[d] for d in range(slabs)]
     green, packed = green_of(blocks, broadening, groups)
     polar = correlate(packed, groups) if groups <= 8 else correlate_spread(green, groups)
     shape = (1, 1, 2, size, size)

time: 47.6 us -> 46.6 us (0.979)
  waiting for transfers between devices: 11.2 us -> 12.6 us
  starting transfers between devices: 10.7 us -> 9.43 us
  Pallas kernels: 21.4 us -> 20.4 us
    ppermute x3, waiting for transfers between devices: 3.9 us -> 5.26 us  [on_device(): blocks[d] = lax.ppermute(own, 'slab', [(s, s ^ d) for s in range(slabs)])]
    ppermute x3, starting transfers between devices: 5.97 us -> 4.63 us  [on_device(): blocks[d] = lax.ppermute(own, 'slab', [(s, s ^ d) for s in range(slabs)])]
    pallas_call x1, Pallas kernels: 19.3 us -> 18.3 us  [green_of(): pl.pallas_call(functools.partial(chain_kernel, count, total_energies), ou...]
where the time goes in v2:
time: 46.6 us; the launch traced here: 46.3 us
  Pallas kernels  20.4 us (44%)
  waiting for transfers between devices  12.6 us (27%)
  starting transfers between devices  9.43 us (20%)
  local copies, waits for them, and re-layouts  2.58 us (6%)
  between operations  1.39 us (3%)
    pallas_call x1, Pallas kernels, green_of(): pl.pallas_call(functools.partial(chain_kernel, count, total_energies), ou...  18.3 us
    ppermute x7, waiting for transfers between devices, swapped(): return lax.ppermute(block, 'energy', [(s, s ^ step) for s in range(groups)])  7.32 us
    ppermute x3, waiting for transfers between devices, on_device(): blocks[d] = lax.ppermute(own, 'slab', [(s, s ^ d) for s in range(slabs)])  5.26 us
    ppermute x7, starting transfers between devices, swapped(): return lax.ppermute(block, 'energy', [(s, s ^ step) for s in range(groups)])  4.8 us
    ppermute x3, starting transfers between devices, on_device(): blocks[d] = lax.ppermute(own, 'slab', [(s, s ^ d) for s in range(slabs)])  4.63 us
    unnamed x25, local copies, waits for them, and re-layouts  2.57 us
    pallas_call x1, Pallas kernels, correlate(): pl.pallas_call(functools.partial(polar_kernel, steps), out_shape=jax.Shap...  2.11 us
  transfers between devices with their start and end apart: 10, of which 8 were waited for; matrix products, arithmetic and copies ran while one was open for 0% of the time, Pallas kernels for 0%

profile of v2, /device:TPU:0, one launch (start us, length us, event | category | flops | bytes accessed | tf_op | source)
XLA Modules:
  0.0 46.3 jit_solution(16250117927545008344)
XLA Ops:
  0.6 0.0 copy-start.11
  0.6 0.9 %constant_dynamic-update-slice_fusion.1 = f32[2,128,128]{2,1,0:T(8,128)S(1)} fusion(f32[1,128,128]{2,1,0:T(8,128)} %param.3), kind=kLoop, calls=%fused_computation.1 | loop fusion | bytes 131072
  1.5 0.0 copy-done.11
  1.5 0.0 copy-start
  1.5 4.0 %collective-permute-start.2 = (f32[2,128,128]{2,1,0:T(8,128)S(1)}, f32[2,128,128]{2,1,0:T(8,128)S(1)}, u32[]{:S(2)}, u32[]{:S(2)}) collective-permute-start(f32[2,128,128]{2,1,0:T(8,128)S(1)} %constant_dynamic-update-slice_fusion.refs_0_), channel_id=1, source_target_pairs={{0,3},{1,2},{2,1},{3,0},{4,7},{5,6},{6,5},{7,4},{8,11},{9,10},{10,... | collective-permute-start | bytes 393224 | tf_op jit(solution)/shard_map/ppermute | solution.py:359
  5.5 0.5 %collective-permute-start.1 = (f32[2,128,128]{2,1,0:T(8,128)S(1)}, f32[2,128,128]{2,1,0:T(8,128)S(1)}, u32[]{:S(2)}, u32[]{:S(2)}) collective-permute-start(f32[2,128,128]{2,1,0:T(8,128)S(1)} %constant_dynamic-update-slice_fusion.refs_0_), channel_id=1, source_target_pairs={{0,2},{1,3},{2,0},{3,1},{4,6},{5,7},{6,4},{7,5},{8,10},{9,11},{10,... | collective-permute-start | bytes 393224 | tf_op jit(solution)/shard_map/ppermute | solution.py:359
  6.0 0.1 collective-permute-start
  6.8 2.6 %collective-permute-done.2.refs_3_ = f32[2,128,128]{2,1,0:T(8,128)S(1)} collective-permute-done((f32[2,128,128]{2,1,0:T(8,128)S(1)}, f32[2,128,128]{2,1,0:T(8,128)S(1)}, u32[]{:S(2)}, u32[]{:S(2)}) %collective-permute-start.2) | collective-permute-done | bytes 131104 | tf_op jit(solution)/shard_map/ppermute | solution.py:359
  9.4 0.0 copy-start.1
  9.4 2.4 %collective-permute-done.1.refs_2_ = f32[2,128,128]{2,1,0:T(8,128)S(1)} collective-permute-done((f32[2,128,128]{2,1,0:T(8,128)S(1)}, f32[2,128,128]{2,1,0:T(8,128)S(1)}, u32[]{:S(2)}, u32[]{:S(2)}) %collective-permute-start.1) | collective-permute-done | bytes 131104 | tf_op jit(solution)/shard_map/ppermute | solution.py:359
  11.8 0.0 copy-start.2
  11.8 0.2 collective-permute-done.refs_1_
  12.1 0.0 copy-done
  12.1 0.0 copy-done.1
  12.1 0.4 copy-done.2
  12.5 0.0 copy-start.3
  12.5 0.6 %copy-done.3 = f32[2,128,128]{2,1,0:T(8,128)} copy-done((f32[2,128,128]{2,1,0:T(8,128)}, f32[2,128,128]{2,1,0:T(8,128)S(1)}, u32[]{:S(2)}) %copy-start.3) | copy-done | bytes 131096
  13.1 18.3 %chain.1 = (f32[2,128,128]{2,1,0:T(8,128)}, f32[2,72,128]{2,1,0:T(8,128)}) custom-call(f32[1]{0:T(128)S(6)} %copy.6.damping_ref, f32[2,128,128]{2,1,0:T(8,128)} %copy-done, f32[2,128,128]{2,1,0:T(8,128)} %copy-done.3, f32[2,128,128]{2,1,0:T(8,128)} %copy-done.2, f32[2,128,128]{2,1,0:T(8,128)} %copy-done.1), custom_call_target="tpu_custom_call" | custom-call | tf_op jit(solution)/shard_map/chain/pallas_call | solution.py:273
  31.4 1.8 %collective-permute-start.5 = (f32[2,72,128]{2,1,0:T(8,128)}, f32[2,72,128]{2,1,0:T(8,128)S(1)}, u32[]{:S(2)}, u32[]{:S(2)}) collective-permute-start(f32[2,72,128]{2,1,0:T(8,128)} %get-tuple-element.5.refs_0_), channel_id=1, source_target_pairs={{0,8},{4,12},{8,0},{12,4},{16,24},{20,28},{24,16},{28,20},{1,9},{5... | collective-permute-start | bytes 221192 | tf_op jit(solution)/shard_map/ppermute | solution.py:319
  33.2 2.6 %collective-permute-start.4 = (f32[2,72,128]{2,1,0:T(8,128)}, f32[2,72,128]{2,1,0:T(8,128)S(1)}, u32[]{:S(2)}, u32[]{:S(2)}) collective-permute-start(f32[2,72,128]{2,1,0:T(8,128)} %get-tuple-element.5.refs_0_), channel_id=1, source_target_pairs={{0,16},{4,20},{8,24},{12,28},{16,0},{20,4},{24,8},{28,12},{1,17},{... | collective-permute-start | bytes 221192 | tf_op jit(solution)/shard_map/ppermute | solution.py:319
  35.8 0.0 collective-permute-start.3
  35.9 0.0 collective-permute-start.6
  35.9 0.2 collective-permute-done.5.refs_3_
  36.0 0.0 copy-start.4
  36.0 0.3 collective-permute-start.9
  36.4 5.1 %collective-permute-done.4.refs_2_ = f32[2,72,128]{2,1,0:T(8,128)S(1)} collective-permute-done((f32[2,72,128]{2,1,0:T(8,128)}, f32[2,72,128]{2,1,0:T(8,128)S(1)}, u32[]{:S(2)}, u32[]{:S(2)}) %collective-permute-start.4) | collective-permute-done | bytes 73760 | tf_op jit(solution)/shard_map/ppermute | solution.py:319
  41.4 0.0 copy-start.5
  41.4 0.0 collective-permute-start.8
  41.4 0.8 %collective-permute-done.3.refs_1_ = f32[2,72,128]{2,1,0:T(8,128)S(1)} collective-permute-done((f32[2,72,128]{2,1,0:T(8,128)}, f32[2,72,128]{2,1,0:T(8,128)S(1)}, u32[]{:S(2)}, u32[]{:S(2)}) %collective-permute-start.3) | collective-permute-done | bytes 73760 | tf_op jit(solution)/shard_map/ppermute | solution.py:319
  42.3 0.0 copy-start.6
  42.3 0.0 collective-permute-start.7
  42.3 0.0 collective-permute-done.6.refs_4_
  42.3 0.0 copy-start.7
  42.3 0.0 collective-permute-done.9.refs_7_
  42.3 0.0 copy-start.8
  42.3 0.4 collective-permute-done.8.refs_6_
  42.7 0.0 copy-start.9
  42.7 0.8 %collective-permute-done.7.refs_5_ = f32[2,72,128]{2,1,0:T(8,128)S(1)} collective-permute-done((f32[2,72,128]{2,1,0:T(8,128)S(1)}, f32[2,72,128]{2,1,0:T(8,128)S(1)}, u32[]{:S(2)}, u32[]{:S(2)}) %collective-permute-start.7) | collective-permute-done | bytes 73760 | tf_op jit(solution)/shard_map/ppermute | solution.py:319
  43.6 0.0 copy-done.4
  43.6 0.0 copy-done.5
  43.6 0.0 copy-done.6
  43.6 0.0 copy-done.7
  43.6 0.0 copy-done.8
  43.6 0.0 copy-done.9
  43.6 0.0 copy-start.10
  43.6 0.6 %copy-done.10 = f32[2,72,128]{2,1,0:T(8,128)} copy-done((f32[2,72,128]{2,1,0:T(8,128)}, f32[2,72,128]{2,1,0:T(8,128)S(1)}, u32[]{:S(2)}) %copy-start.10) | copy-done | bytes 73752
  44.2 2.1 %polar.1 = f32[2,128,128]{2,1,0:T(8,128)} custom-call(f32[2,72,128]{2,1,0:T(8,128)} %get-tuple-element.5.refs_0_, f32[2,72,128]{2,1,0:T(8,128)} %copy-done.6, f32[2,72,128]{2,1,0:T(8,128)} %copy-done.5, f32[2,72,128]{2,1,0:T(8,128)} %copy-done.4, f32[2,72,128]{2,1,0:T(8,128)} %copy-done.7, f32[2,72,128]{2,1,0:T(8,128)} %copy-done.10, ...), custom_call_target="tpu_custom_call" | custom-call | tf_op jit(solution)/shard_map/polar/pallas_call | solution.py:327
  (1 shorter events, 0.0 us)
Async XLA Ops:
  0.6 0.9 %copy-start.11 = (f32[1,128,128]{2,1,0:T(8,128)S(1)}, f32[1,128,128]{2,1,0:T(8,128)}, u32[]{:S(2)}) copy-start(f32[1,128,128]{2,1,0:T(8,128)} %param.4) | copy-start | bytes 196612
  1.5 10.6 %copy-start = (f32[2,128,128]{2,1,0:T(8,128)}, f32[2,128,128]{2,1,0:T(8,128)S(1)}, u32[]{:S(2)}) copy-start(f32[2,128,128]{2,1,0:T(8,128)S(1)} %constant_dynamic-update-slice_fusion.refs_0_) | copy-start | bytes 393220
  1.5 7.9 %collective-permute-start.2 = (f32[2,128,128]{2,1,0:T(8,128)S(1)}, f32[2,128,128]{2,1,0:T(8,128)S(1)}, u32[]{:S(2)}, u32[]{:S(2)}) collective-permute-start(f32[2,128,128]{2,1,0:T(8,128)S(1)} %constant_dynamic-update-slice_fusion.refs_0_), channel_id=1, source_target_pairs={{0,3},{1,2},{2,1},{3,0},{4,7},{5,6},{6,5},{7,4},{8,11},{9,10},{10,... | collective-permute-start | bytes 393224 | tf_op jit(solution)/shard_map/ppermute | solution.py:359
  5.5 6.3 %collective-permute-start.1 = (f32[2,128,128]{2,1,0:T(8,128)S(1)}, f32[2,128,128]{2,1,0:T(8,128)S(1)}, u32[]{:S(2)}, u32[]{:S(2)}) collective-permute-start(f32[2,128,128]{2,1,0:T(8,128)S(1)} %constant_dynamic-update-slice_fusion.refs_0_), channel_id=1, source_target_pairs={{0,2},{1,3},{2,0},{3,1},{4,6},{5,7},{6,4},{7,5},{8,10},{9,11},{10,... | collective-permute-start | bytes 393224 | tf_op jit(solution)/shard_map/ppermute | solution.py:359
  6.0 6.0 %collective-permute-start = (f32[2,128,128]{2,1,0:T(8,128)S(1)}, f32[2,128,128]{2,1,0:T(8,128)S(1)}, u32[]{:S(2)}, u32[]{:S(2)}) collective-permute-start(f32[2,128,128]{2,1,0:T(8,128)S(1)} %constant_dynamic-update-slice_fusion.refs_0_), channel_id=1, source_target_pairs={{0,1},{1,0},{2,3},{3,2},{4,5},{5,4},{6,7},{7,6},{8,9},{9,8},{10,11... | collective-permute-start | bytes 393224 | tf_op jit(solution)/shard_map/ppermute | solution.py:359
  9.4 2.7 %copy-start.1 = (f32[2,128,128]{2,1,0:T(8,128)}, f32[2,128,128]{2,1,0:T(8,128)S(1)}, u32[]{:S(2)}) copy-start(f32[2,128,128]{2,1,0:T(8,128)S(1)} %collective-permute-done.2.refs_3_) | copy-start | bytes 393220
  11.8 0.6 %copy-start.2 = (f32[2,128,128]{2,1,0:T(8,128)}, f32[2,128,128]{2,1,0:T(8,128)S(1)}, u32[]{:S(2)}) copy-start(f32[2,128,128]{2,1,0:T(8,128)S(1)} %collective-permute-done.1.refs_2_) | copy-start | bytes 393220
  12.5 0.6 %copy-start.3 = (f32[2,128,128]{2,1,0:T(8,128)}, f32[2,128,128]{2,1,0:T(8,128)S(1)}, u32[]{:S(2)}) copy-start(f32[2,128,128]{2,1,0:T(8,128)S(1)} %collective-permute-done.refs_1_) | copy-start | bytes 393220
  31.4 4.6 %collective-permute-start.5 = (f32[2,72,128]{2,1,0:T(8,128)}, f32[2,72,128]{2,1,0:T(8,128)S(1)}, u32[]{:S(2)}, u32[]{:S(2)}) collective-permute-start(f32[2,72,128]{2,1,0:T(8,128)} %get-tuple-element.5.refs_0_), channel_id=1, source_target_pairs={{0,8},{4,12},{8,0},{12,4},{16,24},{20,28},{24,16},{28,20},{1,9},{5... | collective-permute-start | bytes 221192 | tf_op jit(solution)/shard_map/ppermute | solution.py:319
  33.2 8.2 %collective-permute-start.4 = (f32[2,72,128]{2,1,0:T(8,128)}, f32[2,72,128]{2,1,0:T(8,128)S(1)}, u32[]{:S(2)}, u32[]{:S(2)}) collective-permute-start(f32[2,72,128]{2,1,0:T(8,128)} %get-tuple-element.5.refs_0_), channel_id=1, source_target_pairs={{0,16},{4,20},{8,24},{12,28},{16,0},{20,4},{24,8},{28,12},{1,17},{... | collective-permute-start | bytes 221192 | tf_op jit(solution)/shard_map/ppermute | solution.py:319
  35.8 6.5 %collective-permute-start.3 = (f32[2,72,128]{2,1,0:T(8,128)}, f32[2,72,128]{2,1,0:T(8,128)S(1)}, u32[]{:S(2)}, u32[]{:S(2)}) collective-permute-start(f32[2,72,128]{2,1,0:T(8,128)} %get-tuple-element.5.refs_0_), channel_id=1, source_target_pairs={{0,24},{4,28},{8,16},{12,20},{16,8},{20,12},{24,0},{28,4},{1,25},{... | collective-permute-start | bytes 221192 | tf_op jit(solution)/shard_map/ppermute | solution.py:319
  35.9 6.4 %collective-permute-start.6 = (f32[2,72,128]{2,1,0:T(8,128)}, f32[2,72,128]{2,1,0:T(8,128)S(1)}, u32[]{:S(2)}, u32[]{:S(2)}) collective-permute-start(f32[2,72,128]{2,1,0:T(8,128)} %get-tuple-element.5.refs_0_), channel_id=1, source_target_pairs={{0,4},{4,0},{8,12},{12,8},{16,20},{20,16},{24,28},{28,24},{1,5},{5... | collective-permute-start | bytes 221192 | tf_op jit(solution)/shard_map/ppermute | solution.py:319
  36.0 7.5 %copy-start.4 = (f32[2,72,128]{2,1,0:T(8,128)}, f32[2,72,128]{2,1,0:T(8,128)S(1)}, u32[]{:S(2)}) copy-start(f32[2,72,128]{2,1,0:T(8,128)S(1)} %collective-permute-done.5.refs_3_) | copy-start | bytes 221188
  36.0 6.3 %collective-permute-start.9 = (f32[2,72,128]{2,1,0:T(8,128)S(1)}, f32[2,72,128]{2,1,0:T(8,128)S(1)}, u32[]{:S(2)}, u32[]{:S(2)}) collective-permute-start(f32[2,72,128]{2,1,0:T(8,128)S(1)} %collective-permute-done.5.refs_3_), channel_id=1, source_target_pairs={{0,4},{4,0},{8,12},{12,8},{16,20},{20,16},{24,28},{28,24},{1,5},{5... | collective-permute-start | bytes 221192 | tf_op jit(solution)/shard_map/ppermute | solution.py:319
  41.4 2.1 %copy-start.5 = (f32[2,72,128]{2,1,0:T(8,128)}, f32[2,72,128]{2,1,0:T(8,128)S(1)}, u32[]{:S(2)}) copy-start(f32[2,72,128]{2,1,0:T(8,128)S(1)} %collective-permute-done.4.refs_2_) | copy-start | bytes 221188
  41.4 1.3 %collective-permute-start.8 = (f32[2,72,128]{2,1,0:T(8,128)S(1)}, f32[2,72,128]{2,1,0:T(8,128)S(1)}, u32[]{:S(2)}, u32[]{:S(2)}) collective-permute-start(f32[2,72,128]{2,1,0:T(8,128)S(1)} %collective-permute-done.4.refs_2_), channel_id=1, source_target_pairs={{0,4},{4,0},{8,12},{12,8},{16,20},{20,16},{24,28},{28,24},{1,5},{5... | collective-permute-start | bytes 221192 | tf_op jit(solution)/shard_map/ppermute | solution.py:319
  42.3 1.3 %copy-start.6 = (f32[2,72,128]{2,1,0:T(8,128)}, f32[2,72,128]{2,1,0:T(8,128)S(1)}, u32[]{:S(2)}) copy-start(f32[2,72,128]{2,1,0:T(8,128)S(1)} %collective-permute-done.3.refs_1_) | copy-start | bytes 221188
  42.3 1.3 %collective-permute-start.7 = (f32[2,72,128]{2,1,0:T(8,128)S(1)}, f32[2,72,128]{2,1,0:T(8,128)S(1)}, u32[]{:S(2)}, u32[]{:S(2)}) collective-permute-start(f32[2,72,128]{2,1,0:T(8,128)S(1)} %collective-permute-done.3.refs_1_), channel_id=1, source_target_pairs={{0,4},{4,0},{8,12},{12,8},{16,20},{20,16},{24,28},{28,24},{1,5},{5... | collective-permute-start | bytes 221192 | tf_op jit(solution)/shard_map/ppermute | solution.py:319
  42.3 1.3 %copy-start.7 = (f32[2,72,128]{2,1,0:T(8,128)}, f32[2,72,128]{2,1,0:T(8,128)S(1)}, u32[]{:S(2)}) copy-start(f32[2,72,128]{2,1,0:T(8,128)S(1)} %collective-permute-done.6.refs_4_) | copy-start | bytes 221188
  42.3 1.3 %copy-start.8 = (f32[2,72,128]{2,1,0:T(8,128)}, f32[2,72,128]{2,1,0:T(8,128)S(1)}, u32[]{:S(2)}) copy-start(f32[2,72,128]{2,1,0:T(8,128)S(1)} %collective-permute-done.9.refs_7_) | copy-start | bytes 221188
  42.7 0.9 %copy-start.9 = (f32[2,72,128]{2,1,0:T(8,128)}, f32[2,72,128]{2,1,0:T(8,128)S(1)}, u32[]{:S(2)}) copy-start(f32[2,72,128]{2,1,0:T(8,128)S(1)} %collective-permute-done.8.refs_6_) | copy-start | bytes 221188
  43.6 0.6 %copy-start.10 = (f32[2,72,128]{2,1,0:T(8,128)}, f32[2,72,128]{2,1,0:T(8,128)S(1)}, u32[]{:S(2)}) copy-start(f32[2,72,128]{2,1,0:T(8,128)S(1)} %collective-permute-done.7.refs_5_) | copy-start | bytes 221188

commit v3 on v2

--- a/solution.py
+++ b/solution.py
@@ -144,28 +144,29 @@
     return jnp.concatenate([wide(real, imag), wide(-imag, real)], 0)
 
 
+def half_masks(rows, size):
+    row = lax.broadcasted_iota(jnp.int32, (rows, size), 0)
+    lane = lax.broadcasted_iota(jnp.int32, (rows, size), 1)
+    past = lax.rem(lane - row + size, size)
+    return past < size // 2, (past == size // 2) & (row < size // 2)
+
+
 def packed_half(value):
     size = value.shape[0]
     half = size // 2
-    row = lax.broadcasted_iota(jnp.int32, (half, size), 0)
-    lane = lax.broadcasted_iota(jnp.int32, (half, size), 1)
-    quarters = jnp.where((lane < half) | (lane - half > row), pltpu.roll(value[:half], half, 1), value[half:])
-    full_row = lax.broadcasted_iota(jnp.int32, (size, size), 0)
-    full_lane = lax.broadcasted_iota(jnp.int32, (size, size), 1)
-    diagonal = jnp.sum(jnp.where(full_row == full_lane, value, 0.0), axis=0, keepdims=True)
-    return jnp.concatenate([quarters, jnp.broadcast_to(diagonal, (TILE, size))], 0)
+    kept, middle = half_masks(half, size)
+    upper = value[:half]
+    extra = jnp.sum(jnp.where(middle, upper, 0.0), axis=0, keepdims=True)
+    return jnp.concatenate([jnp.where(kept, upper, value[half:]), jnp.broadcast_to(extra, (TILE, size))], 0)
 
 
 def unpacked(packed):
     size = packed.shape[1]
     half = size // 2
-    quarters = packed[:half]
-    whole = jnp.concatenate([pltpu.roll(quarters, half, 1), quarters], 0)
-    row = lax.broadcasted_iota(jnp.int32, (size, size), 0)
-    lane = lax.broadcasted_iota(jnp.int32, (size, size), 1)
-    as_is = ((row < half) & (lane > row)) | ((row >= half) & (lane >= half) & (lane < row))
-    full = jnp.where(as_is, whole, whole.T)
-    return jnp.where(row == lane, jnp.broadcast_to(packed[half : half + 1], (size, size)), full)
+    kept, middle = half_masks(size, size)
+    whole = jnp.concatenate([packed[:half], packed[:half]], 0)
+    whole = jnp.where(middle, jnp.broadcast_to(packed[half : half + 1], (size, size)), whole)
+    return jnp.where(kept | middle, whole, whole.T)
 
 
 def exact_dot(left, right, dims):
@@ -201,19 +202,22 @@
     def is_last(step):
         return ((slab + step) & (count - 1)) == count - 1
 
+    def link_of(step):
+        return slab_ref[step, size // 2 + TILE :, :]
+
     def cut_link(step):
-        return slab_ref[step, 1] * jnp.where(is_last(step), 0.0, 1.0)
+        return link_of(step) * jnp.where(is_last(step), 0.0, 1.0)
 
     def place(steps):
         for d in steps:
             copies[d].wait()
         for step in steps:
-            diagonal_ref[step, 0] = energy * identity - slab_ref[step, 0]
+            diagonal_ref[step, 0] = energy * identity - unpacked(slab_ref[step, : size // 2 + TILE, :])
             diagonal_ref[step, 1] = damping * identity
 
             @pl.when(is_last(step))
             def _():
-                link = slab_ref[step, 1]
+                link = link_of(step)
                 diagonal_ref[step, 1] = diagonal_ref[step, 1] + 0.5 * exact_dot(link, link, ((1,), (1,)))
 
     def subtract(node, real, imag):
@@ -276,10 +280,10 @@
             jax.ShapeDtypeStruct((2, size, size), f32),
             jax.ShapeDtypeStruct((2, size // 2 + TILE, size), f32),
         ),
-        in_specs=[scalar] + [pl.BlockSpec(memory_space=pl.ANY)] * count,
+        in_specs=[scalar] + [pl.BlockSpec(memory_space=pltpu.HBM)] * count,
         out_specs=(whole, whole),
         scratch_shapes=[
-            pltpu.VMEM((count, 2, size, size), f32),
+            pltpu.VMEM((count,) + blocks[0].shape, f32),
             pltpu.VMEM((count, 2, size, size), f32),
             pltpu.VMEM((count, 2, size, size), f32),
             pltpu.VMEM((2, 2, size, size), f32),
@@ -327,7 +331,7 @@
     return pl.pallas_call(
         functools.partial(polar_kernel, steps),
         out_shape=jax.ShapeDtypeStruct((2, size, size), f32),
-        in_specs=[pl.BlockSpec(memory_space=pl.ANY)] * groups,
+        in_specs=[pl.BlockSpec(memory_space=pltpu.HBM)] * groups,
         out_specs=whole,
         scratch_shapes=[pltpu.VMEM((groups,) + packed.shape, f32), pltpu.SemaphoreType.DMA((groups,))],
         name="polar",
@@ -353,7 +357,7 @@
     slabs = lax.axis_size("slab")
     groups = lax.axis_size("energy")
     size = h_diag.shape[-1]
-    own = jnp.concatenate([h_diag, coupling], 0)
+    own = jnp.concatenate([packed_half(h_diag[0]), coupling[0]], 0)
     blocks = {0: own}
     for d in list(range(slabs - 1, 0, -2)) + list(range(slabs - 2, 0, -2)):
         blocks[d] = lax.ppermute(own, "slab", [(s, s ^ d) for s in range(slabs)])

time: 46.6 us -> 45.7 us (0.981)
  waiting for transfers between devices: 12.6 us -> 11.4 us
  local copies, waits for them, and re-layouts: 2.58 us -> 1.62 us
  other arithmetic: 0 us -> 0.92 us
    ppermute x3, waiting for transfers between devices: 5.26 us -> 4.06 us  [on_device(): blocks[d] = lax.ppermute(own, 'slab', [(s, s ^ d) for s in range(slabs)])]
    unnamed x25 -> x24, local copies, waits for them, and re-layouts: 2.57 us -> 1.62 us
    select_n x0 -> x1, other arithmetic: none -> 0.9 us  [packed_half(): jnp.where(kept, upper, value[half:])]
  transfers between devices with their start and end apart: 10 -> 10, of which waited for: 8 -> 7; matrix products, arithmetic and copies ran while one was open for 0% -> 0% of each run, Pallas kernels for 0% -> 0%
where the time goes in v3:
time: 45.7 us; the launch traced here: 45.4 us
  Pallas kernels  20.7 us (45%)
  waiting for transfers between devices  11.4 us (25%)
  starting transfers between devices  9.45 us (21%)
  local copies, waits for them, and re-layouts  1.62 us (4%)
  between operations  1.41 us (3%)
  other arithmetic  0.92 us (2%)
    pallas_call x1, Pallas kernels, green_of(): pl.pallas_call(functools.partial(chain_kernel, count, total_energies), ou...  18.6 us
    ppermute x7, waiting for transfers between devices, swapped(): return lax.ppermute(block, 'energy', [(s, s ^ step) for s in range(groups)])  7.32 us
    ppermute x7, starting transfers between devices, swapped(): return lax.ppermute(block, 'energy', [(s, s ^ step) for s in range(groups)])  4.82 us
    ppermute x3, starting transfers between devices, on_device(): blocks[d] = lax.ppermute(own, 'slab', [(s, s ^ d) for s in range(slabs)])  4.63 us
    ppermute x3, waiting for transfers between devices, on_device(): blocks[d] = lax.ppermute(own, 'slab', [(s, s ^ d) for s in range(slabs)])  4.06 us
    pallas_call x1, Pallas kernels, correlate(): pl.pallas_call(functools.partial(polar_kernel, steps), out_shape=jax.Shap...  2.06 us
    unnamed x24, local copies, waits for them, and re-layouts  1.62 us
  transfers between devices with their start and end apart: 10, of which 7 were waited for; matrix products, arithmetic and copies ran while one was open for 0% of the time, Pallas kernels for 0%

profile of v3, /device:TPU:0, one launch (start us, length us, event | category | flops | bytes accessed | tf_op | source)
XLA Modules:
  0.0 45.4 jit_solution(727199519390878962)
XLA Ops:
  0.6 0.0 copy-start.11
  0.7 0.9 %bitcast_select_fusion = (f32[64,128]{1,0:T(8,128)S(1)}, f32[128]{0:T(128)S(1)}) fusion(f32[1,128,128]{2,1,0:T(8,128)} %param.3, pred[64]{0:T(512)(128)(4,1)S(1)} %iota_compare_fusion), kind=kLoop, calls=%fused_computation.4 | loop fusion | flops 114560 | bytes 98880 | tf_op jit(solution)/shard_map/jit(_where)/select_n | solution.py:160
  1.6 0.0 copy-done.11
  1.6 0.0 copy-start
  1.6 4.0 %collective-permute-start.2 = (f32[200,128]{1,0:T(8,128)S(1)}, f32[200,128]{1,0:T(8,128)S(1)}, u32[]{:S(2)}, u32[]{:S(2)}) collective-permute-start(f32[200,128]{1,0:T(8,128)S(1)} %pad_maximum_fusion.refs_0_), channel_id=1, source_target_pairs={{0,3},{1,2},{2,1},{3,0},{4,7},{5,6},{6,5},{7,4},{8,11},{9,10},{10,... | collective-permute-start | bytes 307208 | tf_op jit(solution)/shard_map/ppermute | solution.py:363
  5.6 0.5 %collective-permute-start.1 = (f32[200,128]{1,0:T(8,128)S(1)}, f32[200,128]{1,0:T(8,128)S(1)}, u32[]{:S(2)}, u32[]{:S(2)}) collective-permute-start(f32[200,128]{1,0:T(8,128)S(1)} %pad_maximum_fusion.refs_0_), channel_id=1, source_target_pairs={{0,2},{1,3},{2,0},{3,1},{4,6},{5,7},{6,4},{7,5},{8,10},{9,11},{10,... | collective-permute-start | bytes 307208 | tf_op jit(solution)/shard_map/ppermute | solution.py:363
  6.1 0.1 collective-permute-start
  6.9 2.0 %collective-permute-done.2.refs_3_ = f32[200,128]{1,0:T(8,128)S(1)} collective-permute-done((f32[200,128]{1,0:T(8,128)S(1)}, f32[200,128]{1,0:T(8,128)S(1)}, u32[]{:S(2)}, u32[]{:S(2)}) %collective-permute-start.2) | collective-permute-done | bytes 102432 | tf_op jit(solution)/shard_map/ppermute | solution.py:363
  8.9 0.0 copy-start.1
  8.9 1.8 %collective-permute-done.1.refs_2_ = f32[200,128]{1,0:T(8,128)S(1)} collective-permute-done((f32[200,128]{1,0:T(8,128)S(1)}, f32[200,128]{1,0:T(8,128)S(1)}, u32[]{:S(2)}, u32[]{:S(2)}) %collective-permute-start.1) | collective-permute-done | bytes 102432 | tf_op jit(solution)/shard_map/ppermute | solution.py:363
  10.7 0.0 copy-start.2
  10.7 0.3 collective-permute-done.refs_1_
  10.9 0.0 copy-done
  11.0 0.0 copy-done.1
  11.0 0.3 copy-done.2
  11.3 0.0 copy-start.3
  11.3 0.6 %copy-done.3 = f32[200,128]{1,0:T(8,128)} copy-done((f32[200,128]{1,0:T(8,128)}, f32[200,128]{1,0:T(8,128)S(1)}, u32[]{:S(2)}) %copy-start.3) | copy-done | bytes 102424
  11.9 18.6 %chain.1 = (f32[2,128,128]{2,1,0:T(8,128)}, f32[2,72,128]{2,1,0:T(8,128)}) custom-call(f32[1]{0:T(128)S(6)} %copy.5.damping_ref, f32[200,128]{1,0:T(8,128)} %copy-done, f32[200,128]{1,0:T(8,128)} %copy-done.3, f32[200,128]{1,0:T(8,128)} %copy-done.2, f32[200,128]{1,0:T(8,128)} %copy-done.1), custom_call_target="tpu_custom_call" | custom-call | tf_op jit(solution)/shard_map/chain/pallas_call | solution.py:277
  30.5 1.9 %collective-permute-start.5 = (f32[2,72,128]{2,1,0:T(8,128)}, f32[2,72,128]{2,1,0:T(8,128)S(1)}, u32[]{:S(2)}, u32[]{:S(2)}) collective-permute-start(f32[2,72,128]{2,1,0:T(8,128)} %get-tuple-element.5.refs_0_), channel_id=1, source_target_pairs={{0,8},{4,12},{8,0},{12,4},{16,24},{20,28},{24,16},{28,20},{1,9},{5... | collective-permute-start | bytes 221192 | tf_op jit(solution)/shard_map/ppermute | solution.py:323
  32.4 2.6 %collective-permute-start.4 = (f32[2,72,128]{2,1,0:T(8,128)}, f32[2,72,128]{2,1,0:T(8,128)S(1)}, u32[]{:S(2)}, u32[]{:S(2)}) collective-permute-start(f32[2,72,128]{2,1,0:T(8,128)} %get-tuple-element.5.refs_0_), channel_id=1, source_target_pairs={{0,16},{4,20},{8,24},{12,28},{16,0},{20,4},{24,8},{28,12},{1,17},{... | collective-permute-start | bytes 221192 | tf_op jit(solution)/shard_map/ppermute | solution.py:323
  35.0 0.0 collective-permute-start.3
  35.0 0.0 collective-permute-start.6
  35.0 0.2 collective-permute-done.5.refs_3_
  35.2 0.0 copy-start.4
  35.2 0.3 collective-permute-start.9
  35.5 4.7 %collective-permute-done.4.refs_2_ = f32[2,72,128]{2,1,0:T(8,128)S(1)} collective-permute-done((f32[2,72,128]{2,1,0:T(8,128)}, f32[2,72,128]{2,1,0:T(8,128)S(1)}, u32[]{:S(2)}, u32[]{:S(2)}) %collective-permute-start.4) | collective-permute-done | bytes 73760 | tf_op jit(solution)/shard_map/ppermute | solution.py:323
  40.2 0.0 copy-start.5
  40.2 0.0 collective-permute-start.8
  40.2 1.2 %collective-permute-done.3.refs_1_ = f32[2,72,128]{2,1,0:T(8,128)S(1)} collective-permute-done((f32[2,72,128]{2,1,0:T(8,128)}, f32[2,72,128]{2,1,0:T(8,128)S(1)}, u32[]{:S(2)}, u32[]{:S(2)}) %collective-permute-start.3) | collective-permute-done | bytes 73760 | tf_op jit(solution)/shard_map/ppermute | solution.py:323
  41.5 0.0 copy-start.6
  41.5 0.0 collective-permute-start.7
  41.5 0.0 collective-permute-done.6.refs_4_
  41.5 0.0 copy-start.7
  41.5 0.0 collective-permute-done.9.refs_7_
  41.5 0.0 copy-start.8
  41.5 0.0 collective-permute-done.8.refs_6_
  41.5 0.0 copy-start.9
  41.5 1.2 %collective-permute-done.7.refs_5_ = f32[2,72,128]{2,1,0:T(8,128)S(1)} collective-permute-done((f32[2,72,128]{2,1,0:T(8,128)S(1)}, f32[2,72,128]{2,1,0:T(8,128)S(1)}, u32[]{:S(2)}, u32[]{:S(2)}) %collective-permute-start.7) | collective-permute-done | bytes 73760 | tf_op jit(solution)/shard_map/ppermute | solution.py:323
  42.7 0.0 copy-done.4
  42.7 0.0 copy-done.5
  42.7 0.0 copy-done.6
  42.7 0.0 copy-done.7
  42.7 0.0 copy-done.8
  42.8 0.0 copy-done.9
  42.8 0.0 copy-start.10
  42.8 0.6 %copy-done.10 = f32[2,72,128]{2,1,0:T(8,128)} copy-done((f32[2,72,128]{2,1,0:T(8,128)}, f32[2,72,128]{2,1,0:T(8,128)S(1)}, u32[]{:S(2)}) %copy-start.10) | copy-done | bytes 73752
  43.4 2.1 %polar.1 = f32[2,128,128]{2,1,0:T(8,128)} custom-call(f32[2,72,128]{2,1,0:T(8,128)} %get-tuple-element.5.refs_0_, f32[2,72,128]{2,1,0:T(8,128)} %copy-done.6, f32[2,72,128]{2,1,0:T(8,128)} %copy-done.5, f32[2,72,128]{2,1,0:T(8,128)} %copy-done.4, f32[2,72,128]{2,1,0:T(8,128)} %copy-done.7, f32[2,72,128]{2,1,0:T(8,128)} %copy-done.10, ...), custom_call_target="tpu_custom_call" | custom-call | tf_op jit(solution)/shard_map/polar/pallas_call | solution.py:331
  (3 shorter events, 0.0 us)
Async XLA Ops:
  0.6 0.9 %copy-start.11 = (f32[1,128,128]{2,1,0:T(8,128)S(1)}, f32[1,128,128]{2,1,0:T(8,128)}, u32[]{:S(2)}) copy-start(f32[1,128,128]{2,1,0:T(8,128)} %param.4) | copy-start | bytes 196612
  1.6 9.4 %copy-start = (f32[200,128]{1,0:T(8,128)}, f32[200,128]{1,0:T(8,128)S(1)}, u32[]{:S(2)}) copy-start(f32[200,128]{1,0:T(8,128)S(1)} %pad_maximum_fusion.refs_0_) | copy-start | bytes 307204
  1.6 7.3 %collective-permute-start.2 = (f32[200,128]{1,0:T(8,128)S(1)}, f32[200,128]{1,0:T(8,128)S(1)}, u32[]{:S(2)}, u32[]{:S(2)}) collective-permute-start(f32[200,128]{1,0:T(8,128)S(1)} %pad_maximum_fusion.refs_0_), channel_id=1, source_target_pairs={{0,3},{1,2},{2,1},{3,0},{4,7},{5,6},{6,5},{7,4},{8,11},{9,10},{10,... | collective-permute-start | bytes 307208 | tf_op jit(solution)/shard_map/ppermute | solution.py:363
  5.6 5.1 %collective-permute-start.1 = (f32[200,128]{1,0:T(8,128)S(1)}, f32[200,128]{1,0:T(8,128)S(1)}, u32[]{:S(2)}, u32[]{:S(2)}) collective-permute-start(f32[200,128]{1,0:T(8,128)S(1)} %pad_maximum_fusion.refs_0_), channel_id=1, source_target_pairs={{0,2},{1,3},{2,0},{3,1},{4,6},{5,7},{6,4},{7,5},{8,10},{9,11},{10,... | collective-permute-start | bytes 307208 | tf_op jit(solution)/shard_map/ppermute | solution.py:363
  6.1 4.9 %collective-permute-start = (f32[200,128]{1,0:T(8,128)S(1)}, f32[200,128]{1,0:T(8,128)S(1)}, u32[]{:S(2)}, u32[]{:S(2)}) collective-permute-start(f32[200,128]{1,0:T(8,128)S(1)} %pad_maximum_fusion.refs_0_), channel_id=1, source_target_pairs={{0,1},{1,0},{2,3},{3,2},{4,5},{5,4},{6,7},{7,6},{8,9},{9,8},{10,11... | collective-permute-start | bytes 307208 | tf_op jit(solution)/shard_map/ppermute | solution.py:363
  8.9 2.1 %copy-start.1 = (f32[200,128]{1,0:T(8,128)}, f32[200,128]{1,0:T(8,128)S(1)}, u32[]{:S(2)}) copy-start(f32[200,128]{1,0:T(8,128)S(1)} %collective-permute-done.2.refs_3_) | copy-start | bytes 307204
  10.7 0.6 %copy-start.2 = (f32[200,128]{1,0:T(8,128)}, f32[200,128]{1,0:T(8,128)S(1)}, u32[]{:S(2)}) copy-start(f32[200,128]{1,0:T(8,128)S(1)} %collective-permute-done.1.refs_2_) | copy-start | bytes 307204
  11.3 0.6 %copy-start.3 = (f32[200,128]{1,0:T(8,128)}, f32[200,128]{1,0:T(8,128)S(1)}, u32[]{:S(2)}) copy-start(f32[200,128]{1,0:T(8,128)S(1)} %collective-permute-done.refs_1_) | copy-start | bytes 307204
  30.5 4.6 %collective-permute-start.5 = (f32[2,72,128]{2,1,0:T(8,128)}, f32[2,72,128]{2,1,0:T(8,128)S(1)}, u32[]{:S(2)}, u32[]{:S(2)}) collective-permute-start(f32[2,72,128]{2,1,0:T(8,128)} %get-tuple-element.5.refs_0_), channel_id=1, source_target_pairs={{0,8},{4,12},{8,0},{12,4},{16,24},{20,28},{24,16},{28,20},{1,9},{5... | collective-permute-start | bytes 221192 | tf_op jit(solution)/shard_map/ppermute | solution.py:323
  32.4 7.8 %collective-permute-start.4 = (f32[2,72,128]{2,1,0:T(8,128)}, f32[2,72,128]{2,1,0:T(8,128)S(1)}, u32[]{:S(2)}, u32[]{:S(2)}) collective-permute-start(f32[2,72,128]{2,1,0:T(8,128)} %get-tuple-element.5.refs_0_), channel_id=1, source_target_pairs={{0,16},{4,20},{8,24},{12,28},{16,0},{20,4},{24,8},{28,12},{1,17},{... | collective-permute-start | bytes 221192 | tf_op jit(solution)/shard_map/ppermute | solution.py:323
  35.0 6.5 %collective-permute-start.3 = (f32[2,72,128]{2,1,0:T(8,128)}, f32[2,72,128]{2,1,0:T(8,128)S(1)}, u32[]{:S(2)}, u32[]{:S(2)}) collective-permute-start(f32[2,72,128]{2,1,0:T(8,128)} %get-tuple-element.5.refs_0_), channel_id=1, source_target_pairs={{0,24},{4,28},{8,16},{12,20},{16,8},{20,12},{24,0},{28,4},{1,25},{... | collective-permute-start | bytes 221192 | tf_op jit(solution)/shard_map/ppermute | solution.py:323
  35.0 6.5 %collective-permute-start.6 = (f32[2,72,128]{2,1,0:T(8,128)}, f32[2,72,128]{2,1,0:T(8,128)S(1)}, u32[]{:S(2)}, u32[]{:S(2)}) collective-permute-start(f32[2,72,128]{2,1,0:T(8,128)} %get-tuple-element.5.refs_0_), channel_id=1, source_target_pairs={{0,4},{4,0},{8,12},{12,8},{16,20},{20,16},{24,28},{28,24},{1,5},{5... | collective-permute-start | bytes 221192 | tf_op jit(solution)/shard_map/ppermute | solution.py:323
  35.2 7.6 %copy-start.4 = (f32[2,72,128]{2,1,0:T(8,128)}, f32[2,72,128]{2,1,0:T(8,128)S(1)}, u32[]{:S(2)}) copy-start(f32[2,72,128]{2,1,0:T(8,128)S(1)} %collective-permute-done.5.refs_3_) | copy-start | bytes 221188
  35.2 6.3 %collective-permute-start.9 = (f32[2,72,128]{2,1,0:T(8,128)S(1)}, f32[2,72,128]{2,1,0:T(8,128)S(1)}, u32[]{:S(2)}, u32[]{:S(2)}) collective-permute-start(f32[2,72,128]{2,1,0:T(8,128)S(1)} %collective-permute-done.5.refs_3_), channel_id=1, source_target_pairs={{0,4},{4,0},{8,12},{12,8},{16,20},{20,16},{24,28},{28,24},{1,5},{5... | collective-permute-start | bytes 221192 | tf_op jit(solution)/shard_map/ppermute | solution.py:323
  40.2 2.5 %copy-start.5 = (f32[2,72,128]{2,1,0:T(8,128)}, f32[2,72,128]{2,1,0:T(8,128)S(1)}, u32[]{:S(2)}) copy-start(f32[2,72,128]{2,1,0:T(8,128)S(1)} %collective-permute-done.4.refs_2_) | copy-start | bytes 221188
  40.2 1.3 %collective-permute-start.8 = (f32[2,72,128]{2,1,0:T(8,128)S(1)}, f32[2,72,128]{2,1,0:T(8,128)S(1)}, u32[]{:S(2)}, u32[]{:S(2)}) collective-permute-start(f32[2,72,128]{2,1,0:T(8,128)S(1)} %collective-permute-done.4.refs_2_), channel_id=1, source_target_pairs={{0,4},{4,0},{8,12},{12,8},{16,20},{20,16},{24,28},{28,24},{1,5},{5... | collective-permute-start | bytes 221192 | tf_op jit(solution)/shard_map/ppermute | solution.py:323
  41.5 1.3 %copy-start.6 = (f32[2,72,128]{2,1,0:T(8,128)}, f32[2,72,128]{2,1,0:T(8,128)S(1)}, u32[]{:S(2)}) copy-start(f32[2,72,128]{2,1,0:T(8,128)S(1)} %collective-permute-done.3.refs_1_) | copy-start | bytes 221188
  41.5 1.3 %collective-permute-start.7 = (f32[2,72,128]{2,1,0:T(8,128)S(1)}, f32[2,72,128]{2,1,0:T(8,128)S(1)}, u32[]{:S(2)}, u32[]{:S(2)}) collective-permute-start(f32[2,72,128]{2,1,0:T(8,128)S(1)} %collective-permute-done.3.refs_1_), channel_id=1, source_target_pairs={{0,4},{4,0},{8,12},{12,8},{16,20},{20,16},{24,28},{28,24},{1,5},{5... | collective-permute-start | bytes 221192 | tf_op jit(solution)/shard_map/ppermute | solution.py:323
  41.5 1.3 %copy-start.7 = (f32[2,72,128]{2,1,0:T(8,128)}, f32[2,72,128]{2,1,0:T(8,128)S(1)}, u32[]{:S(2)}) copy-start(f32[2,72,128]{2,1,0:T(8,128)S(1)} %collective-permute-done.6.refs_4_) | copy-start | bytes 221188
  41.5 1.3 %copy-start.8 = (f32[2,72,128]{2,1,0:T(8,128)}, f32[2,72,128]{2,1,0:T(8,128)S(1)}, u32[]{:S(2)}) copy-start(f32[2,72,128]{2,1,0:T(8,128)S(1)} %collective-permute-done.9.refs_7_) | copy-start | bytes 221188
  41.5 1.2 %copy-start.9 = (f32[2,72,128]{2,1,0:T(8,128)}, f32[2,72,128]{2,1,0:T(8,128)S(1)}, u32[]{:S(2)}) copy-start(f32[2,72,128]{2,1,0:T(8,128)S(1)} %collective-permute-done.8.refs_6_) | copy-start | bytes 221188
  42.8 0.6 %copy-start.10 = (f32[2,72,128]{2,1,0:T(8,128)}, f32[2,72,128]{2,1,0:T(8,128)S(1)}, u32[]{:S(2)}) copy-start(f32[2,72,128]{2,1,0:T(8,128)S(1)} %collective-permute-done.7.refs_5_) | copy-start | bytes 221188

commit v4 on v3

--- a/solution.py
+++ b/solution.py
@@ -11,6 +11,7 @@
 bf16 = jnp.bfloat16
 PANEL = 16
 TILE = 8
+GRANT = 24 << 20
 
 
 def three_parts(value):
@@ -280,7 +281,7 @@
             jax.ShapeDtypeStruct((2, size, size), f32),
             jax.ShapeDtypeStruct((2, size // 2 + TILE, size), f32),
         ),
-        in_specs=[scalar] + [pl.BlockSpec(memory_space=pltpu.HBM)] * count,
+        in_specs=[scalar] + [pl.BlockSpec(memory_space=pl.ANY)] * count,
         out_specs=(whole, whole),
         scratch_shapes=[
             pltpu.VMEM((count,) + blocks[0].shape, f32),
@@ -289,13 +290,14 @@
             pltpu.VMEM((2, 2, size, size), f32),
             pltpu.SemaphoreType.DMA((count,)),
         ],
+        compiler_params=pltpu.CompilerParams(vmem_limit_bytes=GRANT),
         name="chain",
     )(damping, *blocks)
 
 
-def polar_kernel(steps, *refs):
+def polar_kernel(steps, green_ref, *refs):
     groups = len(steps)
-    blocks, (out_ref, held, arrived) = refs[:groups], refs[groups:]
+    blocks, (green_out_ref, out_ref, held, result, arrived, left) = refs[:groups], refs[groups:]
     me = lax.axis_index("energy")
     copies = [
         pltpu.make_async_copy(block, held.at[me ^ step], arrived.at[i])
@@ -303,6 +305,8 @@
     ]
     for copy in copies:
         copy.start()
+    leaving = [pltpu.make_async_copy(green_ref, green_out_ref, left.at[2])]
+    leaving[0].start()
     for copy in copies:
         copy.wait()
     real = imag = jnp.zeros(held.shape[2:], f32)
@@ -314,11 +318,15 @@
         ar, ai = held[second, 0], held[second, 1]
         real = real + (ar * br + ai * bi)
         imag = imag + (ai * br - ar * bi)
-    out_ref[0] = unpacked(real)
-    out_ref[1] = unpacked(imag)
-
-
-def correlate(packed, groups):
+    for part, value in enumerate((real, imag)):
+        result[part] = unpacked(value)
+        leaving.append(pltpu.make_async_copy(result.at[part], out_ref.at[part], left.at[part]))
+        leaving[-1].start()
+    for copy in leaving:
+        copy.wait()
+
+
+def correlate(green, packed, groups):
     def swapped(block, step):
         return lax.ppermute(block, "energy", [(s, s ^ step) for s in range(groups)])
 
@@ -326,16 +334,22 @@
     gathered.insert(0, (0, packed))
     gathered = gathered + [(step ^ 1, swapped(block, 1)) for step, block in gathered]
     steps, blocks = zip(*gathered)
-    size = packed.shape[-1]
-    whole = pl.BlockSpec(memory_space=pltpu.VMEM)
+    anywhere = pl.BlockSpec(memory_space=pl.ANY)
+    result = jax.ShapeDtypeStruct(green.shape, f32)
     return pl.pallas_call(
         functools.partial(polar_kernel, steps),
-        out_shape=jax.ShapeDtypeStruct((2, size, size), f32),
-        in_specs=[pl.BlockSpec(memory_space=pltpu.HBM)] * groups,
-        out_specs=whole,
-        scratch_shapes=[pltpu.VMEM((groups,) + packed.shape, f32), pltpu.SemaphoreType.DMA((groups,))],
+        out_shape=(result, result),
+        in_specs=[anywhere] * (1 + groups),
+        out_specs=(anywhere, anywhere),
+        scratch_shapes=[
+            pltpu.VMEM((groups,) + packed.shape, f32),
+            pltpu.VMEM(green.shape, f32),
+            pltpu.SemaphoreType.DMA((groups,)),
+            pltpu.SemaphoreType.DMA((3,)),
+        ],
+        compiler_params=pltpu.CompilerParams(vmem_limit_bytes=GRANT),
         name="polar",
-    )(*blocks)
+    )(green, *blocks)
 
 
 def correlate_spread(own, groups):
@@ -363,7 +377,10 @@
         blocks[d] = lax.ppermute(own, "slab", [(s, s ^ d) for s in range(slabs)])
     blocks = [blocks[d] for d in range(slabs)]
     green, packed = green_of(blocks, broadening, groups)
-    polar = correlate(packed, groups) if groups <= 8 else correlate_spread(green, groups)
+    if groups <= 8:
+        green, polar = correlate(green, packed, groups)
+    else:
+        polar = correlate_spread(green, groups)
     shape = (1, 1, 2, size, size)
     return green.reshape(shape), polar.reshape(shape)
 

time: 45.7 us -> 42 us (0.919)
  local copies, waits for them, and re-layouts: 1.62 us -> 0.01 us
  Pallas kernels: 20.7 us -> 19.2 us
  waiting for transfers between devices: 11.4 us -> 10.8 us
    unnamed x24 -> x2, local copies, waits for them, and re-layouts: 1.62 us -> 0.01 us
    pallas_call x1, Pallas kernels: 18.6 us -> 17.5 us  [green_of(): pl.pallas_call(functools.partial(chain_kernel, count, total_energies), ou...]
    ppermute x7, waiting for transfers between devices: 7.32 us -> 6.77 us  [swapped(): return lax.ppermute(block, 'energy', [(s, s ^ step) for s in range(groups)])]
  transfers between devices with their start and end apart: 10 -> 10, of which waited for: 7 -> 6; matrix products, arithmetic and copies ran while one was open for 0% -> 0% of each run, Pallas kernels for 0% -> 0%
where the time goes in v4:
time: 42 us; the launch traced here: 41.9 us
  Pallas kernels  19.2 us (46%)
  waiting for transfers between devices  10.8 us (26%)
  starting transfers between devices  9.6 us (23%)
  between operations  1.34 us (3%)
  other arithmetic  0.92 us (2%)
    pallas_call x1, Pallas kernels, green_of(): pl.pallas_call(functools.partial(chain_kernel, count, total_energies), ou...  17.5 us
    ppermute x7, waiting for transfers between devices, swapped(): return lax.ppermute(block, 'energy', [(s, s ^ step) for s in range(groups)])  6.77 us
    ppermute x7, starting transfers between devices, swapped(): return lax.ppermute(block, 'energy', [(s, s ^ step) for s in range(groups)])  4.97 us
    ppermute x3, starting transfers between devices, on_device(): blocks[d] = lax.ppermute(own, 'slab', [(s, s ^ d) for s in range(slabs)])  4.63 us
    ppermute x3, waiting for transfers between devices, on_device(): blocks[d] = lax.ppermute(own, 'slab', [(s, s ^ d) for s in range(slabs)])  4.07 us
    pallas_call x1, Pallas kernels, correlate(): pl.pallas_call(functools.partial(polar_kernel, steps), out_shape=(result,...  1.69 us
    select_n x1, other arithmetic, packed_half(): jnp.where(kept, upper, value[half:])  0.9 us
  transfers between devices with their start and end apart: 10, of which 6 were waited for; matrix products, arithmetic and copies ran while one was open for 0% of the time, Pallas kernels for 0%

profile of v4, /device:TPU:0, one launch (start us, length us, event | category | flops | bytes accessed | tf_op | source)
XLA Modules:
  0.0 41.9 jit_solution(10783357947952965223)
XLA Ops:
  0.6 0.0 copy-start
  0.7 0.9 %bitcast_select_fusion = (f32[64,128]{1,0:T(8,128)S(1)}, f32[128]{0:T(128)S(1)}) fusion(f32[1,128,128]{2,1,0:T(8,128)} %param.3, pred[64]{0:T(512)(128)(4,1)S(1)} %iota_compare_fusion), kind=kLoop, calls=%fused_computation.4 | loop fusion | flops 114560 | bytes 98880 | tf_op jit(solution)/shard_map/jit(_where)/select_n | solution.py:161
  1.6 0.0 copy-done
  1.6 4.0 %collective-permute-start.2 = (f32[200,128]{1,0:T(8,128)S(1)}, f32[200,128]{1,0:T(8,128)S(1)}, u32[]{:S(2)}, u32[]{:S(2)}) collective-permute-start(f32[200,128]{1,0:T(8,128)S(1)} %pad_maximum_fusion.refs_0_), channel_id=1, source_target_pairs={{0,3},{1,2},{2,1},{3,0},{4,7},{5,6},{6,5},{7,4},{8,11},{9,10},{10,... | collective-permute-start | bytes 307208 | tf_op jit(solution)/shard_map/ppermute | solution.py:377
  5.6 0.5 %collective-permute-start.1 = (f32[200,128]{1,0:T(8,128)S(1)}, f32[200,128]{1,0:T(8,128)S(1)}, u32[]{:S(2)}, u32[]{:S(2)}) collective-permute-start(f32[200,128]{1,0:T(8,128)S(1)} %pad_maximum_fusion.refs_0_), channel_id=1, source_target_pairs={{0,2},{1,3},{2,0},{3,1},{4,6},{5,7},{6,4},{7,5},{8,10},{9,11},{10,... | collective-permute-start | bytes 307208 | tf_op jit(solution)/shard_map/ppermute | solution.py:377
  6.1 0.1 collective-permute-start
  6.9 2.0 %collective-permute-done.2.refs_3_ = f32[200,128]{1,0:T(8,128)S(1)} collective-permute-done((f32[200,128]{1,0:T(8,128)S(1)}, f32[200,128]{1,0:T(8,128)S(1)}, u32[]{:S(2)}, u32[]{:S(2)}) %collective-permute-start.2) | collective-permute-done | bytes 102432 | tf_op jit(solution)/shard_map/ppermute | solution.py:377
  8.8 1.8 %collective-permute-done.1.refs_2_ = f32[200,128]{1,0:T(8,128)S(1)} collective-permute-done((f32[200,128]{1,0:T(8,128)S(1)}, f32[200,128]{1,0:T(8,128)S(1)}, u32[]{:S(2)}, u32[]{:S(2)}) %collective-permute-start.1) | collective-permute-done | bytes 102432 | tf_op jit(solution)/shard_map/ppermute | solution.py:377
  10.6 0.3 collective-permute-done.refs_1_
  10.9 17.5 %chain.1 = (f32[2,128,128]{2,1,0:T(8,128)S(1)}, f32[2,72,128]{2,1,0:T(8,128)S(1)}) custom-call(f32[1]{0:T(128)S(6)} %copy.5.damping_ref, f32[200,128]{1,0:T(8,128)S(1)} %pad_maximum_fusion.refs_0_, f32[200,128]{1,0:T(8,128)S(1)} %collective-permute-done.refs_1_, f32[200,128]{1,0:T(8,128)S(1)} %collective-permute-done.1.refs_2_, ...), custom_call_target="tpu_custom_call" | custom-call | tf_op jit(solution)/shard_map/chain/pallas_call | solution.py:278
  28.4 1.6 %collective-permute-start.5 = (f32[2,72,128]{2,1,0:T(8,128)S(1)}, f32[2,72,128]{2,1,0:T(8,128)S(1)}, u32[]{:S(2)}, u32[]{:S(2)}) collective-permute-start(f32[2,72,128]{2,1,0:T(8,128)S(1)} %get-tuple-element.7.refs_0_), channel_id=1, source_target_pairs={{0,8},{4,12},{8,0},{12,4},{16,24},{20,28},{24,16},{28,20},{1,9},{5... | collective-permute-start | bytes 221192 | tf_op jit(solution)/shard_map/ppermute | solution.py:331
  30.1 2.6 %collective-permute-start.4 = (f32[2,72,128]{2,1,0:T(8,128)S(1)}, f32[2,72,128]{2,1,0:T(8,128)S(1)}, u32[]{:S(2)}, u32[]{:S(2)}) collective-permute-start(f32[2,72,128]{2,1,0:T(8,128)S(1)} %get-tuple-element.7.refs_0_), channel_id=1, source_target_pairs={{0,16},{4,20},{8,24},{12,28},{16,0},{20,4},{24,8},{28,12},{1,17},{... | collective-permute-start | bytes 221192 | tf_op jit(solution)/shard_map/ppermute | solution.py:331
  32.7 0.2 collective-permute-start.3
  32.9 0.0 collective-permute-start.6
  32.9 0.0 collective-permute-done.5.refs_3_
  32.9 0.5 %collective-permute-start.9 = (f32[2,72,128]{2,1,0:T(8,128)S(1)}, f32[2,72,128]{2,1,0:T(8,128)S(1)}, u32[]{:S(2)}, u32[]{:S(2)}) collective-permute-start(f32[2,72,128]{2,1,0:T(8,128)S(1)} %collective-permute-done.5.refs_3_), channel_id=1, source_target_pairs={{0,4},{4,0},{8,12},{12,8},{16,20},{20,16},{24,28},{28,24},{1,5},{5... | collective-permute-start | bytes 221192 | tf_op jit(solution)/shard_map/ppermute | solution.py:331
  33.4 4.2 %collective-permute-done.4.refs_2_ = f32[2,72,128]{2,1,0:T(8,128)S(1)} collective-permute-done((f32[2,72,128]{2,1,0:T(8,128)S(1)}, f32[2,72,128]{2,1,0:T(8,128)S(1)}, u32[]{:S(2)}, u32[]{:S(2)}) %collective-permute-start.4) | collective-permute-done | bytes 73760 | tf_op jit(solution)/shard_map/ppermute | solution.py:331
  37.6 0.0 collective-permute-start.8
  37.6 1.3 %collective-permute-done.3.refs_1_ = f32[2,72,128]{2,1,0:T(8,128)S(1)} collective-permute-done((f32[2,72,128]{2,1,0:T(8,128)S(1)}, f32[2,72,128]{2,1,0:T(8,128)S(1)}, u32[]{:S(2)}, u32[]{:S(2)}) %collective-permute-start.3) | collective-permute-done | bytes 73760 | tf_op jit(solution)/shard_map/ppermute | solution.py:331
  38.9 0.0 collective-permute-start.7
  38.9 0.0 collective-permute-done.6.refs_4_
  38.9 0.0 collective-permute-done.9.refs_7_
  38.9 0.0 collective-permute-done.8.refs_6_
  38.9 1.2 %collective-permute-done.7.refs_5_ = f32[2,72,128]{2,1,0:T(8,128)S(1)} collective-permute-done((f32[2,72,128]{2,1,0:T(8,128)S(1)}, f32[2,72,128]{2,1,0:T(8,128)S(1)}, u32[]{:S(2)}, u32[]{:S(2)}) %collective-permute-start.7) | collective-permute-done | bytes 73760 | tf_op jit(solution)/shard_map/ppermute | solution.py:331
  40.2 1.7 %polar.1 = (f32[2,128,128]{2,1,0:T(8,128)}, f32[2,128,128]{2,1,0:T(8,128)}) custom-call(f32[2,128,128]{2,1,0:T(8,128)S(1)} %get-tuple-element.6.green_ref, f32[2,72,128]{2,1,0:T(8,128)S(1)} %get-tuple-element.7.refs_0_, f32[2,72,128]{2,1,0:T(8,128)S(1)} %collective-permute-done.3.refs_1_, f32[2,72,128]{2,1,0:T(8,128)S(1)} %collective-permute-done.4.refs_2_, ...), custom_call_target="tpu_custom_call" | custom-call | tf_op jit(solution)/shard_map/polar/pallas_call | solution.py:339
  (3 shorter events, 0.0 us)
Async XLA Ops:
  0.6 0.9 %copy-start = (f32[1,128,128]{2,1,0:T(8,128)S(1)}, f32[1,128,128]{2,1,0:T(8,128)}, u32[]{:S(2)}) copy-start(f32[1,128,128]{2,1,0:T(8,128)} %param.4) | copy-start | bytes 196612
  1.6 7.3 %collective-permute-start.2 = (f32[200,128]{1,0:T(8,128)S(1)}, f32[200,128]{1,0:T(8,128)S(1)}, u32[]{:S(2)}, u32[]{:S(2)}) collective-permute-start(f32[200,128]{1,0:T(8,128)S(1)} %pad_maximum_fusion.refs_0_), channel_id=1, source_target_pairs={{0,3},{1,2},{2,1},{3,0},{4,7},{5,6},{6,5},{7,4},{8,11},{9,10},{10,... | collective-permute-start | bytes 307208 | tf_op jit(solution)/shard_map/ppermute | solution.py:377
  5.6 5.1 %collective-permute-start.1 = (f32[200,128]{1,0:T(8,128)S(1)}, f32[200,128]{1,0:T(8,128)S(1)}, u32[]{:S(2)}, u32[]{:S(2)}) collective-permute-start(f32[200,128]{1,0:T(8,128)S(1)} %pad_maximum_fusion.refs_0_), channel_id=1, source_target_pairs={{0,2},{1,3},{2,0},{3,1},{4,6},{5,7},{6,4},{7,5},{8,10},{9,11},{10,... | collective-permute-start | bytes 307208 | tf_op jit(solution)/shard_map/ppermute | solution.py:377
  6.1 4.9 %collective-permute-start = (f32[200,128]{1,0:T(8,128)S(1)}, f32[200,128]{1,0:T(8,128)S(1)}, u32[]{:S(2)}, u32[]{:S(2)}) collective-permute-start(f32[200,128]{1,0:T(8,128)S(1)} %pad_maximum_fusion.refs_0_), channel_id=1, source_target_pairs={{0,1},{1,0},{2,3},{3,2},{4,5},{5,4},{6,7},{7,6},{8,9},{9,8},{10,11... | collective-permute-start | bytes 307208 | tf_op jit(solution)/shard_map/ppermute | solution.py:377
  28.4 4.5 %collective-permute-start.5 = (f32[2,72,128]{2,1,0:T(8,128)S(1)}, f32[2,72,128]{2,1,0:T(8,128)S(1)}, u32[]{:S(2)}, u32[]{:S(2)}) collective-permute-start(f32[2,72,128]{2,1,0:T(8,128)S(1)} %get-tuple-element.7.refs_0_), channel_id=1, source_target_pairs={{0,8},{4,12},{8,0},{12,4},{16,24},{20,28},{24,16},{28,20},{1,9},{5... | collective-permute-start | bytes 221192 | tf_op jit(solution)/shard_map/ppermute | solution.py:331
  30.1 7.6 %collective-permute-start.4 = (f32[2,72,128]{2,1,0:T(8,128)S(1)}, f32[2,72,128]{2,1,0:T(8,128)S(1)}, u32[]{:S(2)}, u32[]{:S(2)}) collective-permute-start(f32[2,72,128]{2,1,0:T(8,128)S(1)} %get-tuple-element.7.refs_0_), channel_id=1, source_target_pairs={{0,16},{4,20},{8,24},{12,28},{16,0},{20,4},{24,8},{28,12},{1,17},{... | collective-permute-start | bytes 221192 | tf_op jit(solution)/shard_map/ppermute | solution.py:331
  32.7 6.3 %collective-permute-start.3 = (f32[2,72,128]{2,1,0:T(8,128)S(1)}, f32[2,72,128]{2,1,0:T(8,128)S(1)}, u32[]{:S(2)}, u32[]{:S(2)}) collective-permute-start(f32[2,72,128]{2,1,0:T(8,128)S(1)} %get-tuple-element.7.refs_0_), channel_id=1, source_target_pairs={{0,24},{4,28},{8,16},{12,20},{16,8},{20,12},{24,0},{28,4},{1,25},{... | collective-permute-start | bytes 221192 | tf_op jit(solution)/shard_map/ppermute | solution.py:331
  32.9 6.0 %collective-permute-start.6 = (f32[2,72,128]{2,1,0:T(8,128)S(1)}, f32[2,72,128]{2,1,0:T(8,128)S(1)}, u32[]{:S(2)}, u32[]{:S(2)}) collective-permute-start(f32[2,72,128]{2,1,0:T(8,128)S(1)} %get-tuple-element.7.refs_0_), channel_id=1, source_target_pairs={{0,4},{4,0},{8,12},{12,8},{16,20},{20,16},{24,28},{28,24},{1,5},{5... | collective-permute-start | bytes 221192 | tf_op jit(solution)/shard_map/ppermute | solution.py:331
  32.9 6.0 %collective-permute-start.9 = (f32[2,72,128]{2,1,0:T(8,128)S(1)}, f32[2,72,128]{2,1,0:T(8,128)S(1)}, u32[]{:S(2)}, u32[]{:S(2)}) collective-permute-start(f32[2,72,128]{2,1,0:T(8,128)S(1)} %collective-permute-done.5.refs_3_), channel_id=1, source_target_pairs={{0,4},{4,0},{8,12},{12,8},{16,20},{20,16},{24,28},{28,24},{1,5},{5... | collective-permute-start | bytes 221192 | tf_op jit(solution)/shard_map/ppermute | solution.py:331
  37.6 1.3 %collective-permute-start.8 = (f32[2,72,128]{2,1,0:T(8,128)S(1)}, f32[2,72,128]{2,1,0:T(8,128)S(1)}, u32[]{:S(2)}, u32[]{:S(2)}) collective-permute-start(f32[2,72,128]{2,1,0:T(8,128)S(1)} %collective-permute-done.4.refs_2_), channel_id=1, source_target_pairs={{0,4},{4,0},{8,12},{12,8},{16,20},{20,16},{24,28},{28,24},{1,5},{5... | collective-permute-start | bytes 221192 | tf_op jit(solution)/shard_map/ppermute | solution.py:331
  38.9 1.3 %collective-permute-start.7 = (f32[2,72,128]{2,1,0:T(8,128)S(1)}, f32[2,72,128]{2,1,0:T(8,128)S(1)}, u32[]{:S(2)}, u32[]{:S(2)}) collective-permute-start(f32[2,72,128]{2,1,0:T(8,128)S(1)} %collective-permute-done.3.refs_1_), channel_id=1, source_target_pairs={{0,4},{4,0},{8,12},{12,8},{16,20},{20,16},{24,28},{28,24},{1,5},{5... | collective-permute-start | bytes 221192 | tf_op jit(solution)/shard_map/ppermute | solution.py:331

commit v5 on v4

--- a/solution.py
+++ b/solution.py
@@ -9,7 +9,7 @@
 
 f32 = jnp.float32
 bf16 = jnp.bfloat16
-PANEL = 16
+PANEL = 32
 TILE = 8
 GRANT = 24 << 20
 
@@ -72,13 +72,75 @@
     return pairs
 
 
+def times(left, right):
+    return left[0] * right[0] - left[1] * right[1], left[0] * right[1] + left[1] * right[0]
+
+
+def minus(left, right):
+    return left[0] - right[0], left[1] - right[1]
+
+
+def eliminate_tiles_by_pairs(pairs, base, row, lane):
+    columns = [spread_columns(real, imag, base) for real, imag in pairs]
+    pairs = list(pairs)
+    for k in range(0, TILE, 2):
+        first, second = row == k, row == k + 1
+        both_rows = first | second
+        first_lane, second_lane = lane == base + k, lane == base + k + 1
+        both_lanes = first_lane | second_lane
+        cleared = both_rows | both_lanes
+        ones = (jnp.where(first_lane, 1.0, 0.0), jnp.where(second_lane, 1.0, 0.0))
+        factors = []
+        for dr, di in columns:
+            p00, p10 = [(row_of(dr[k], r), row_of(di[k], r)) for r in (k, k + 1)]
+            p01, p11 = [(row_of(dr[k + 1], r), row_of(di[k + 1], r)) for r in (k, k + 1)]
+            det = minus(times(p00, p11), times(p01, p10))
+            inverse = 1.0 / (det[0] * det[0] + det[1] * det[1])
+            conjugate = (det[0], -det[1])
+            c0, c1 = [
+                (
+                    jnp.where(both_rows, jnp.where(own, -1.0, 0.0), dr[k + i]),
+                    jnp.where(both_rows, 0.0, di[k + i]),
+                )
+                for i, own in enumerate((first, second))
+            ]
+            t0 = times(minus(times(c0, p11), times(c1, p10)), conjugate)
+            t1 = times(minus(times(c1, p00), times(c0, p01)), conjugate)
+            scaled = [(t[0] * inverse, t[1] * inverse) for t in (t0, t1)]
+            factors.append((t0, t1, inverse, *scaled))
+
+        def change(f0, f1, a0, a1):
+            w0, w1 = times(f0, a0), times(f1, a1)
+            return w0[0] + w1[0], w0[1] + w1[1]
+
+        for c in range(k + 2, TILE):
+            for (dr, di), (t0, t1, inverse, f0, f1) in zip(columns, factors):
+                a0, a1 = [(row_of(dr[c], r), row_of(di[c], r)) for r in (k, k + 1)]
+                zr, zi = jnp.where(both_rows, 0.0, dr[c]), jnp.where(both_rows, 0.0, di[c])
+                if c < k + 4:
+                    w = change(t0, t1, a0, a1)
+                    dr[c], di[c] = zr - w[0] * inverse, zi - w[1] * inverse
+                else:
+                    w = change(f0, f1, a0, a1)
+                    dr[c], di[c] = zr - w[0], zi - w[1]
+        for m, ((real, imag), (_, _, _, f0, f1)) in enumerate(zip(pairs, factors)):
+            a0, a1 = [
+                (jnp.where(both_lanes, one, row_of(real, r)), jnp.where(both_lanes, 0.0, row_of(imag, r)))
+                for one, r in zip(ones, (k, k + 1))
+            ]
+            w = change(f0, f1, a0, a1)
+            pairs[m] = (jnp.where(cleared, 0.0, real) - w[0], jnp.where(cleared, 0.0, imag) - w[1])
+    return pairs
+
+
 def eliminate_panel(panels, first, row, lane):
     tiles = len(panels[0])
     for s in range(tiles):
         base = first + s * TILE
         others = [(s + 1 + u) % tiles for u in range(tiles - 1)]
         columns = [{t: spread_columns(*panel[t], base) for t in others} for panel in panels]
-        done = eliminate_tiles([panel[s] for panel in panels], base, row, lane)
+        eliminate = eliminate_tiles_by_pairs if len(panels) == 1 else eliminate_tiles
+        done = eliminate([panel[s] for panel in panels], base, row, lane)
         rows = [[(row_of(real, k), row_of(imag, k)) for k in range(TILE)] for real, imag in done]
         inside = (lane >= base) & (lane < base + TILE)
         for t in others:
@@ -93,9 +155,9 @@
     return panels
 
 
-def invert_in_place(ref, count):
+def invert_in_place(ref, count, unrolled):
     size = ref.shape[-1]
-    width = min(PANEL, size)
+    width = min(PANEL // count, size)
     tiles = width // TILE
 
     def step(j, carry):
@@ -134,7 +196,7 @@
             ref[m, 1, rows, :] = wi
         return carry
 
-    lax.fori_loop(0, size // width, step, 0)
+    lax.fori_loop(0, size // width, step, 0, unroll=size // width if unrolled else 1)
 
 
 def wide(real, imag):
@@ -158,15 +220,14 @@
     kept, middle = half_masks(half, size)
     upper = value[:half]
     extra = jnp.sum(jnp.where(middle, upper, 0.0), axis=0, keepdims=True)
-    return jnp.concatenate([jnp.where(kept, upper, value[half:]), jnp.broadcast_to(extra, (TILE, size))], 0)
-
-
-def unpacked(packed):
+    return jnp.where(kept, upper, value[half:]), jnp.broadcast_to(extra, (TILE, size))
+
+
+def unpacked(packed, extra):
     size = packed.shape[1]
-    half = size // 2
     kept, middle = half_masks(size, size)
-    whole = jnp.concatenate([packed[:half], packed[:half]], 0)
-    whole = jnp.where(middle, jnp.broadcast_to(packed[half : half + 1], (size, size)), whole)
+    whole = jnp.concatenate([packed, packed], 0)
+    whole = jnp.where(middle, jnp.broadcast_to(extra, (size, size)), whole)
     return jnp.where(kept | middle, whole, whole.T)
 
 
@@ -213,7 +274,9 @@
         for d in steps:
             copies[d].wait()
         for step in steps:
-            diagonal_ref[step, 0] = energy * identity - unpacked(slab_ref[step, : size // 2 + TILE, :])
+            diagonal_ref[step, 0] = energy * identity - unpacked(
+                slab_ref[step, : size // 2, :], slab_ref[step, size // 2 : size // 2 + 1, :]
+            )
             diagonal_ref[step, 1] = damping * identity
 
             @pl.when(is_last(step))
@@ -234,7 +297,7 @@
             group = odds[first : first + 2]
             for m, node in enumerate(group):
                 work_ref[m] = diagonal_ref[node]
-            invert_in_place(work_ref, len(group))
+            invert_in_place(work_ref, len(group), count <= 4)
             if level == 0 and first == 0:
                 place(range(0, count, 2))
             for m, node in enumerate(group):
@@ -264,11 +327,15 @@
                     link_ref[before, 0] = real[:size, size:]
                     link_ref[before, 1] = imag[:size, size:]
     work_ref[0] = diagonal_ref[0]
-    invert_in_place(work_ref, 1)
+    invert_in_place(work_ref, 1, count <= 4)
+    extras = []
     for part in range(2):
         value = -work_ref[0, part]
         green_ref[part] = value
-        packed_ref[part] = packed_half(value)
+        packed_ref[part * size // 2 : (part + 1) * size // 2, :], extra = packed_half(value)
+        extras.append(extra)
+    which = lax.broadcasted_iota(jnp.int32, (TILE, size), 0)
+    packed_ref[size:, :] = jnp.where(which == 0, extras[0], extras[1])
 
 
 def green_of(blocks, damping, total_energies):
@@ -279,7 +346,7 @@
         functools.partial(chain_kernel, count, total_energies),
         out_shape=(
             jax.ShapeDtypeStruct((2, size, size), f32),
-            jax.ShapeDtypeStruct((2, size // 2 + TILE, size), f32),
+            jax.ShapeDtypeStruct((size + TILE, size), f32),
         ),
         in_specs=[scalar] + [pl.BlockSpec(memory_space=pl.ANY)] * count,
         out_specs=(whole, whole),
@@ -309,17 +376,24 @@
     leaving[0].start()
     for copy in copies:
         copy.wait()
-    real = imag = jnp.zeros(held.shape[2:], f32)
+    size = held.shape[-1]
+    half = size // 2
+    real = imag = jnp.zeros((half, size), f32)
+    extra_real = extra_imag = jnp.zeros((TILE, size), f32)
     for first in range(groups):
         inside = first + me < groups
         second = jnp.where(inside, first + me, 0)
         weight = jnp.where(inside, 1.0 / groups, 0.0)
-        br, bi = held[first, 0] * weight, held[first, 1] * weight
-        ar, ai = held[second, 0], held[second, 1]
+        br, bi = held[first, :half, :] * weight, held[first, half:size, :] * weight
+        ar, ai = held[second, :half, :], held[second, half:size, :]
         real = real + (ar * br + ai * bi)
         imag = imag + (ai * br - ar * bi)
-    for part, value in enumerate((real, imag)):
-        result[part] = unpacked(value)
+        b, a = held[first, size:, :] * weight, held[second, size:, :]
+        br, bi, ar, ai = row_of(b, 0), row_of(b, 1), row_of(a, 0), row_of(a, 1)
+        extra_real = extra_real + (ar * br + ai * bi)
+        extra_imag = extra_imag + (ai * br - ar * bi)
+    for part, (value, extra) in enumerate(((real, extra_real), (imag, extra_imag))):
+        result[part] = unpacked(value, extra[:1])
         leaving.append(pltpu.make_async_copy(result.at[part], out_ref.at[part], left.at[part]))
         leaving[-1].start()
     for copy in leaving:
@@ -371,7 +445,7 @@
     slabs = lax.axis_size("slab")
     groups = lax.axis_size("energy")
     size = h_diag.shape[-1]
-    own = jnp.concatenate([packed_half(h_diag[0]), coupling[0]], 0)
+    own = jnp.concatenate([*packed_half(h_diag[0]), coupling[0]], 0)
     blocks = {0: own}
     for d in list(range(slabs - 1, 0, -2)) + list(range(slabs - 2, 0, -2)):
         blocks[d] = lax.ppermute(own, "slab", [(s, s ^ d) for s in range(slabs)])

time: 42 us -> 41.1 us (0.979)
  Pallas kernels: 19.2 us -> 18.2 us
    pallas_call x1, Pallas kernels: 17.5 us -> 16.5 us  [green_of(): pl.pallas_call(functools.partial(chain_kernel, count, total_energies), ou...]
where the time goes in v5:
time: 41.1 us; the launch traced here: 41 us
  Pallas kernels  18.2 us (44%)
  waiting for transfers between devices  10.8 us (26%)
  starting transfers between devices  9.6 us (23%)
  between operations  1.5 us (4%)
  other arithmetic  0.92 us (2%)
    pallas_call x1, Pallas kernels, green_of(): pl.pallas_call(functools.partial(chain_kernel, count, total_energies), ou...  16.5 us
    ppermute x7, waiting for transfers between devices, swapped(): return lax.ppermute(block, 'energy', [(s, s ^ step) for s in range(groups)])  6.71 us
    ppermute x7, starting transfers between devices, swapped(): return lax.ppermute(block, 'energy', [(s, s ^ step) for s in range(groups)])  4.97 us
    ppermute x3, starting transfers between devices, on_device(): blocks[d] = lax.ppermute(own, 'slab', [(s, s ^ d) for s in range(slabs)])  4.63 us
    ppermute x3, waiting for transfers between devices, on_device(): blocks[d] = lax.ppermute(own, 'slab', [(s, s ^ d) for s in range(slabs)])  4.07 us
    pallas_call x1, Pallas kernels, correlate(): pl.pallas_call(functools.partial(polar_kernel, steps), out_shape=(result,...  1.66 us
    select_n x1, other arithmetic, packed_half(): jnp.where(kept, upper, value[half:])  0.9 us
  transfers between devices with their start and end apart: 10, of which 6 were waited for; matrix products, arithmetic and copies ran while one was open for 0% of the time, Pallas kernels for 0%

profile of v5, /device:TPU:0, one launch (start us, length us, event | category | flops | bytes accessed | tf_op | source)
XLA Modules:
  0.0 41.0 jit_solution(2648796525347508516)
XLA Ops:
  0.6 0.0 copy-start
  0.7 0.9 %bitcast_select_fusion = (f32[64,128]{1,0:T(8,128)S(1)}, f32[128]{0:T(128)S(1)}) fusion(f32[1,128,128]{2,1,0:T(8,128)} %param.3, pred[64]{0:T(512)(128)(4,1)S(1)} %iota_compare_fusion), kind=kLoop, calls=%fused_computation.4 | loop fusion | flops 114560 | bytes 98880 | tf_op jit(solution)/shard_map/jit(_where)/select_n | solution.py:223
  1.6 0.0 copy-done
  1.6 4.0 %collective-permute-start.2 = (f32[200,128]{1,0:T(8,128)S(1)}, f32[200,128]{1,0:T(8,128)S(1)}, u32[]{:S(2)}, u32[]{:S(2)}) collective-permute-start(f32[200,128]{1,0:T(8,128)S(1)} %pad_maximum_fusion.refs_0_), channel_id=1, source_target_pairs={{0,3},{1,2},{2,1},{3,0},{4,7},{5,6},{6,5},{7,4},{8,11},{9,10},{10,... | collective-permute-start | bytes 307208 | tf_op jit(solution)/shard_map/ppermute | solution.py:451
  5.6 0.5 %collective-permute-start.1 = (f32[200,128]{1,0:T(8,128)S(1)}, f32[200,128]{1,0:T(8,128)S(1)}, u32[]{:S(2)}, u32[]{:S(2)}) collective-permute-start(f32[200,128]{1,0:T(8,128)S(1)} %pad_maximum_fusion.refs_0_), channel_id=1, source_target_pairs={{0,2},{1,3},{2,0},{3,1},{4,6},{5,7},{6,4},{7,5},{8,10},{9,11},{10,... | collective-permute-start | bytes 307208 | tf_op jit(solution)/shard_map/ppermute | solution.py:451
  6.1 0.1 collective-permute-start
  6.9 2.0 %collective-permute-done.2.refs_3_ = f32[200,128]{1,0:T(8,128)S(1)} collective-permute-done((f32[200,128]{1,0:T(8,128)S(1)}, f32[200,128]{1,0:T(8,128)S(1)}, u32[]{:S(2)}, u32[]{:S(2)}) %collective-permute-start.2) | collective-permute-done | bytes 102432 | tf_op jit(solution)/shard_map/ppermute | solution.py:451
  8.8 1.8 %collective-permute-done.1.refs_2_ = f32[200,128]{1,0:T(8,128)S(1)} collective-permute-done((f32[200,128]{1,0:T(8,128)S(1)}, f32[200,128]{1,0:T(8,128)S(1)}, u32[]{:S(2)}, u32[]{:S(2)}) %collective-permute-start.1) | collective-permute-done | bytes 102432 | tf_op jit(solution)/shard_map/ppermute | solution.py:451
  10.6 0.3 collective-permute-done.refs_1_
  10.9 16.5 %chain.1 = (f32[2,128,128]{2,1,0:T(8,128)S(1)}, f32[136,128]{1,0:T(8,128)S(1)}) custom-call(f32[1]{0:T(128)S(6)} %copy.5.damping_ref, f32[200,128]{1,0:T(8,128)S(1)} %pad_maximum_fusion.refs_0_, f32[200,128]{1,0:T(8,128)S(1)} %collective-permute-done.refs_1_, f32[200,128]{1,0:T(8,128)S(1)} %collective-permute-done.1.refs_2_, ...), custom_call_target="tpu_custom_call" | custom-call | tf_op jit(solution)/shard_map/chain/pallas_call | solution.py:345
  27.4 1.6 %collective-permute-start.5 = (f32[136,128]{1,0:T(8,128)S(1)}, f32[136,128]{1,0:T(8,128)S(1)}, u32[]{:S(2)}, u32[]{:S(2)}) collective-permute-start(f32[136,128]{1,0:T(8,128)S(1)} %get-tuple-element.7.refs_0_), channel_id=1, source_target_pairs={{0,8},{4,12},{8,0},{12,4},{16,24},{20,28},{24,16},{28,20},{1,9},{5... | collective-permute-start | bytes 208904 | tf_op jit(solution)/shard_map/ppermute | solution.py:405
  29.1 2.6 %collective-permute-start.4 = (f32[136,128]{1,0:T(8,128)S(1)}, f32[136,128]{1,0:T(8,128)S(1)}, u32[]{:S(2)}, u32[]{:S(2)}) collective-permute-start(f32[136,128]{1,0:T(8,128)S(1)} %get-tuple-element.7.refs_0_), channel_id=1, source_target_pairs={{0,16},{4,20},{8,24},{12,28},{16,0},{20,4},{24,8},{28,12},{1,17},{... | collective-permute-start | bytes 208904 | tf_op jit(solution)/shard_map/ppermute | solution.py:405
  31.7 0.2 collective-permute-start.3
  31.9 0.0 collective-permute-start.6
  31.9 0.0 collective-permute-done.5.refs_3_
  31.9 0.5 %collective-permute-start.9 = (f32[136,128]{1,0:T(8,128)S(1)}, f32[136,128]{1,0:T(8,128)S(1)}, u32[]{:S(2)}, u32[]{:S(2)}) collective-permute-start(f32[136,128]{1,0:T(8,128)S(1)} %collective-permute-done.5.refs_3_), channel_id=1, source_target_pairs={{0,4},{4,0},{8,12},{12,8},{16,20},{20,16},{24,28},{28,24},{1,5},{5... | collective-permute-start | bytes 208904 | tf_op jit(solution)/shard_map/ppermute | solution.py:405
  32.4 4.0 %collective-permute-done.4.refs_2_ = f32[136,128]{1,0:T(8,128)S(1)} collective-permute-done((f32[136,128]{1,0:T(8,128)S(1)}, f32[136,128]{1,0:T(8,128)S(1)}, u32[]{:S(2)}, u32[]{:S(2)}) %collective-permute-start.4) | collective-permute-done | bytes 69664 | tf_op jit(solution)/shard_map/ppermute | solution.py:405
  36.4 0.0 collective-permute-start.8
  36.4 1.5 %collective-permute-done.3.refs_1_ = f32[136,128]{1,0:T(8,128)S(1)} collective-permute-done((f32[136,128]{1,0:T(8,128)S(1)}, f32[136,128]{1,0:T(8,128)S(1)}, u32[]{:S(2)}, u32[]{:S(2)}) %collective-permute-start.3) | collective-permute-done | bytes 69664 | tf_op jit(solution)/shard_map/ppermute | solution.py:405
  37.9 0.0 collective-permute-start.7
  37.9 0.0 collective-permute-done.6.refs_4_
  37.9 0.0 collective-permute-done.9.refs_7_
  37.9 0.0 collective-permute-done.8.refs_6_
  37.9 1.2 %collective-permute-done.7.refs_5_ = f32[136,128]{1,0:T(8,128)S(1)} collective-permute-done((f32[136,128]{1,0:T(8,128)S(1)}, f32[136,128]{1,0:T(8,128)S(1)}, u32[]{:S(2)}, u32[]{:S(2)}) %collective-permute-start.7) | collective-permute-done | bytes 69664 | tf_op jit(solution)/shard_map/ppermute | solution.py:405
  39.1 1.7 %polar.1 = (f32[2,128,128]{2,1,0:T(8,128)}, f32[2,128,128]{2,1,0:T(8,128)}) custom-call(f32[2,128,128]{2,1,0:T(8,128)S(1)} %get-tuple-element.6.green_ref, f32[136,128]{1,0:T(8,128)S(1)} %get-tuple-element.7.refs_0_, f32[136,128]{1,0:T(8,128)S(1)} %collective-permute-done.3.refs_1_, f32[136,128]{1,0:T(8,128)S(1)} %collective-permute-done.4.refs_2_, ...), custom_call_target="tpu_custom_call" | custom-call | tf_op jit(solution)/shard_map/polar/pallas_call | solution.py:413
  (3 shorter events, 0.0 us)
Async XLA Ops:
  0.6 0.9 %copy-start = (f32[1,128,128]{2,1,0:T(8,128)S(1)}, f32[1,128,128]{2,1,0:T(8,128)}, u32[]{:S(2)}) copy-start(f32[1,128,128]{2,1,0:T(8,128)} %param.4) | copy-start | bytes 196612
  1.6 7.3 %collective-permute-start.2 = (f32[200,128]{1,0:T(8,128)S(1)}, f32[200,128]{1,0:T(8,128)S(1)}, u32[]{:S(2)}, u32[]{:S(2)}) collective-permute-start(f32[200,128]{1,0:T(8,128)S(1)} %pad_maximum_fusion.refs_0_), channel_id=1, source_target_pairs={{0,3},{1,2},{2,1},{3,0},{4,7},{5,6},{6,5},{7,4},{8,11},{9,10},{10,... | collective-permute-start | bytes 307208 | tf_op jit(solution)/shard_map/ppermute | solution.py:451
  5.6 5.1 %collective-permute-start.1 = (f32[200,128]{1,0:T(8,128)S(1)}, f32[200,128]{1,0:T(8,128)S(1)}, u32[]{:S(2)}, u32[]{:S(2)}) collective-permute-start(f32[200,128]{1,0:T(8,128)S(1)} %pad_maximum_fusion.refs_0_), channel_id=1, source_target_pairs={{0,2},{1,3},{2,0},{3,1},{4,6},{5,7},{6,4},{7,5},{8,10},{9,11},{10,... | collective-permute-start | bytes 307208 | tf_op jit(solution)/shard_map/ppermute | solution.py:451
  6.1 4.9 %collective-permute-start = (f32[200,128]{1,0:T(8,128)S(1)}, f32[200,128]{1,0:T(8,128)S(1)}, u32[]{:S(2)}, u32[]{:S(2)}) collective-permute-start(f32[200,128]{1,0:T(8,128)S(1)} %pad_maximum_fusion.refs_0_), channel_id=1, source_target_pairs={{0,1},{1,0},{2,3},{3,2},{4,5},{5,4},{6,7},{7,6},{8,9},{9,8},{10,11... | collective-permute-start | bytes 307208 | tf_op jit(solution)/shard_map/ppermute | solution.py:451
  27.4 4.5 %collective-permute-start.5 = (f32[136,128]{1,0:T(8,128)S(1)}, f32[136,128]{1,0:T(8,128)S(1)}, u32[]{:S(2)}, u32[]{:S(2)}) collective-permute-start(f32[136,128]{1,0:T(8,128)S(1)} %get-tuple-element.7.refs_0_), channel_id=1, source_target_pairs={{0,8},{4,12},{8,0},{12,4},{16,24},{20,28},{24,16},{28,20},{1,9},{5... | collective-permute-start | bytes 208904 | tf_op jit(solution)/shard_map/ppermute | solution.py:405
  29.1 7.3 %collective-permute-start.4 = (f32[136,128]{1,0:T(8,128)S(1)}, f32[136,128]{1,0:T(8,128)S(1)}, u32[]{:S(2)}, u32[]{:S(2)}) collective-permute-start(f32[136,128]{1,0:T(8,128)S(1)} %get-tuple-element.7.refs_0_), channel_id=1, source_target_pairs={{0,16},{4,20},{8,24},{12,28},{16,0},{20,4},{24,8},{28,12},{1,17},{... | collective-permute-start | bytes 208904 | tf_op jit(solution)/shard_map/ppermute | solution.py:405
  31.7 6.2 %collective-permute-start.3 = (f32[136,128]{1,0:T(8,128)S(1)}, f32[136,128]{1,0:T(8,128)S(1)}, u32[]{:S(2)}, u32[]{:S(2)}) collective-permute-start(f32[136,128]{1,0:T(8,128)S(1)} %get-tuple-element.7.refs_0_), channel_id=1, source_target_pairs={{0,24},{4,28},{8,16},{12,20},{16,8},{20,12},{24,0},{28,4},{1,25},{... | collective-permute-start | bytes 208904 | tf_op jit(solution)/shard_map/ppermute | solution.py:405
  31.9 6.0 %collective-permute-start.6 = (f32[136,128]{1,0:T(8,128)S(1)}, f32[136,128]{1,0:T(8,128)S(1)}, u32[]{:S(2)}, u32[]{:S(2)}) collective-permute-start(f32[136,128]{1,0:T(8,128)S(1)} %get-tuple-element.7.refs_0_), channel_id=1, source_target_pairs={{0,4},{4,0},{8,12},{12,8},{16,20},{20,16},{24,28},{28,24},{1,5},{5... | collective-permute-start | bytes 208904 | tf_op jit(solution)/shard_map/ppermute | solution.py:405
  31.9 6.0 %collective-permute-start.9 = (f32[136,128]{1,0:T(8,128)S(1)}, f32[136,128]{1,0:T(8,128)S(1)}, u32[]{:S(2)}, u32[]{:S(2)}) collective-permute-start(f32[136,128]{1,0:T(8,128)S(1)} %collective-permute-done.5.refs_3_), channel_id=1, source_target_pairs={{0,4},{4,0},{8,12},{12,8},{16,20},{20,16},{24,28},{28,24},{1,5},{5... | collective-permute-start | bytes 208904 | tf_op jit(solution)/shard_map/ppermute | solution.py:405
  36.4 1.5 %collective-permute-start.8 = (f32[136,128]{1,0:T(8,128)S(1)}, f32[136,128]{1,0:T(8,128)S(1)}, u32[]{:S(2)}, u32[]{:S(2)}) collective-permute-start(f32[136,128]{1,0:T(8,128)S(1)} %collective-permute-done.4.refs_2_), channel_id=1, source_target_pairs={{0,4},{4,0},{8,12},{12,8},{16,20},{20,16},{24,28},{28,24},{1,5},{5... | collective-permute-start | bytes 208904 | tf_op jit(solution)/shard_map/ppermute | solution.py:405
  37.9 1.3 %collective-permute-start.7 = (f32[136,128]{1,0:T(8,128)S(1)}, f32[136,128]{1,0:T(8,128)S(1)}, u32[]{:S(2)}, u32[]{:S(2)}) collective-permute-start(f32[136,128]{1,0:T(8,128)S(1)} %collective-permute-done.3.refs_1_), channel_id=1, source_target_pairs={{0,4},{4,0},{8,12},{12,8},{16,20},{20,16},{24,28},{28,24},{1,5},{5... | collective-permute-start | bytes 208904 | tf_op jit(solution)/shard_map/ppermute | solution.py:405

commit v6 on v5

--- a/solution.py
+++ b/solution.py
@@ -245,18 +245,13 @@
 
 def chain_kernel(count, total_energies, damping_ref, *refs):
     blocks, refs = refs[:count], refs[count:]
-    green_ref, packed_ref, slab_ref, diagonal_ref, link_ref, work_ref, arrived = refs
+    green_ref, packed_ref, slab_ref, diagonal_ref, link_ref, work_ref = refs
     size = green_ref.shape[-1]
     slab, position = lax.axis_index("slab"), lax.axis_index("energy")
     energy = -4.0 + 8.0 * position.astype(f32) / (total_energies - 1)
     damping = damping_ref[0]
-    copies = [
-        pltpu.make_async_copy(blocks[d], slab_ref.at[((slab ^ d) - slab) & (count - 1)], arrived.at[d])
-        for d in range(count)
-    ]
-    in_order = list(range(1, count, 2)) + list(range(0, count, 2))
-    for d in in_order:
-        copies[d].start()
+    for d in range(count):
+        slab_ref[((slab ^ d) - slab) & (count - 1)] = blocks[d][...]
     row = lax.broadcasted_iota(jnp.int32, (size, size), 0)
     lane = lax.broadcasted_iota(jnp.int32, (size, size), 1)
     identity = jnp.where(row == lane, 1.0, 0.0).astype(f32)
@@ -271,8 +266,6 @@
         return link_of(step) * jnp.where(is_last(step), 0.0, 1.0)
 
     def place(steps):
-        for d in steps:
-            copies[d].wait()
         for step in steps:
             diagonal_ref[step, 0] = energy * identity - unpacked(
                 slab_ref[step, : size // 2, :], slab_ref[step, size // 2 : size // 2 + 1, :]
@@ -348,14 +341,13 @@
             jax.ShapeDtypeStruct((2, size, size), f32),
             jax.ShapeDtypeStruct((size + TILE, size), f32),
         ),
-        in_specs=[scalar] + [pl.BlockSpec(memory_space=pl.ANY)] * count,
+        in_specs=[scalar] + [whole] * count,
         out_specs=(whole, whole),
         scratch_shapes=[
             pltpu.VMEM((count,) + blocks[0].shape, f32),
             pltpu.VMEM((count, 2, size, size), f32),
             pltpu.VMEM((count, 2, size, size), f32),
             pltpu.VMEM((2, 2, size, size), f32),
-            pltpu.SemaphoreType.DMA((count,)),
         ],
         compiler_params=pltpu.CompilerParams(vmem_limit_bytes=GRANT),
         name="chain",
@@ -364,18 +356,12 @@
 
 def polar_kernel(steps, green_ref, *refs):
     groups = len(steps)
-    blocks, (green_out_ref, out_ref, held, result, arrived, left) = refs[:groups], refs[groups:]
+    blocks, (green_out_ref, out_ref, held, result, left) = refs[:groups], refs[groups:]
     me = lax.axis_index("energy")
-    copies = [
-        pltpu.make_async_copy(block, held.at[me ^ step], arrived.at[i])
-        for i, (step, block) in enumerate(zip(steps, blocks))
-    ]
-    for copy in copies:
-        copy.start()
     leaving = [pltpu.make_async_copy(green_ref, green_out_ref, left.at[2])]
     leaving[0].start()
-    for copy in copies:
-        copy.wait()
+    for step, block in zip(steps, blocks):
+        held[me ^ step] = block[...]
     size = held.shape[-1]
     half = size // 2
     real = imag = jnp.zeros((half, size), f32)
@@ -413,12 +399,11 @@
     return pl.pallas_call(
         functools.partial(polar_kernel, steps),
         out_shape=(result, result),
-        in_specs=[anywhere] * (1 + groups),
+        in_specs=[anywhere] + [pl.BlockSpec(memory_space=pltpu.VMEM)] * groups,
         out_specs=(anywhere, anywhere),
         scratch_shapes=[
             pltpu.VMEM((groups,) + packed.shape, f32),
             pltpu.VMEM(green.shape, f32),
-            pltpu.SemaphoreType.DMA((groups,)),
             pltpu.SemaphoreType.DMA((3,)),
         ],
         compiler_params=pltpu.CompilerParams(vmem_limit_bytes=GRANT),

time: 41.1 us -> 39.8 us (0.968)
  Pallas kernels: 18.2 us -> 16.8 us
    pallas_call x1, Pallas kernels: 1.66 us -> 0.93 us  [correlate(): pl.pallas_call(functools.partial(polar_kernel, steps), out_shape=(result,...]
    pallas_call x1, Pallas kernels: 16.5 us -> 15.9 us  [green_of(): pl.pallas_call(functools.partial(chain_kernel, count, total_energies), ou...]
where the time goes in v6:
time: 39.8 us; the launch traced here: 39.6 us
  Pallas kernels  16.8 us (42%)
  waiting for transfers between devices  10.8 us (27%)
  starting transfers between devices  9.6 us (24%)
  between operations  1.5 us (4%)
  other arithmetic  0.92 us (2%)
    pallas_call x1, Pallas kernels, green_of(): pl.pallas_call(functools.partial(chain_kernel, count, total_energies), ou...  15.9 us
    ppermute x7, waiting for transfers between devices, swapped(): return lax.ppermute(block, 'energy', [(s, s ^ step) for s in range(groups)])  6.7 us
    ppermute x7, starting transfers between devices, swapped(): return lax.ppermute(block, 'energy', [(s, s ^ step) for s in range(groups)])  4.97 us
    ppermute x3, starting transfers between devices, on_device(): blocks[d] = lax.ppermute(own, 'slab', [(s, s ^ d) for s in range(slabs)])  4.63 us
    ppermute x3, waiting for transfers between devices, on_device(): blocks[d] = lax.ppermute(own, 'slab', [(s, s ^ d) for s in range(slabs)])  4.07 us
    pallas_call x1, Pallas kernels, correlate(): pl.pallas_call(functools.partial(polar_kernel, steps), out_shape=(result,...  0.93 us
    select_n x1, other arithmetic, packed_half(): jnp.where(kept, upper, value[half:])  0.9 us
  transfers between devices with their start and end apart: 10, of which 6 were waited for; matrix products, arithmetic and copies ran while one was open for 0% of the time, Pallas kernels for 0%

profile of v6, /device:TPU:0, one launch (start us, length us, event | category | flops | bytes accessed | tf_op | source)
XLA Modules:
  0.0 39.6 jit_solution(8425369886413765295)
XLA Ops:
  0.6 0.0 copy-start
  0.7 0.9 %bitcast_select_fusion = (f32[64,128]{1,0:T(8,128)S(1)}, f32[128]{0:T(128)S(1)}) fusion(f32[1,128,128]{2,1,0:T(8,128)} %param.3, pred[64]{0:T(512)(128)(4,1)S(1)} %iota_compare_fusion), kind=kLoop, calls=%fused_computation.4 | loop fusion | flops 114560 | bytes 98880 | tf_op jit(solution)/shard_map/jit(_where)/select_n | solution.py:223
  1.6 0.0 copy-done
  1.6 4.0 %collective-permute-start.2 = (f32[200,128]{1,0:T(8,128)S(1)}, f32[200,128]{1,0:T(8,128)S(1)}, u32[]{:S(2)}, u32[]{:S(2)}) collective-permute-start(f32[200,128]{1,0:T(8,128)S(1)} %pad_maximum_fusion.refs_0_), channel_id=1, source_target_pairs={{0,3},{1,2},{2,1},{3,0},{4,7},{5,6},{6,5},{7,4},{8,11},{9,10},{10,... | collective-permute-start | bytes 307208 | tf_op jit(solution)/shard_map/ppermute | solution.py:436
  5.6 0.5 %collective-permute-start.1 = (f32[200,128]{1,0:T(8,128)S(1)}, f32[200,128]{1,0:T(8,128)S(1)}, u32[]{:S(2)}, u32[]{:S(2)}) collective-permute-start(f32[200,128]{1,0:T(8,128)S(1)} %pad_maximum_fusion.refs_0_), channel_id=1, source_target_pairs={{0,2},{1,3},{2,0},{3,1},{4,6},{5,7},{6,4},{7,5},{8,10},{9,11},{10,... | collective-permute-start | bytes 307208 | tf_op jit(solution)/shard_map/ppermute | solution.py:436
  6.1 0.1 collective-permute-start
  6.9 2.0 %collective-permute-done.2.refs_3_ = f32[200,128]{1,0:T(8,128)S(1)} collective-permute-done((f32[200,128]{1,0:T(8,128)S(1)}, f32[200,128]{1,0:T(8,128)S(1)}, u32[]{:S(2)}, u32[]{:S(2)}) %collective-permute-start.2) | collective-permute-done | bytes 102432 | tf_op jit(solution)/shard_map/ppermute | solution.py:436
  8.8 1.8 %collective-permute-done.1.refs_2_ = f32[200,128]{1,0:T(8,128)S(1)} collective-permute-done((f32[200,128]{1,0:T(8,128)S(1)}, f32[200,128]{1,0:T(8,128)S(1)}, u32[]{:S(2)}, u32[]{:S(2)}) %collective-permute-start.1) | collective-permute-done | bytes 102432 | tf_op jit(solution)/shard_map/ppermute | solution.py:436
  10.6 0.3 collective-permute-done.refs_1_
  10.9 15.9 %chain.1 = (f32[2,128,128]{2,1,0:T(8,128)S(1)}, f32[136,128]{1,0:T(8,128)S(1)}) custom-call(f32[1]{0:T(128)S(6)} %copy.5.damping_ref, f32[200,128]{1,0:T(8,128)S(1)} %pad_maximum_fusion.refs_0_, f32[200,128]{1,0:T(8,128)S(1)} %collective-permute-done.refs_1_, f32[200,128]{1,0:T(8,128)S(1)} %collective-permute-done.1.refs_2_, ...), custom_call_target="tpu_custom_call" | custom-call | tf_op jit(solution)/shard_map/chain/pallas_call | solution.py:338
  26.8 1.6 %collective-permute-start.5 = (f32[136,128]{1,0:T(8,128)S(1)}, f32[136,128]{1,0:T(8,128)S(1)}, u32[]{:S(2)}, u32[]{:S(2)}) collective-permute-start(f32[136,128]{1,0:T(8,128)S(1)} %get-tuple-element.7.refs_0_), channel_id=1, source_target_pairs={{0,8},{4,12},{8,0},{12,4},{16,24},{20,28},{24,16},{28,20},{1,9},{5... | collective-permute-start | bytes 208904 | tf_op jit(solution)/shard_map/ppermute | solution.py:391
  28.5 2.6 %collective-permute-start.4 = (f32[136,128]{1,0:T(8,128)S(1)}, f32[136,128]{1,0:T(8,128)S(1)}, u32[]{:S(2)}, u32[]{:S(2)}) collective-permute-start(f32[136,128]{1,0:T(8,128)S(1)} %get-tuple-element.7.refs_0_), channel_id=1, source_target_pairs={{0,16},{4,20},{8,24},{12,28},{16,0},{20,4},{24,8},{28,12},{1,17},{... | collective-permute-start | bytes 208904 | tf_op jit(solution)/shard_map/ppermute | solution.py:391
  31.1 0.2 collective-permute-start.3
  31.3 0.0 collective-permute-start.6
  31.3 0.0 collective-permute-done.5.refs_3_
  31.3 0.5 %collective-permute-start.9 = (f32[136,128]{1,0:T(8,128)S(1)}, f32[136,128]{1,0:T(8,128)S(1)}, u32[]{:S(2)}, u32[]{:S(2)}) collective-permute-start(f32[136,128]{1,0:T(8,128)S(1)} %collective-permute-done.5.refs_3_), channel_id=1, source_target_pairs={{0,4},{4,0},{8,12},{12,8},{16,20},{20,16},{24,28},{28,24},{1,5},{5... | collective-permute-start | bytes 208904 | tf_op jit(solution)/shard_map/ppermute | solution.py:391
  31.8 4.0 %collective-permute-done.4.refs_2_ = f32[136,128]{1,0:T(8,128)S(1)} collective-permute-done((f32[136,128]{1,0:T(8,128)S(1)}, f32[136,128]{1,0:T(8,128)S(1)}, u32[]{:S(2)}, u32[]{:S(2)}) %collective-permute-start.4) | collective-permute-done | bytes 69664 | tf_op jit(solution)/shard_map/ppermute | solution.py:391
  35.8 0.0 collective-permute-start.8
  35.8 1.5 %collective-permute-done.3.refs_1_ = f32[136,128]{1,0:T(8,128)S(1)} collective-permute-done((f32[136,128]{1,0:T(8,128)S(1)}, f32[136,128]{1,0:T(8,128)S(1)}, u32[]{:S(2)}, u32[]{:S(2)}) %collective-permute-start.3) | collective-permute-done | bytes 69664 | tf_op jit(solution)/shard_map/ppermute | solution.py:391
  37.2 0.0 collective-permute-start.7
  37.2 0.0 collective-permute-done.6.refs_4_
  37.3 0.0 collective-permute-done.9.refs_7_
  37.3 0.0 collective-permute-done.8.refs_6_
  37.3 1.2 %collective-permute-done.7.refs_5_ = f32[136,128]{1,0:T(8,128)S(1)} collective-permute-done((f32[136,128]{1,0:T(8,128)S(1)}, f32[136,128]{1,0:T(8,128)S(1)}, u32[]{:S(2)}, u32[]{:S(2)}) %collective-permute-start.7) | collective-permute-done | bytes 69664 | tf_op jit(solution)/shard_map/ppermute | solution.py:391
  38.5 0.9 %polar.1 = (f32[2,128,128]{2,1,0:T(8,128)}, f32[2,128,128]{2,1,0:T(8,128)}) custom-call(f32[2,128,128]{2,1,0:T(8,128)S(1)} %get-tuple-element.6.green_ref, f32[136,128]{1,0:T(8,128)S(1)} %get-tuple-element.7.refs_0_, f32[136,128]{1,0:T(8,128)S(1)} %collective-permute-done.3.refs_1_, f32[136,128]{1,0:T(8,128)S(1)} %collective-permute-done.4.refs_2_, ...), custom_call_target="tpu_custom_call" | custom-call | tf_op jit(solution)/shard_map/polar/pallas_call | solution.py:399
  (3 shorter events, 0.0 us)
Async XLA Ops:
  0.6 0.9 %copy-start = (f32[1,128,128]{2,1,0:T(8,128)S(1)}, f32[1,128,128]{2,1,0:T(8,128)}, u32[]{:S(2)}) copy-start(f32[1,128,128]{2,1,0:T(8,128)} %param.4) | copy-start | bytes 196612
  1.6 7.3 %collective-permute-start.2 = (f32[200,128]{1,0:T(8,128)S(1)}, f32[200,128]{1,0:T(8,128)S(1)}, u32[]{:S(2)}, u32[]{:S(2)}) collective-permute-start(f32[200,128]{1,0:T(8,128)S(1)} %pad_maximum_fusion.refs_0_), channel_id=1, source_target_pairs={{0,3},{1,2},{2,1},{3,0},{4,7},{5,6},{6,5},{7,4},{8,11},{9,10},{10,... | collective-permute-start | bytes 307208 | tf_op jit(solution)/shard_map/ppermute | solution.py:436
  5.6 5.1 %collective-permute-start.1 = (f32[200,128]{1,0:T(8,128)S(1)}, f32[200,128]{1,0:T(8,128)S(1)}, u32[]{:S(2)}, u32[]{:S(2)}) collective-permute-start(f32[200,128]{1,0:T(8,128)S(1)} %pad_maximum_fusion.refs_0_), channel_id=1, source_target_pairs={{0,2},{1,3},{2,0},{3,1},{4,6},{5,7},{6,4},{7,5},{8,10},{9,11},{10,... | collective-permute-start | bytes 307208 | tf_op jit(solution)/shard_map/ppermute | solution.py:436
  6.1 4.9 %collective-permute-start = (f32[200,128]{1,0:T(8,128)S(1)}, f32[200,128]{1,0:T(8,128)S(1)}, u32[]{:S(2)}, u32[]{:S(2)}) collective-permute-start(f32[200,128]{1,0:T(8,128)S(1)} %pad_maximum_fusion.refs_0_), channel_id=1, source_target_pairs={{0,1},{1,0},{2,3},{3,2},{4,5},{5,4},{6,7},{7,6},{8,9},{9,8},{10,11... | collective-permute-start | bytes 307208 | tf_op jit(solution)/shard_map/ppermute | solution.py:436
  26.8 4.5 %collective-permute-start.5 = (f32[136,128]{1,0:T(8,128)S(1)}, f32[136,128]{1,0:T(8,128)S(1)}, u32[]{:S(2)}, u32[]{:S(2)}) collective-permute-start(f32[136,128]{1,0:T(8,128)S(1)} %get-tuple-element.7.refs_0_), channel_id=1, source_target_pairs={{0,8},{4,12},{8,0},{12,4},{16,24},{20,28},{24,16},{28,20},{1,9},{5... | collective-permute-start | bytes 208904 | tf_op jit(solution)/shard_map/ppermute | solution.py:391
  28.5 7.3 %collective-permute-start.4 = (f32[136,128]{1,0:T(8,128)S(1)}, f32[136,128]{1,0:T(8,128)S(1)}, u32[]{:S(2)}, u32[]{:S(2)}) collective-permute-start(f32[136,128]{1,0:T(8,128)S(1)} %get-tuple-element.7.refs_0_), channel_id=1, source_target_pairs={{0,16},{4,20},{8,24},{12,28},{16,0},{20,4},{24,8},{28,12},{1,17},{... | collective-permute-start | bytes 208904 | tf_op jit(solution)/shard_map/ppermute | solution.py:391
  31.1 6.2 %collective-permute-start.3 = (f32[136,128]{1,0:T(8,128)S(1)}, f32[136,128]{1,0:T(8,128)S(1)}, u32[]{:S(2)}, u32[]{:S(2)}) collective-permute-start(f32[136,128]{1,0:T(8,128)S(1)} %get-tuple-element.7.refs_0_), channel_id=1, source_target_pairs={{0,24},{4,28},{8,16},{12,20},{16,8},{20,12},{24,0},{28,4},{1,25},{... | collective-permute-start | bytes 208904 | tf_op jit(solution)/shard_map/ppermute | solution.py:391
  31.3 6.0 %collective-permute-start.6 = (f32[136,128]{1,0:T(8,128)S(1)}, f32[136,128]{1,0:T(8,128)S(1)}, u32[]{:S(2)}, u32[]{:S(2)}) collective-permute-start(f32[136,128]{1,0:T(8,128)S(1)} %get-tuple-element.7.refs_0_), channel_id=1, source_target_pairs={{0,4},{4,0},{8,12},{12,8},{16,20},{20,16},{24,28},{28,24},{1,5},{5... | collective-permute-start | bytes 208904 | tf_op jit(solution)/shard_map/ppermute | solution.py:391
  31.3 6.0 %collective-permute-start.9 = (f32[136,128]{1,0:T(8,128)S(1)}, f32[136,128]{1,0:T(8,128)S(1)}, u32[]{:S(2)}, u32[]{:S(2)}) collective-permute-start(f32[136,128]{1,0:T(8,128)S(1)} %collective-permute-done.5.refs_3_), channel_id=1, source_target_pairs={{0,4},{4,0},{8,12},{12,8},{16,20},{20,16},{24,28},{28,24},{1,5},{5... | collective-permute-start | bytes 208904 | tf_op jit(solution)/shard_map/ppermute | solution.py:391
  35.8 1.5 %collective-permute-start.8 = (f32[136,128]{1,0:T(8,128)S(1)}, f32[136,128]{1,0:T(8,128)S(1)}, u32[]{:S(2)}, u32[]{:S(2)}) collective-permute-start(f32[136,128]{1,0:T(8,128)S(1)} %collective-permute-done.4.refs_2_), channel_id=1, source_target_pairs={{0,4},{4,0},{8,12},{12,8},{16,20},{20,16},{24,28},{28,24},{1,5},{5... | collective-permute-start | bytes 208904 | tf_op jit(solution)/shard_map/ppermute | solution.py:391
  37.2 1.3 %collective-permute-start.7 = (f32[136,128]{1,0:T(8,128)S(1)}, f32[136,128]{1,0:T(8,128)S(1)}, u32[]{:S(2)}, u32[]{:S(2)}) collective-permute-start(f32[136,128]{1,0:T(8,128)S(1)} %collective-permute-done.3.refs_1_), channel_id=1, source_target_pairs={{0,4},{4,0},{8,12},{12,8},{16,20},{20,16},{24,28},{28,24},{1,5},{5... | collective-permute-start | bytes 208904 | tf_op jit(solution)/shard_map/ppermute | solution.py:391

commit v7 on v6

--- a/solution.py
+++ b/solution.py
@@ -178,7 +178,7 @@
         for m in range(count):
             wr = jnp.concatenate([jnp.where(block, -real, real) for real, _ in panels[m]], 0)
             wi = jnp.concatenate([jnp.where(block, -imag, imag) for _, imag in panels[m]], 0)
-            rh, rm, rl = three_parts(square(wr, wi))
+            rh, rm, rl = [square(*parts) for parts in zip(three_parts(wr), three_parts(wi))]
             change = lax.dot_general(
                 lefts[m],
                 jnp.concatenate([rh, rm, rh, rl, rm, rh], 0),
@@ -207,6 +207,10 @@
     return jnp.concatenate([wide(real, imag), wide(-imag, real)], 0)
 
 
+def turned_square(real, imag):
+    return jnp.concatenate([wide(real, -imag), wide(imag, real)], 0)
+
+
 def half_masks(rows, size):
     row = lax.broadcasted_iota(jnp.int32, (rows, size), 0)
     lane = lax.broadcasted_iota(jnp.int32, (rows, size), 1)
@@ -234,7 +238,11 @@
 def exact_dot(left, right, dims):
     (over_left,), (over_right,) = dims
     lh, lm, ll = three_parts(left)
-    rh, rm, rl = three_parts(right)
+    if isinstance(right, tuple):
+        layout, real, imag = right
+        rh, rm, rl = [layout(*parts) for parts in zip(three_parts(real), three_parts(imag))]
+    else:
+        rh, rm, rl = three_parts(right)
     return lax.dot_general(
         jnp.concatenate([lh, lh, lm, lh, lm, ll], over_left),
         jnp.concatenate([rh, rm, rh, rl, rm, rh], over_right),
@@ -310,9 +318,8 @@
                     both = exact_dot(both, ends[0], ((1,), (1,)))
                     real, imag = both[:height], both[height:]
                 else:
-                    both = exact_dot(wide(*ends), square(*middle), ((1,), (0,)))
-                    turned = jnp.concatenate([wide(ends[0], -ends[1]), wide(ends[1], ends[0])], 0)
-                    both = exact_dot(both, turned, ((1,), (1,)))
+                    both = exact_dot(wide(*ends), (square, *middle), ((1,), (0,)))
+                    both = exact_dot(both, (turned_square, *ends), ((1,), (1,)))
                     real, imag = both[:, :height], both[:, height:]
                 subtract(before, -real[:size, :size], -imag[:size, :size])
                 if before != after:

time: 39.8 us -> 39.8 us (level)
  no operation moved by 1% of the time
where the time goes in v7:
time: 39.8 us; the launch traced here: 39.6 us
  Pallas kernels  16.8 us (42%)
  waiting for transfers between devices  10.8 us (27%)
  starting transfers between devices  9.6 us (24%)
  between operations  1.5 us (4%)
  other arithmetic  0.92 us (2%)
    pallas_call x1, Pallas kernels, green_of(): pl.pallas_call(functools.partial(chain_kernel, count, total_energies), ou...  15.9 us
    ppermute x7, waiting for transfers between devices, swapped(): return lax.ppermute(block, 'energy', [(s, s ^ step) for s in range(groups)])  6.7 us
    ppermute x7, starting transfers between devices, swapped(): return lax.ppermute(block, 'energy', [(s, s ^ step) for s in range(groups)])  4.97 us
    ppermute x3, starting transfers between devices, on_device(): blocks[d] = lax.ppermute(own, 'slab', [(s, s ^ d) for s in range(slabs)])  4.63 us
    ppermute x3, waiting for transfers between devices, on_device(): blocks[d] = lax.ppermute(own, 'slab', [(s, s ^ d) for s in range(slabs)])  4.07 us
    pallas_call x1, Pallas kernels, correlate(): pl.pallas_call(functools.partial(polar_kernel, steps), out_shape=(result,...  0.93 us
    select_n x1, other arithmetic, packed_half(): jnp.where(kept, upper, value[half:])  0.9 us
  transfers between devices with their start and end apart: 10, of which 6 were waited for; matrix products, arithmetic and copies ran while one was open for 0% of the time, Pallas kernels for 0%

profile of v7, /device:TPU:0, one launch (start us, length us, event | category | flops | bytes accessed | tf_op | source)
XLA Modules:
  0.0 39.6 jit_solution(3359698416031119265)
XLA Ops:
  0.6 0.0 copy-start
  0.7 0.9 %bitcast_select_fusion = (f32[64,128]{1,0:T(8,128)S(1)}, f32[128]{0:T(128)S(1)}) fusion(f32[1,128,128]{2,1,0:T(8,128)} %param.3, pred[64]{0:T(512)(128)(4,1)S(1)} %iota_compare_fusion), kind=kLoop, calls=%fused_computation.4 | loop fusion | flops 114560 | bytes 98880 | tf_op jit(solution)/shard_map/jit(_where)/select_n | solution.py:227
  1.6 0.0 copy-done
  1.6 4.0 %collective-permute-start.2 = (f32[200,128]{1,0:T(8,128)S(1)}, f32[200,128]{1,0:T(8,128)S(1)}, u32[]{:S(2)}, u32[]{:S(2)}) collective-permute-start(f32[200,128]{1,0:T(8,128)S(1)} %pad_maximum_fusion.refs_0_), channel_id=1, source_target_pairs={{0,3},{1,2},{2,1},{3,0},{4,7},{5,6},{6,5},{7,4},{8,11},{9,10},{10,... | collective-permute-start | bytes 307208 | tf_op jit(solution)/shard_map/ppermute | solution.py:443
  5.6 0.5 %collective-permute-start.1 = (f32[200,128]{1,0:T(8,128)S(1)}, f32[200,128]{1,0:T(8,128)S(1)}, u32[]{:S(2)}, u32[]{:S(2)}) collective-permute-start(f32[200,128]{1,0:T(8,128)S(1)} %pad_maximum_fusion.refs_0_), channel_id=1, source_target_pairs={{0,2},{1,3},{2,0},{3,1},{4,6},{5,7},{6,4},{7,5},{8,10},{9,11},{10,... | collective-permute-start | bytes 307208 | tf_op jit(solution)/shard_map/ppermute | solution.py:443
  6.1 0.1 collective-permute-start
  6.9 2.0 %collective-permute-done.2.refs_3_ = f32[200,128]{1,0:T(8,128)S(1)} collective-permute-done((f32[200,128]{1,0:T(8,128)S(1)}, f32[200,128]{1,0:T(8,128)S(1)}, u32[]{:S(2)}, u32[]{:S(2)}) %collective-permute-start.2) | collective-permute-done | bytes 102432 | tf_op jit(solution)/shard_map/ppermute | solution.py:443
  8.8 1.8 %collective-permute-done.1.refs_2_ = f32[200,128]{1,0:T(8,128)S(1)} collective-permute-done((f32[200,128]{1,0:T(8,128)S(1)}, f32[200,128]{1,0:T(8,128)S(1)}, u32[]{:S(2)}, u32[]{:S(2)}) %collective-permute-start.1) | collective-permute-done | bytes 102432 | tf_op jit(solution)/shard_map/ppermute | solution.py:443
  10.6 0.3 collective-permute-done.refs_1_
  10.9 15.9 %chain.1 = (f32[2,128,128]{2,1,0:T(8,128)S(1)}, f32[136,128]{1,0:T(8,128)S(1)}) custom-call(f32[1]{0:T(128)S(6)} %copy.5.damping_ref, f32[200,128]{1,0:T(8,128)S(1)} %pad_maximum_fusion.refs_0_, f32[200,128]{1,0:T(8,128)S(1)} %collective-permute-done.refs_1_, f32[200,128]{1,0:T(8,128)S(1)} %collective-permute-done.1.refs_2_, ...), custom_call_target="tpu_custom_call" | custom-call | tf_op jit(solution)/shard_map/chain/pallas_call | solution.py:345
  26.8 1.6 %collective-permute-start.5 = (f32[136,128]{1,0:T(8,128)S(1)}, f32[136,128]{1,0:T(8,128)S(1)}, u32[]{:S(2)}, u32[]{:S(2)}) collective-permute-start(f32[136,128]{1,0:T(8,128)S(1)} %get-tuple-element.7.refs_0_), channel_id=1, source_target_pairs={{0,8},{4,12},{8,0},{12,4},{16,24},{20,28},{24,16},{28,20},{1,9},{5... | collective-permute-start | bytes 208904 | tf_op jit(solution)/shard_map/ppermute | solution.py:398
  28.5 2.6 %collective-permute-start.4 = (f32[136,128]{1,0:T(8,128)S(1)}, f32[136,128]{1,0:T(8,128)S(1)}, u32[]{:S(2)}, u32[]{:S(2)}) collective-permute-start(f32[136,128]{1,0:T(8,128)S(1)} %get-tuple-element.7.refs_0_), channel_id=1, source_target_pairs={{0,16},{4,20},{8,24},{12,28},{16,0},{20,4},{24,8},{28,12},{1,17},{... | collective-permute-start | bytes 208904 | tf_op jit(solution)/shard_map/ppermute | solution.py:398
  31.1 0.2 collective-permute-start.3
  31.3 0.0 collective-permute-start.6
  31.3 0.0 collective-permute-done.5.refs_3_
  31.3 0.5 %collective-permute-start.9 = (f32[136,128]{1,0:T(8,128)S(1)}, f32[136,128]{1,0:T(8,128)S(1)}, u32[]{:S(2)}, u32[]{:S(2)}) collective-permute-start(f32[136,128]{1,0:T(8,128)S(1)} %collective-permute-done.5.refs_3_), channel_id=1, source_target_pairs={{0,4},{4,0},{8,12},{12,8},{16,20},{20,16},{24,28},{28,24},{1,5},{5... | collective-permute-start | bytes 208904 | tf_op jit(solution)/shard_map/ppermute | solution.py:398
  31.8 4.0 %collective-permute-done.4.refs_2_ = f32[136,128]{1,0:T(8,128)S(1)} collective-permute-done((f32[136,128]{1,0:T(8,128)S(1)}, f32[136,128]{1,0:T(8,128)S(1)}, u32[]{:S(2)}, u32[]{:S(2)}) %collective-permute-start.4) | collective-permute-done | bytes 69664 | tf_op jit(solution)/shard_map/ppermute | solution.py:398
  35.8 0.0 collective-permute-start.8
  35.8 1.5 %collective-permute-done.3.refs_1_ = f32[136,128]{1,0:T(8,128)S(1)} collective-permute-done((f32[136,128]{1,0:T(8,128)S(1)}, f32[136,128]{1,0:T(8,128)S(1)}, u32[]{:S(2)}, u32[]{:S(2)}) %collective-permute-start.3) | collective-permute-done | bytes 69664 | tf_op jit(solution)/shard_map/ppermute | solution.py:398
  37.3 0.0 collective-permute-start.7
  37.3 0.0 collective-permute-done.6.refs_4_
  37.3 0.0 collective-permute-done.9.refs_7_
  37.3 0.0 collective-permute-done.8.refs_6_
  37.3 1.2 %collective-permute-done.7.refs_5_ = f32[136,128]{1,0:T(8,128)S(1)} collective-permute-done((f32[136,128]{1,0:T(8,128)S(1)}, f32[136,128]{1,0:T(8,128)S(1)}, u32[]{:S(2)}, u32[]{:S(2)}) %collective-permute-start.7) | collective-permute-done | bytes 69664 | tf_op jit(solution)/shard_map/ppermute | solution.py:398
  38.5 0.9 %polar.1 = (f32[2,128,128]{2,1,0:T(8,128)}, f32[2,128,128]{2,1,0:T(8,128)}) custom-call(f32[2,128,128]{2,1,0:T(8,128)S(1)} %get-tuple-element.6.green_ref, f32[136,128]{1,0:T(8,128)S(1)} %get-tuple-element.7.refs_0_, f32[136,128]{1,0:T(8,128)S(1)} %collective-permute-done.3.refs_1_, f32[136,128]{1,0:T(8,128)S(1)} %collective-permute-done.4.refs_2_, ...), custom_call_target="tpu_custom_call" | custom-call | tf_op jit(solution)/shard_map/polar/pallas_call | solution.py:406
  (3 shorter events, 0.0 us)
Async XLA Ops:
  0.6 0.9 %copy-start = (f32[1,128,128]{2,1,0:T(8,128)S(1)}, f32[1,128,128]{2,1,0:T(8,128)}, u32[]{:S(2)}) copy-start(f32[1,128,128]{2,1,0:T(8,128)} %param.4) | copy-start | bytes 196612
  1.6 7.3 %collective-permute-start.2 = (f32[200,128]{1,0:T(8,128)S(1)}, f32[200,128]{1,0:T(8,128)S(1)}, u32[]{:S(2)}, u32[]{:S(2)}) collective-permute-start(f32[200,128]{1,0:T(8,128)S(1)} %pad_maximum_fusion.refs_0_), channel_id=1, source_target_pairs={{0,3},{1,2},{2,1},{3,0},{4,7},{5,6},{6,5},{7,4},{8,11},{9,10},{10,... | collective-permute-start | bytes 307208 | tf_op jit(solution)/shard_map/ppermute | solution.py:443
  5.6 5.1 %collective-permute-start.1 = (f32[200,128]{1,0:T(8,128)S(1)}, f32[200,128]{1,0:T(8,128)S(1)}, u32[]{:S(2)}, u32[]{:S(2)}) collective-permute-start(f32[200,128]{1,0:T(8,128)S(1)} %pad_maximum_fusion.refs_0_), channel_id=1, source_target_pairs={{0,2},{1,3},{2,0},{3,1},{4,6},{5,7},{6,4},{7,5},{8,10},{9,11},{10,... | collective-permute-start | bytes 307208 | tf_op jit(solution)/shard_map/ppermute | solution.py:443
  6.1 4.9 %collective-permute-start = (f32[200,128]{1,0:T(8,128)S(1)}, f32[200,128]{1,0:T(8,128)S(1)}, u32[]{:S(2)}, u32[]{:S(2)}) collective-permute-start(f32[200,128]{1,0:T(8,128)S(1)} %pad_maximum_fusion.refs_0_), channel_id=1, source_target_pairs={{0,1},{1,0},{2,3},{3,2},{4,5},{5,4},{6,7},{7,6},{8,9},{9,8},{10,11... | collective-permute-start | bytes 307208 | tf_op jit(solution)/shard_map/ppermute | solution.py:443
  26.8 4.5 %collective-permute-start.5 = (f32[136,128]{1,0:T(8,128)S(1)}, f32[136,128]{1,0:T(8,128)S(1)}, u32[]{:S(2)}, u32[]{:S(2)}) collective-permute-start(f32[136,128]{1,0:T(8,128)S(1)} %get-tuple-element.7.refs_0_), channel_id=1, source_target_pairs={{0,8},{4,12},{8,0},{12,4},{16,24},{20,28},{24,16},{28,20},{1,9},{5... | collective-permute-start | bytes 208904 | tf_op jit(solution)/shard_map/ppermute | solution.py:398
  28.5 7.3 %collective-permute-start.4 = (f32[136,128]{1,0:T(8,128)S(1)}, f32[136,128]{1,0:T(8,128)S(1)}, u32[]{:S(2)}, u32[]{:S(2)}) collective-permute-start(f32[136,128]{1,0:T(8,128)S(1)} %get-tuple-element.7.refs_0_), channel_id=1, source_target_pairs={{0,16},{4,20},{8,24},{12,28},{16,0},{20,4},{24,8},{28,12},{1,17},{... | collective-permute-start | bytes 208904 | tf_op jit(solution)/shard_map/ppermute | solution.py:398
  31.1 6.2 %collective-permute-start.3 = (f32[136,128]{1,0:T(8,128)S(1)}, f32[136,128]{1,0:T(8,128)S(1)}, u32[]{:S(2)}, u32[]{:S(2)}) collective-permute-start(f32[136,128]{1,0:T(8,128)S(1)} %get-tuple-element.7.refs_0_), channel_id=1, source_target_pairs={{0,24},{4,28},{8,16},{12,20},{16,8},{20,12},{24,0},{28,4},{1,25},{... | collective-permute-start | bytes 208904 | tf_op jit(solution)/shard_map/ppermute | solution.py:398
  31.3 6.0 %collective-permute-start.6 = (f32[136,128]{1,0:T(8,128)S(1)}, f32[136,128]{1,0:T(8,128)S(1)}, u32[]{:S(2)}, u32[]{:S(2)}) collective-permute-start(f32[136,128]{1,0:T(8,128)S(1)} %get-tuple-element.7.refs_0_), channel_id=1, source_target_pairs={{0,4},{4,0},{8,12},{12,8},{16,20},{20,16},{24,28},{28,24},{1,5},{5... | collective-permute-start | bytes 208904 | tf_op jit(solution)/shard_map/ppermute | solution.py:398
  31.3 6.0 %collective-permute-start.9 = (f32[136,128]{1,0:T(8,128)S(1)}, f32[136,128]{1,0:T(8,128)S(1)}, u32[]{:S(2)}, u32[]{:S(2)}) collective-permute-start(f32[136,128]{1,0:T(8,128)S(1)} %collective-permute-done.5.refs_3_), channel_id=1, source_target_pairs={{0,4},{4,0},{8,12},{12,8},{16,20},{20,16},{24,28},{28,24},{1,5},{5... | collective-permute-start | bytes 208904 | tf_op jit(solution)/shard_map/ppermute | solution.py:398
  35.8 1.5 %collective-permute-start.8 = (f32[136,128]{1,0:T(8,128)S(1)}, f32[136,128]{1,0:T(8,128)S(1)}, u32[]{:S(2)}, u32[]{:S(2)}) collective-permute-start(f32[136,128]{1,0:T(8,128)S(1)} %collective-permute-done.4.refs_2_), channel_id=1, source_target_pairs={{0,4},{4,0},{8,12},{12,8},{16,20},{20,16},{24,28},{28,24},{1,5},{5... | collective-permute-start | bytes 208904 | tf_op jit(solution)/shard_map/ppermute | solution.py:398
  37.3 1.3 %collective-permute-start.7 = (f32[136,128]{1,0:T(8,128)S(1)}, f32[136,128]{1,0:T(8,128)S(1)}, u32[]{:S(2)}, u32[]{:S(2)}) collective-permute-start(f32[136,128]{1,0:T(8,128)S(1)} %collective-permute-done.3.refs_1_), channel_id=1, source_target_pairs={{0,4},{4,0},{8,12},{12,8},{16,20},{20,16},{24,28},{28,24},{1,5},{5... | collective-permute-start | bytes 208904 | tf_op jit(solution)/shard_map/ppermute | solution.py:398
